TPU v7x, 128 devices: a whole 4x4x4 slice. The times are simulated.
128 devices in a mesh: grp: 8 (over z, x_hi), blk: 16 (over x_lo, y, core).
Axes of the slice: x: 4 (x_hi: 2, x_lo: 2; x = x_hi * 2 + x_lo), y: 4, z: 4, core: 2. Of those that a mesh axis runs over, the one named last changes fastest.
Arguments:
- slab: bfloat16 [32, 4096, 4096], P('grp', 'blk'), may hold values from -0.59765625 to 0.59765625
- block_mask: int32 [8, 128, 128], P('grp', 'blk'), may hold values 0 or 1
- orbitals: bfloat16 [4096, 1024], P('blk'), may hold values from -0.09375 to 0.09375
- margin: bfloat16 [4096, 4096], P('blk', 'grp'), as said below
- env_flag: int32 [1024], replicated, may hold values from 0 to 1
Outputs:
- projected: float32 [4096, 4096], P('blk', 'grp')
Inputs may be any that keep to these rules, and one draw needn't show every extreme that they name: margin is symmetric positive definite with unit diagonal.
All inputs are finite; a program needn't handle non-finite values. No bound on the sum of `block_mask` on one device may be relied on, other than what follows from the above.
Results may differ from a plain program's by a relative error of at most 0.003.
Values may be sent and summed in bfloat16 or wider, within the bound.
No kernel may reach another device: no remote copies, remote signals or barrier semaphores. Data moves between devices by JAX's collectives and lax.ppermute only.
A program may use at most 128 MiB of HBM per device.

v0:
```python
import jax
import jax.numpy as jnp
from jax import lax
from jax.sharding import PartitionSpec as P

ATILE = 32


def inner_rows(left, right):
    return lax.dot_general(
        left, right, (((0,), (0,)), ((), ())), preferred_element_type=jnp.float32
    )


def pair_block(half, other):
    return jnp.einsum("pmi,pni->mn", half, other, preferred_element_type=jnp.float32)


def on_device(slab, block_mask, orbitals, margin, env_flag):
    aux_dev, ao_dev, nao = slab.shape
    keep_tile = jnp.repeat(jnp.repeat(block_mask[0], ATILE, axis=0), ATILE, axis=1).astype(
        jnp.bfloat16
    )
    masked = slab * keep_tile[None, :, :]
    whole_c = lax.all_gather(orbitals, "blk", axis=0, tiled=True)
    occ = whole_c.shape[1]
    half = jnp.dot(
        masked.reshape(aux_dev * ao_dev, nao), whole_c, preferred_element_type=jnp.float32
    )
    half = half.astype(jnp.bfloat16).reshape(aux_dev, ao_dev, occ)
    position = lax.axis_index("blk")
    rows_k = pair_block(half, lax.all_gather(half, "blk", axis=1, tiled=True))
    k_tile = lax.psum_scatter(rows_k, "grp", scatter_dimension=1, tiled=True)
    width = k_tile.shape[1]
    ce_whole = whole_c * env_flag.astype(jnp.bfloat16)[None, :]
    ce_rows = lax.dynamic_slice_in_dim(ce_whole, position * ao_dev, ao_dev, 0)
    ce_cols = lax.dynamic_slice_in_dim(ce_whole, lax.axis_index("grp") * width, width, 0)
    k_bf = k_tile.astype(jnp.bfloat16)
    left_part = inner_rows(ce_rows, k_bf)
    envov_part = inner_rows(ce_rows, margin)
    left_env, env_margin = lax.psum((left_part, envov_part), "blk")
    right_part = jnp.dot(k_bf, ce_cols, preferred_element_type=jnp.float32)
    ovenv_part = jnp.dot(margin, ce_cols, preferred_element_type=jnp.float32)
    right_env, margin_env = lax.psum((right_part, ovenv_part), "grp")
    first = jnp.dot(
        margin_env.astype(jnp.bfloat16),
        left_env.astype(jnp.bfloat16),
        preferred_element_type=jnp.float32,
    )
    second = jnp.dot(
        right_env.astype(jnp.bfloat16),
        env_margin.astype(jnp.bfloat16),
        preferred_element_type=jnp.float32,
    )
    return k_tile - first - second


def solution(mesh):
    placed = (P("grp", "blk", None), P("grp", "blk", None), P("blk", None), P("blk", "grp"), P())
    return jax.shard_map(
        on_device, mesh=mesh, in_specs=placed, out_specs=P("blk", "grp"), check_vma=False
    )
```

profile of v0, /device:TPU:0, one launch (start us, length us, event | category | flops | bytes accessed | tf_op | source)
XLA Modules:
  0.0 537.7 jit_solution(16283713551685349303)
XLA Ops:
  6.5 0.0 copy-start
  6.5 0.0 all-gather.3.cloned.1.call-start
  6.5 0.7 all-gather.3.cloned.1.call-update
  7.3 0.0 all-gather.5.cloned.1.call-start
  7.3 0.7 convert_bitcast_fusion
  8.0 0.1 copy.8
  8.1 1.5 broadcast_in_dim.9
  9.6 2.9 copy.9
  12.5 7.5 %broadcast_multiply_fusion.1 = bf16[4,256,4096]{2,1,0:T(8,128)(2,1)} fusion(bf16[4,256,4096]{2,1,0:T(8,128)(2,1)} %param.5, bf16[256,4096]{1,0:T(8,128)(2,1)S(1)} %copy.9), kind=kLoop, calls=%fused_computation.2 | loop fusion | flops 4194304 | bytes 18874368 | tf_op jit(solution)/shard_map/mul | solution.py:24
  20.0 43.7 %all-gather.3.cloned.1.call-done = bf16[4096,1024]{1,0:T(8,128)(2,1)} async-done(((bf16[256,1024]{1,0:T(8,128)(2,1)}), bf16[4096,1024]{1,0:T(8,128)(2,1)}) %all-gather.3.cloned.1.call-update) | async-done | bytes 8388624 | tf_op jit(solution)/shard_map/all_gather | solution.py:25
  63.7 14.7 %convolution_convert_fusion = bf16[1024,1024]{1,0:T(8,128)(2,1)} fusion(bf16[1024,4096]{1,0:T(8,128)(2,1)} %bitcast.20, bf16[4096,1024]{1,0:T(8,128)(2,1)} %all-gather.3.cloned.1.call-done), kind=kOutput, calls=%fused_computation.3 | convolution fusion | flops 8590983168 | bytes 18874368 | tf_op jit(solution)/shard_map/dot_general | solution.py:27
  78.3 0.0 all-gather.5.cloned.1.call-update
  78.4 0.0 copy-start.2
  78.4 0.0 reduce-scatter.2.cloned.1.call-start
  78.4 171.6 %all-gather.5.cloned.1.call-done = bf16[4,4096,1024]{2,1,0:T(8,128)(2,1)} async-done(((bf16[4,256,1024]{2,1,0:T(8,128)(2,1)}), bf16[4,4096,1024]{2,1,0:T(8,128)(2,1)}) %all-gather.5.cloned.1.call-update) | async-done | bytes 33554448 | tf_op jit(solution)/shard_map/all_gather | solution.py:32
  250.1 17.5 %convolution_bitcast_fusion = f32[256,4096]{1,0:T(8,128)} fusion(bf16[4,256,1024]{2,1,0:T(8,128)(2,1)} %bitcast.23, bf16[4,4096,1024]{2,1,0:T(8,128)(2,1)} %all-gather.5.cloned.1.call-done), kind=kOutput, calls=%fused_computation | convolution fusion | flops 8589934592 | bytes 39845888 | tf_op jit(solution)/shard_map/pmi,pni->mn/dot_general | solution.py:16
  267.5 0.0 reduce-scatter.2.cloned.1.call-update
  267.6 0.0 copy-done.2
  267.6 7.2 %broadcast_multiply_fusion = bf16[4096,1024]{1,0:T(8,128)(2,1)} fusion(bf16[4096,1024]{1,0:T(8,128)(2,1)} %all-gather.3.cloned.1.call-done, bf16[1024]{0:T(1024)(128)(2,1)S(1)} %convert_element_type.44), kind=kLoop, calls=%fused_computation.1 | loop fusion | flops 4194304 | bytes 16779264 | tf_op jit(solution)/shard_map/mul | solution.py:35
  274.7 0.0 copy-done
  274.7 1.5 fusion.7
  276.3 2.7 convolution_bitcast_fusion.1
  279.0 74.5 %reduce-scatter.2.cloned.1.call-done = f32[256,512]{1,0:T(8,128)} async-done(((f32[256,4096]{1,0:T(8,128)}), f32[256,512]{1,0:T(8,128)}) %reduce-scatter.2.cloned.1.call-update) | async-done | bytes 524304 | tf_op jit(solution)/shard_map/reduce_scatter | solution.py:33
  353.4 0.0 copy-start.1
  353.5 3.1 fusion.9
  356.5 2.8 fusion.2
  359.4 71.0 %all-reduce.4 = (bf16[1024,512]{1,0:T(8,128)(2,1)}, bf16[1024,512]{1,0:T(8,128)(2,1)}) all-reduce(f32[1024,512]{1,0:T(8,128)} %fusion.9, f32[1024,512]{1,0:T(8,128)S(1)} %fusion.7), channel_id=1, replica_groups=mesh['grp'=8,'blk'=16] {'blk'}, use_global_device_ids=true, to_apply=%region_2.0 | all-reduce | flops 1048576 | bytes 6291456 | tf_op jit(solution)/shard_map/psum | solution.py:41
  430.4 96.6 %all-reduce.5 = (bf16[256,1024]{0,1:T(8,128)(2,1)S(1)}, bf16[256,1024]{1,0:T(8,128)(2,1)S(1)}) all-reduce(f32[256,1024]{0,1:T(8,128)} %convolution_bitcast_fusion.1, f32[256,1024]{1,0:T(8,128)} %fusion.2), channel_id=1, replica_groups=mesh['grp'=8,'blk'=16] {'grp'}, use_global_device_ids=true, to_apply=%region_1.0 | all-reduce | flops 524288 | bytes 3145728 | tf_op jit(solution)/shard_map/psum | solution.py:44
  527.0 0.0 copy-done.1
  527.0 1.7 convolution_subtract_fusion.1
  528.7 2.5 convolution_subtract_fusion
  (2 shorter events, 0.0 us)
Async XLA Ops:
  6.5 268.2 %copy-start = (bf16[256,512]{1,0:T(8,128)(2,1)S(1)}, bf16[256,512]{1,0:T(8,128)(2,1)}, u32[]{:S(2)}) copy-start(bf16[256,512]{1,0:T(8,128)(2,1)} %param.8) | copy-start | bytes 786436
  6.5 57.1 %all-gather.3.cloned.1.call-start = ((), (), s32[]{:S(2)}) async-start(), calls=%async_computation.1 | async-start | bytes 8912896 | tf_op jit(solution)/shard_map/all_gather | solution.py:25
  7.3 242.8 %all-gather.5.cloned.1.call-start = ((), (), s32[]{:S(2)}) async-start(), calls=%async_computation.2 | async-start | bytes 35651584 | tf_op jit(solution)/shard_map/all_gather | solution.py:32
  78.4 189.2 %copy-start.2 = (s32[1024]{0:T(1024)S(1)}, s32[1024]{0:T(1024)}, u32[]{:S(2)}) copy-start(s32[1024]{0:T(1024)} %param.9) | copy-start | bytes 12292
  78.4 275.1 %reduce-scatter.2.cloned.1.call-start = ((), (), s32[]{:S(2)}) async-start(), calls=%async_computation.3 | async-start | bytes 4718592 | tf_op jit(solution)/shard_map/reduce_scatter | solution.py:33
  353.4 173.6 %copy-start.1 = (f32[256,512]{1,0:T(8,128)S(1)}, f32[256,512]{1,0:T(8,128)}, u32[]{:S(2)}) copy-start(f32[256,512]{1,0:T(8,128)} %reduce-scatter.2.cloned.1.call-done) | copy-start | bytes 1572868
Sparse Core Ops, SparseCore 0:
  9.1 54.5 all-gather.2
  78.5 171.5 all-gather.4
  267.7 85.7 reduce-scatter.1
where the time goes:
time: 538 us
  waiting for transfers between devices  291 us (54%)
  blocking collectives  168 us (31%)
  matrix products  46.4 us (9%)
  other arithmetic  15.3 us (3%)
  between operations  13.2 us (2%)
    all_gather x1, waiting for transfers between devices, on_device(): rows_k = pair_block(half, lax.all_gather(half, 'blk', axis=1, tiled=True))  172 us
    psum x1, blocking collectives, on_device(): right_env, margin_env = lax.psum((right_part, ovenv_part), 'grp')  96.6 us
    reduce_scatter x1, waiting for transfers between devices, on_device(): k_tile = lax.psum_scatter(rows_k, 'grp', scatter_dimension=1, tiled=True)  74.5 us
    psum x1, blocking collectives, on_device(): left_env, env_margin = lax.psum((left_part, envov_part), 'blk')  71 us
    all_gather x1, waiting for transfers between devices, on_device(): whole_c = lax.all_gather(orbitals, 'blk', axis=0, tiled=True)  43.7 us
    dot_general x1, matrix products, pair_block(): jnp.einsum('pmi,pni->mn', half, other, preferred_element_type=jnp.float32)  17.5 us
    dot_general x1, matrix products, on_device(): jnp.dot(masked.reshape(aux_dev * ao_dev, nao), whole_c, preferred_element...  14.7 us
  transfers between devices with their start and end apart: 3, of which 3 were waited for; matrix products, arithmetic and copies ran while one was open for 4% of the time, Pallas kernels for 0%

commit v1 on v0

v1 whole, which is shorter than its diff:
```python
import jax
import jax.numpy as jnp
from jax import lax
from jax.sharding import PartitionSpec as P

ATILE = 32
AXES = ("grp", "blk")
NZ, NH, NA, NY, NK = 4, 2, 2, 4, 2


def device(z, h, a, y, k):
    return ((z * NH + h) * NA + a) * NY * NK + y * NK + k


def moved(x, where):
    pairs = []
    for z in range(NZ):
        for h in range(NH):
            for a in range(NA):
                for y in range(NY):
                    for k in range(NK):
                        pairs.append((device(z, h, a, y, k), device(*where(z, h, a, y, k))))
    return lax.ppermute(x, AXES, pairs)


def from_next(x):
    return moved(x, lambda z, h, a, y, k: (z, h, a, (y - 1) % NY, k))


def from_prev(x):
    return moved(x, lambda z, h, a, y, k: (z, h, a, (y + 1) % NY, k))


def across_in(x):
    return moved(x, lambda z, h, a, y, k: (z, h, 1 - a, y, k))


def across_out(x):
    return moved(x, lambda z, h, a, y, k: (z, 1 - h, 1 - a, y, k))


def other_core(x):
    return moved(x, lambda z, h, a, y, k: (z, h, a, y, 1 - k))


def mirror(z, h, a, y, k):
    chip, group = a * NY + y, z * NH + h
    return (chip // NH, chip % NH, group // NY, group % NY, k)


def mirrored(x):
    return moved(x, mirror)


def mirrored_cross(x):
    def where(z, h, a, y, k):
        return mirror(z, h, a, y, 1 - k)

    return moved(x, where)


def to_absolute(rel, a, y):
    twice = jnp.concatenate([rel, rel], axis=1)
    turned = lax.dynamic_slice_in_dim(twice, (NY - y) % NY, NY, 1)
    return jnp.where(a == 0, turned, turned[::-1])


def tile_dot(left, right):
    return jnp.einsum("pmi,pni->mn", left, right, preferred_element_type=jnp.float32)


def gather_half(part):
    nxt, prv, acr = from_next(part), from_prev(part), across_in(part)
    mate = other_core(part)
    rows = jnp.concatenate([part, mate], axis=1)
    acr_nxt, acr_prv = from_next(acr), from_prev(acr)
    far0, far1 = from_next(nxt[:1]), from_prev(prv[1:])
    acr_far0, acr_far1 = across_in(far0), across_in(far1)
    early = [part, nxt, acr, prv]
    late = [acr_nxt, acr_prv, jnp.concatenate([far0, far1]), jnp.concatenate([acr_far0, acr_far1])]
    return rows, early + late


def summed_rows(tiles):
    wide = jnp.concatenate([t.astype(jnp.bfloat16) for t in tiles], axis=1)
    cols = wide.shape[1]
    cut = wide.reshape(2, 8, 32, cols).transpose(1, 0, 2, 3)
    got = lax.all_to_all(cut, "grp", 0, 0)
    total = got.astype(jnp.float32).sum(0)
    return [total[:, :, 256 * i : 256 * (i + 1)] for i in range(len(tiles))]


def on_device(slab, block_mask, orbitals, margin, env_flag):
    aux_dev, ao_dev, nao = slab.shape
    occ = orbitals.shape[1]
    blk = lax.axis_index("blk")
    chip, core = blk // NK, blk % NK
    a, y = chip // NY, chip % NY
    hb = ao_dev // 2

    margin_row = lax.all_gather(margin, "grp", axis=0)

    own = orbitals
    nxt, prv = from_next(own), from_prev(own)
    far = jnp.concatenate([from_next(nxt[:hb]), from_prev(prv[hb:])])
    near = [own, nxt, far, prv]
    cross = [jnp.concatenate([across_in(t[:hb]), across_out(t[hb:])]) for t in near]
    c_rel = jnp.stack(near + cross).reshape(NA, NY, ao_dev, occ)
    whole_c = jnp.zeros((NA, NY, NK, ao_dev, occ), jnp.bfloat16)
    for side, blocks in ((a, c_rel[:1]), (1 - a, c_rel[1:])):
        twice = jnp.concatenate([blocks, blocks], axis=1)
        mine = lax.dynamic_slice_in_dim(twice, (NY - y) % NY, NY, 1)[:, :, None]
        theirs = other_core(mine)
        whole_c = lax.dynamic_update_slice(whole_c, mine, (side, 0, core, 0, 0))
        whole_c = lax.dynamic_update_slice(whole_c, theirs, (side, 0, 1 - core, 0, 0))
    whole_c = whole_c.reshape(nao, occ)

    keep_tile = jnp.repeat(jnp.repeat(block_mask[0], ATILE, axis=0), ATILE, axis=1).astype(
        jnp.bfloat16
    )
    masked = slab * keep_tile[None, :, :]
    tiles = None
    for q in range(2):
        part = jnp.dot(
            masked[2 * q : 2 * q + 2].reshape(2 * ao_dev, nao),
            whole_c,
            preferred_element_type=jnp.float32,
        )
        part = part.astype(jnp.bfloat16).reshape(2, ao_dev, occ)
        rows, blocks = gather_half(part)
        new = [tile_dot(rows, b) for b in blocks]
        tiles = new if tiles is None else [t + n for t, n in zip(tiles, new)]

    flag = env_flag.astype(jnp.bfloat16)[None, :]
    ce_whole = whole_c * flag
    ce_rel = c_rel * flag
    a_rows = jnp.einsum(
        "gmn,gni->mi",
        margin_row,
        ce_whole.reshape(8, nao // 8, occ),
        preferred_element_type=jnp.float32,
    ).astype(jnp.bfloat16)
    a_own = mirrored(a_rows)
    a_oth = other_core(a_own)

    k00, k01, k10, k03 = summed_rows(tiles[:4])
    k11, k13, k02, k12 = summed_rows(tiles[4:])
    rel = jnp.stack([k00, k01, k02, k03, k10, k11, k12, k13])
    mine, theirs = rel[:, 0], other_core(rel[:, 1])
    k_rows = jnp.stack([mine, theirs], axis=2)
    k_bf = rel.astype(jnp.bfloat16)
    b_part = jnp.einsum(
        "tsmn,tni->smi",
        k_bf,
        ce_rel.reshape(8, ao_dev, occ),
        preferred_element_type=jnp.float32,
    )
    b_rows = (b_part[0] + other_core(b_part[1])).astype(jnp.bfloat16)
    k_abs = to_absolute(k_rows.reshape(NA, NY, 32, NK, ao_dev), a, y).reshape(8, 32, 512)
    hi = k_abs.astype(jnp.bfloat16)
    lo = (k_abs - hi.astype(jnp.float32)).astype(jnp.bfloat16)
    packed = jnp.concatenate(
        [jnp.broadcast_to(b_rows[None], (8, 32, occ)), hi, lo], axis=2
    )
    got = lax.all_to_all(packed, "grp", 0, 0).reshape(256, occ + 1024)
    b_all = got[:, :occ]
    k_tile = got[:, occ : occ + 512].astype(jnp.float32) + got[:, occ + 512 :].astype(jnp.float32)
    contract = (((1,), (1,)), ((), ()))
    z_own = lax.dot_general(b_all, a_own, contract, preferred_element_type=jnp.float32)
    z_oth = lax.dot_general(b_all, a_oth, contract, preferred_element_type=jnp.float32)
    t_own = mirrored(z_own.astype(jnp.bfloat16))
    t_oth = mirrored_cross(z_oth.astype(jnp.bfloat16))
    out_own = k_tile[:, :256] - z_own - t_own.astype(jnp.float32).T
    out_oth = k_tile[:, 256:] - z_oth - t_oth.astype(jnp.float32).T
    straight = jnp.concatenate([out_own, out_oth], axis=1)
    swapped = jnp.concatenate([out_oth, out_own], axis=1)
    return jnp.where(core == 0, straight, swapped)


def solution(mesh):
    placed = (P("grp", "blk", None), P("grp", "blk", None), P("blk", None), P("blk", "grp"), P())
    return jax.shard_map(
        on_device, mesh=mesh, in_specs=placed, out_specs=P("blk", "grp"), check_vma=False
    )
```

time: 538 us -> 372 us (0.69)
  the two profiles are of different devices: /device:TPU:0 before, /device:TPU:7 now
where the time goes in v1:
time: 372 us; the launch traced here: 364 us
  waiting for transfers between devices  137 us (37%)
  starting transfers between devices  80 us (22%)
  matrix products  60.9 us (16%)
  local copies, waits for them, and re-layouts  40 us (11%)
  other arithmetic  31.7 us (9%)
  between operations  14.5 us (4%)
    ppermute x40, waiting for transfers between devices, moved(): return lax.ppermute(x, AXES, pairs)  134 us
    ppermute x40, starting transfers between devices, moved(): return lax.ppermute(x, AXES, pairs)  58.3 us
    dot_general x16, matrix products, tile_dot(): jnp.einsum('pmi,pni->mn', left, right, preferred_element_type=jnp.float32)  39.8 us
    all_to_all x2, starting transfers between devices, summed_rows(): got = lax.all_to_all(cut, 'grp', 0, 0)  15.6 us
    reshape x1, local copies, waits for them, and re-layouts, on_device(): whole_c = whole_c.reshape(nao, occ)  11.4 us
    dot_general x2, matrix products, on_device(): jnp.dot(masked[2 * q:2 * q + 2].reshape(2 * ao_dev, nao), whole_c, prefer...  11.1 us
    mul x1, other arithmetic, on_device(): masked = slab * keep_tile[None, :, :]  8.12 us
  transfers between devices with their start and end apart: 44, of which 15 were waited for; matrix products, arithmetic and copies ran while one was open for 33% of the time, Pallas kernels for 0%

profile of v1, /device:TPU:7, one launch (start us, length us, event | category | flops | bytes accessed | tf_op | source)
XLA Modules:
  0.0 364.2 jit_solution(6979449017330755708)
XLA Ops:
  6.5 2.7 collective-permute-start
  12.6 7.6 %collective-permute-done = bf16[256,1024]{1,0:T(8,128)(2,1)S(1)} collective-permute-done((bf16[256,1024]{1,0:T(8,128)(2,1)}, bf16[256,1024]{1,0:T(8,128)(2,1)S(1)}, u32[]{:S(2)}, u32[]{:S(2)}) %collective-permute-start) | collective-permute-done | bytes 524320 | tf_op jit(solution)/shard_map/ppermute | solution.py:23
  21.1 3.4 collective-permute-start.1
  26.4 2.9 copy.53
  40.0 3.7 %collective-permute-done.8 = bf16[128,1024]{1,0:T(8,128)(2,1)S(1)} collective-permute-done((bf16[128,1024]{1,0:T(8,128)(2,1)}, bf16[128,1024]{1,0:T(8,128)(2,1)S(1)}, u32[]{:S(2)}, u32[]{:S(2)}) %collective-permute-start.8) | collective-permute-done | bytes 262176 | tf_op jit(solution)/shard_map/ppermute | solution.py:23
  43.7 5.7 %collective-permute-start.4 = (bf16[1,4,1,256,1024]{4,3,1,2,0:T(8,128)(2,1)}, bf16[1,4,1,256,1024]{4,3,1,2,0:T(8,128)(2,1)}, u32[]{:S(2)}, u32[]{:S(2)}) collective-permute-start(bf16[1,4,1,256,1024]{4,3,1,2,0:T(8,128)(2,1)} %fusion.73), channel_id=1, source_target_pairs={{0,1},{1,0},{2,3},{3,2},{4,5},{5,4},{6,7},{7,6},{8,9},{9,8},{10,11... | collective-permute-start | bytes 6291464 | tf_op jit(solution)/shard_map/ppermute | solution.py:23
  54.6 3.0 collective-permute-start.13
  57.6 8.1 %broadcast_multiply_fusion = bf16[4,256,4096]{2,1,0:T(8,128)(2,1)} fusion(bf16[4,256,4096]{2,1,0:T(8,128)(2,1)} %param.5, bf16[256,4096]{1,0:T(8,128)(2,1)} %copy.53), kind=kLoop, calls=%fused_computation.10 | loop fusion | flops 4194304 | bytes 18874368 | tf_op jit(solution)/shard_map/mul | solution.py:121
  65.7 3.8 %fusion.75 = (bf16[2,256,4096]{2,1,0:T(8,128)(2,1)S(1)}, bf16[2,256,4096]{2,1,0:T(8,128)(2,1)S(1)}) fusion(bf16[4,256,4096]{2,1,0:T(8,128)(2,1)} %broadcast_multiply_fusion), kind=kLoop, calls=%fused_computation.138 | loop fusion | bytes 16777216 | tf_op jit(solution)/shard_map/slice | solution.py:125
  77.1 5.5 %convolution_convert_fusion = bf16[512,1024]{1,0:T(8,128)(2,1)} fusion(bf16[512,4096]{1,0:T(8,128)(2,1)S(1)} %bitcast.234, bf16[4096,1024]{1,0:T(8,128)(2,1)S(1)} %bitcast.221), kind=kOutput, calls=%fused_computation.24 | convolution fusion | flops 4295491584 | bytes 13631488 | tf_op jit(solution)/shard_map/dot_general | solution.py:124
  82.6 2.7 collective-permute-start.17
  85.7 5.5 %convolution_convert_fusion.1 = bf16[512,1024]{1,0:T(8,128)(2,1)} fusion(bf16[512,4096]{1,0:T(8,128)(2,1)S(1)} %bitcast.233, bf16[4096,1024]{1,0:T(8,128)(2,1)S(1)} %bitcast.222), kind=kOutput, calls=%fused_computation.25 | convolution fusion | flops 4295491584 | bytes 13631488 | tf_op jit(solution)/shard_map/dot_general | solution.py:124
  94.8 13.4 %collective-permute-done.17 = bf16[2,256,1024]{2,1,0:T(8,128)(2,1)S(1)} collective-permute-done((bf16[2,256,1024]{2,1,0:T(8,128)(2,1)}, bf16[2,256,1024]{2,1,0:T(8,128)(2,1)S(1)}, u32[]{:S(2)}, u32[]{:S(2)}) %collective-permute-start.17) | collective-permute-done | bytes 1048608 | tf_op jit(solution)/shard_map/ppermute | solution.py:23
  116.7 13.9 %collective-permute-done.16 = bf16[2,256,1024]{2,1,0:T(8,128)(2,1)} collective-permute-done((bf16[2,256,1024]{2,1,0:T(8,128)(2,1)}, bf16[2,256,1024]{2,1,0:T(8,128)(2,1)}, u32[]{:S(2)}, u32[]{:S(2)}) %collective-permute-start.16) | collective-permute-done | bytes 1048608 | tf_op jit(solution)/shard_map/ppermute | solution.py:23
  157.2 17.1 %collective-permute-done.18 = bf16[2,256,1024]{2,1,0:T(8,128)(2,1)S(1)} collective-permute-done((bf16[2,256,1024]{2,1,0:T(8,128)(2,1)}, bf16[2,256,1024]{2,1,0:T(8,128)(2,1)S(1)}, u32[]{:S(2)}, u32[]{:S(2)}) %collective-permute-start.18) | collective-permute-done | bytes 1048608 | tf_op jit(solution)/shard_map/ppermute | solution.py:23
  174.3 3.5 collective-permute-start.23
  183.4 7.8 %all-to-all-start = ((bf16[8,2,32,1024]{3,2,1,0:T(8,128)(2,1)}), bf16[8,2,32,1024]{3,2,1,0:T(8,128)(2,1)S(1)}, u32[]{:S(2)}, u32[]{:S(2)}) async-start(bf16[8,2,32,1024]{3,2,1,0:T(8,128)(2,1)} %copy.59), calls=%async_computation | async-start | bytes 2097152 | tf_op jit(solution)/shard_map/all_to_all | solution.py:88
  197.9 3.8 %collective-permute-done.33 = bf16[1,256,1024]{2,1,0:T(8,128)(2,1)} collective-permute-done((bf16[1,256,1024]{2,1,0:T(8,128)(2,1)}, bf16[1,256,1024]{2,1,0:T(8,128)(2,1)}, u32[]{:S(2)}, u32[]{:S(2)}) %collective-permute-start.33) | collective-permute-done | bytes 524320 | tf_op jit(solution)/shard_map/ppermute | solution.py:23
  204.7 19.4 %collective-permute-done.30 = bf16[1,256,1024]{2,1,0:T(8,128)(2,1)S(1)} collective-permute-done((bf16[1,256,1024]{2,1,0:T(8,128)(2,1)}, bf16[1,256,1024]{2,1,0:T(8,128)(2,1)S(1)}, u32[]{:S(2)}, u32[]{:S(2)}) %collective-permute-start.30) | collective-permute-done | bytes 524320 | tf_op jit(solution)/shard_map/ppermute | solution.py:23
  224.1 11.2 %collective-permute-done.31 = bf16[1,256,1024]{2,1,0:T(8,128)(2,1)S(1)} collective-permute-done((bf16[1,256,1024]{2,1,0:T(8,128)(2,1)}, bf16[1,256,1024]{2,1,0:T(8,128)(2,1)S(1)}, u32[]{:S(2)}, u32[]{:S(2)}) %collective-permute-start.31) | collective-permute-done | bytes 524320 | tf_op jit(solution)/shard_map/ppermute | solution.py:23
  250.4 7.9 %all-to-all-start.1 = ((bf16[8,2,32,1024]{3,2,1,0:T(8,128)(2,1)}), bf16[8,2,32,1024]{3,2,1,0:T(8,128)(2,1)S(1)}, u32[]{:S(2)}, u32[]{:S(2)}) async-start(bf16[8,2,32,1024]{3,2,1,0:T(8,128)(2,1)} %copy.61), calls=%async_computation.1 | async-start | bytes 2097152 | tf_op jit(solution)/shard_map/all_to_all | solution.py:88
  262.8 11.4 %copy.70 = bf16[8,512,1024]{1,2,0:T(8,128)(2,1)} copy(bf16[8,512,1024]{2,1,0:T(8,128)(2,1)} %bitcast.223) | data formatting | bytes 16777216 | tf_op jit(solution)/shard_map/reshape | solution.py:116
  274.8 3.0 fusion.34
  277.8 5.2 %collective-permute-start.34 = (f32[32,1024]{1,0:T(8,128)S(1)}, f32[32,1024]{1,0:T(8,128)S(1)}, u32[]{:S(2)}, u32[]{:S(2)}) collective-permute-start(f32[32,1024]{1,0:T(8,128)S(1)} %slice_bitcast_fusion.1), channel_id=1, source_target_pairs={{0,1},{1,0},{2,3},{3,2},{4,5},{5,4},{6,7},{7,6},{8,9},{9,8},{10,11... | collective-permute-start | bytes 393224 | tf_op jit(solution)/shard_map/ppermute | solution.py:23
  283.3 6.3 %fusion.15 = bf16[256,1024]{0,1:T(8,128)(2,1)S(1)} fusion(bf16[8,256,512]{2,1,0:T(8,128)(2,1)} %bitcast.238, bf16[8,512,1024]{1,2,0:T(8,128)(2,1)} %copy.70, bf16[1024]{0:T(1024)(128)(2,1)S(1)} %convert_element_type.109), kind=kOutput, calls=%fused_computation.28 | convolution fusion | flops 2151940096 | bytes 11012096 | tf_op jit(solution)/shard_map/gmn,gni->mi/dot_general | solution.py:137
  289.7 2.8 collective-permute-start.36
  296.1 6.1 %all-to-all-start.2 = ((bf16[8,32,2048]{2,1,0:T(8,128)(2,1)}), bf16[8,32,2048]{2,1,0:T(8,128)(2,1)S(1)}, u32[]{:S(2)}, u32[]{:S(2)}) async-start(bf16[8,32,2048]{2,1,0:T(8,128)(2,1)} %pad_maximum_fusion.4), calls=%async_computation.2 | async-start | bytes 2097152 | tf_op jit(solution)/shard_map/all_to_all | solution.py:165
  302.2 31.4 %collective-permute-done.36 = bf16[256,1024]{0,1:T(8,128)(2,1)S(1)} collective-permute-done((bf16[256,1024]{0,1:T(8,128)(2,1)S(1)}, bf16[256,1024]{0,1:T(8,128)(2,1)S(1)}, u32[]{:S(2)}, u32[]{:S(2)}) %collective-permute-start.36) | collective-permute-done | bytes 524320 | tf_op jit(solution)/shard_map/ppermute | solution.py:23
  336.8 3.1 all-to-all-done.2
  340.9 8.2 %collective-permute-start.37 = (bf16[256,256]{0,1:T(8,128)(2,1)S(1)}, bf16[256,256]{0,1:T(8,128)(2,1)S(1)}, u32[]{:S(2)}, u32[]{:S(2)}) collective-permute-start(bf16[256,256]{0,1:T(8,128)(2,1)S(1)} %get-tuple-element.19), channel_id=1, source_target_pairs={{0,0},{1,1},{2,16},{3,17},{4,32},{5,33},{6,48},{7,49},{8,64},{9,65... | collective-permute-start | bytes 393224 | tf_op jit(solution)/shard_map/ppermute | solution.py:23
  349.2 4.1 %collective-permute-done.39 = bf16[256,256]{0,1:T(8,128)(2,1)S(1)} collective-permute-done((bf16[256,256]{0,1:T(8,128)(2,1)S(1)}, bf16[256,256]{0,1:T(8,128)(2,1)S(1)}, u32[]{:S(2)}, u32[]{:S(2)}) %collective-permute-start.39) | collective-permute-done | bytes 131104 | tf_op jit(solution)/shard_map/ppermute | solution.py:23
  353.4 2.8 collective-permute-done.37
  (183 shorter events, 112.6 us)
Async XLA Ops:
  6.5 276.8 %all-gather.3.cloned.1.call-start = ((), (), s32[]{:S(2)}) async-start(), calls=%async_computation.3 | async-start | bytes 2359296 | tf_op jit(solution)/shard_map/all_gather | solution.py:101
  11.2 18.1 %collective-permute-start.5 = (bf16[128,1024]{1,0:T(8,128)(2,1)}, bf16[128,1024]{1,0:T(8,128)(2,1)S(1)}, u32[]{:S(2)}, u32[]{:S(2)}) collective-permute-start(bf16[128,1024]{1,0:T(8,128)(2,1)} %get-tuple-element.13), channel_id=1, source_target_pairs={{0,8},{1,9},{2,10},{3,11},{4,12},{5,13},{6,14},{7,15},{8,0},{9,1},... | collective-permute-start | bytes 786440 | tf_op jit(solution)/shard_map/ppermute | solution.py:23
  11.7 17.6 %collective-permute-start.6 = (bf16[128,1024]{1,0:T(8,128)(2,1)}, bf16[128,1024]{1,0:T(8,128)(2,1)}, u32[]{:S(2)}, u32[]{:S(2)}) collective-permute-start(bf16[128,1024]{1,0:T(8,128)(2,1)} %get-tuple-element.14), channel_id=1, source_target_pairs={{0,24},{1,25},{2,26},{3,27},{4,28},{5,29},{6,30},{7,31},{8,16},{9,... | collective-permute-start | bytes 786440 | tf_op jit(solution)/shard_map/ppermute | solution.py:23
  30.9 18.4 %collective-permute-start.12 = (bf16[128,1024]{1,0:T(8,128)(2,1)}, bf16[128,1024]{1,0:T(8,128)(2,1)S(1)}, u32[]{:S(2)}, u32[]{:S(2)}) collective-permute-start(bf16[128,1024]{1,0:T(8,128)(2,1)} %get-tuple-element.18), channel_id=1, source_target_pairs={{0,24},{1,25},{2,26},{3,27},{4,28},{5,29},{6,30},{7,31},{8,16},{9,... | collective-permute-start | bytes 786440 | tf_op jit(solution)/shard_map/ppermute | solution.py:23
  33.6 15.8 %collective-permute-start.11 = (bf16[128,1024]{1,0:T(8,128)(2,1)}, bf16[128,1024]{1,0:T(8,128)(2,1)S(1)}, u32[]{:S(2)}, u32[]{:S(2)}) collective-permute-start(bf16[128,1024]{1,0:T(8,128)(2,1)} %get-tuple-element.17), channel_id=1, source_target_pairs={{0,8},{1,9},{2,10},{3,11},{4,12},{5,13},{6,14},{7,15},{8,0},{9,1},... | collective-permute-start | bytes 786440 | tf_op jit(solution)/shard_map/ppermute | solution.py:23
  33.6 15.8 %collective-permute-start.10 = (bf16[128,1024]{1,0:T(8,128)(2,1)}, bf16[128,1024]{1,0:T(8,128)(2,1)S(1)}, u32[]{:S(2)}, u32[]{:S(2)}) collective-permute-start(bf16[128,1024]{1,0:T(8,128)(2,1)} %collective-permute-done.3), channel_id=1, source_target_pairs={{0,24},{1,25},{2,26},{3,27},{4,28},{5,29},{6,30},{7,31},{8,16},{9,... | collective-permute-start | bytes 786440 | tf_op jit(solution)/shard_map/ppermute | solution.py:23
  43.7 28.2 %collective-permute-start.4 = (bf16[1,4,1,256,1024]{4,3,1,2,0:T(8,128)(2,1)}, bf16[1,4,1,256,1024]{4,3,1,2,0:T(8,128)(2,1)}, u32[]{:S(2)}, u32[]{:S(2)}) collective-permute-start(bf16[1,4,1,256,1024]{4,3,1,2,0:T(8,128)(2,1)} %fusion.73), channel_id=1, source_target_pairs={{0,1},{1,0},{2,3},{3,2},{4,5},{5,4},{6,7},{7,6},{8,9},{9,8},{10,11... | collective-permute-start | bytes 6291464 | tf_op jit(solution)/shard_map/ppermute | solution.py:23
  54.6 20.6 %collective-permute-start.13 = (bf16[1,4,1,256,1024]{4,3,1,2,0:T(8,128)(2,1)}, bf16[1,4,1,256,1024]{4,3,1,2,0:T(8,128)(2,1)}, u32[]{:S(2)}, u32[]{:S(2)}) collective-permute-start(bf16[1,4,1,256,1024]{4,3,1,2,0:T(8,128)(2,1)} %fusion.74), channel_id=1, source_target_pairs={{0,1},{1,0},{2,3},{3,2},{4,5},{5,4},{6,7},{7,6},{8,9},{9,8},{10,11... | collective-permute-start | bytes 6291464 | tf_op jit(solution)/shard_map/ppermute | solution.py:23
  82.6 25.6 %collective-permute-start.17 = (bf16[2,256,1024]{2,1,0:T(8,128)(2,1)}, bf16[2,256,1024]{2,1,0:T(8,128)(2,1)S(1)}, u32[]{:S(2)}, u32[]{:S(2)}) collective-permute-start(bf16[2,256,1024]{2,1,0:T(8,128)(2,1)} %bitcast.24), channel_id=1, source_target_pairs={{0,6},{1,7},{2,0},{3,1},{4,2},{5,3},{6,4},{7,5},{8,14},{9,15},{10,... | collective-permute-start | bytes 3145736 | tf_op jit(solution)/shard_map/ppermute | solution.py:23
  85.3 30.3 %collective-permute-start.21 = (bf16[2,256,1024]{2,1,0:T(8,128)(2,1)}, bf16[2,256,1024]{2,1,0:T(8,128)(2,1)}, u32[]{:S(2)}, u32[]{:S(2)}) collective-permute-start(bf16[2,256,1024]{2,1,0:T(8,128)(2,1)} %bitcast.24), channel_id=1, source_target_pairs={{0,2},{1,3},{2,4},{3,5},{4,6},{5,7},{6,0},{7,1},{8,10},{9,11},{10,... | collective-permute-start | bytes 3145736 | tf_op jit(solution)/shard_map/ppermute | solution.py:23
  91.2 39.4 %collective-permute-start.16 = (bf16[2,256,1024]{2,1,0:T(8,128)(2,1)}, bf16[2,256,1024]{2,1,0:T(8,128)(2,1)}, u32[]{:S(2)}, u32[]{:S(2)}) collective-permute-start(bf16[2,256,1024]{2,1,0:T(8,128)(2,1)} %bitcast.21), channel_id=1, source_target_pairs={{0,6},{1,7},{2,0},{3,1},{4,2},{5,3},{6,4},{7,5},{8,14},{9,15},{10,... | collective-permute-start | bytes 3145736 | tf_op jit(solution)/shard_map/ppermute | solution.py:23
  93.9 40.2 %collective-permute-start.20 = (bf16[2,256,1024]{2,1,0:T(8,128)(2,1)}, bf16[2,256,1024]{2,1,0:T(8,128)(2,1)}, u32[]{:S(2)}, u32[]{:S(2)}) collective-permute-start(bf16[2,256,1024]{2,1,0:T(8,128)(2,1)} %bitcast.21), channel_id=1, source_target_pairs={{0,2},{1,3},{2,4},{3,5},{4,6},{5,7},{6,0},{7,1},{8,10},{9,11},{10,... | collective-permute-start | bytes 3145736 | tf_op jit(solution)/shard_map/ppermute | solution.py:23
  93.9 42.4 %collective-permute-start.15 = (bf16[2,256,1024]{2,1,0:T(8,128)(2,1)}, bf16[2,256,1024]{2,1,0:T(8,128)(2,1)}, u32[]{:S(2)}, u32[]{:S(2)}) collective-permute-start(bf16[2,256,1024]{2,1,0:T(8,128)(2,1)} %bitcast.24), channel_id=1, source_target_pairs={{0,1},{1,0},{2,3},{3,2},{4,5},{5,4},{6,7},{7,6},{8,9},{9,8},{10,11... | collective-permute-start | bytes 3145736 | tf_op jit(solution)/shard_map/ppermute | solution.py:23
  108.2 31.2 %collective-permute-start.14 = (bf16[2,256,1024]{2,1,0:T(8,128)(2,1)}, bf16[2,256,1024]{2,1,0:T(8,128)(2,1)}, u32[]{:S(2)}, u32[]{:S(2)}) collective-permute-start(bf16[2,256,1024]{2,1,0:T(8,128)(2,1)} %bitcast.21), channel_id=1, source_target_pairs={{0,1},{1,0},{2,3},{3,2},{4,5},{5,4},{6,7},{7,6},{8,9},{9,8},{10,11... | collective-permute-start | bytes 3145736 | tf_op jit(solution)/shard_map/ppermute | solution.py:23
  115.6 39.0 %collective-permute-start.19 = (bf16[2,256,1024]{2,1,0:T(8,128)(2,1)}, bf16[2,256,1024]{2,1,0:T(8,128)(2,1)}, u32[]{:S(2)}, u32[]{:S(2)}) collective-permute-start(bf16[2,256,1024]{2,1,0:T(8,128)(2,1)} %bitcast.24), channel_id=1, source_target_pairs={{0,8},{1,9},{2,10},{3,11},{4,12},{5,13},{6,14},{7,15},{8,0},{9,1},... | collective-permute-start | bytes 3145736 | tf_op jit(solution)/shard_map/ppermute | solution.py:23
  130.6 43.7 %collective-permute-start.18 = (bf16[2,256,1024]{2,1,0:T(8,128)(2,1)}, bf16[2,256,1024]{2,1,0:T(8,128)(2,1)S(1)}, u32[]{:S(2)}, u32[]{:S(2)}) collective-permute-start(bf16[2,256,1024]{2,1,0:T(8,128)(2,1)} %bitcast.21), channel_id=1, source_target_pairs={{0,8},{1,9},{2,10},{3,11},{4,12},{5,13},{6,14},{7,15},{8,0},{9,1},... | collective-permute-start | bytes 3145736 | tf_op jit(solution)/shard_map/ppermute | solution.py:23
  134.1 43.7 %collective-permute-start.28 = (bf16[1,256,1024]{2,1,0:T(8,128)(2,1)S(1)}, bf16[1,256,1024]{2,1,0:T(8,128)(2,1)}, u32[]{:S(2)}, u32[]{:S(2)}) collective-permute-start(bf16[1,256,1024]{2,1,0:T(8,128)(2,1)S(1)} %slice.140), channel_id=1, source_target_pairs={{0,6},{1,7},{2,0},{3,1},{4,2},{5,3},{6,4},{7,5},{8,14},{9,15},{10,... | collective-permute-start | bytes 1572872 | tf_op jit(solution)/shard_map/ppermute | solution.py:23
  136.3 43.9 %collective-permute-start.29 = (bf16[1,256,1024]{2,1,0:T(8,128)(2,1)S(1)}, bf16[1,256,1024]{2,1,0:T(8,128)(2,1)}, u32[]{:S(2)}, u32[]{:S(2)}) collective-permute-start(bf16[1,256,1024]{2,1,0:T(8,128)(2,1)S(1)} %slice.141), channel_id=1, source_target_pairs={{0,2},{1,3},{2,4},{3,5},{4,6},{5,7},{6,0},{7,1},{8,10},{9,11},{10,... | collective-permute-start | bytes 1572872 | tf_op jit(solution)/shard_map/ppermute | solution.py:23
  139.4 51.7 %collective-permute-start.26 = (bf16[1,256,1024]{2,1,0:T(8,128)(2,1)S(1)}, bf16[1,256,1024]{2,1,0:T(8,128)(2,1)}, u32[]{:S(2)}, u32[]{:S(2)}) collective-permute-start(bf16[1,256,1024]{2,1,0:T(8,128)(2,1)S(1)} %slice.138), channel_id=1, source_target_pairs={{0,6},{1,7},{2,0},{3,1},{4,2},{5,3},{6,4},{7,5},{8,14},{9,15},{10,... | collective-permute-start | bytes 1572872 | tf_op jit(solution)/shard_map/ppermute | solution.py:23
  154.5 36.7 %collective-permute-start.27 = (bf16[1,256,1024]{2,1,0:T(8,128)(2,1)S(1)}, bf16[1,256,1024]{2,1,0:T(8,128)(2,1)}, u32[]{:S(2)}, u32[]{:S(2)}) collective-permute-start(bf16[1,256,1024]{2,1,0:T(8,128)(2,1)S(1)} %slice.139), channel_id=1, source_target_pairs={{0,2},{1,3},{2,4},{3,5},{4,6},{5,7},{6,0},{7,1},{8,10},{9,11},{10,... | collective-permute-start | bytes 1572872 | tf_op jit(solution)/shard_map/ppermute | solution.py:23
  174.3 63.3 %collective-permute-start.23 = (bf16[2,256,1024]{2,1,0:T(8,128)(2,1)}, bf16[2,256,1024]{2,1,0:T(8,128)(2,1)}, u32[]{:S(2)}, u32[]{:S(2)}) collective-permute-start(bf16[2,256,1024]{2,1,0:T(8,128)(2,1)} %collective-permute-done.19), channel_id=1, source_target_pairs={{0,6},{1,7},{2,0},{3,1},{4,2},{5,3},{6,4},{7,5},{8,14},{9,15},{10,... | collective-permute-start | bytes 3145736 | tf_op jit(solution)/shard_map/ppermute | solution.py:23
  177.8 17.4 %collective-permute-start.32 = (bf16[1,256,1024]{2,1,0:T(8,128)(2,1)}, bf16[1,256,1024]{2,1,0:T(8,128)(2,1)}, u32[]{:S(2)}, u32[]{:S(2)}) collective-permute-start(bf16[1,256,1024]{2,1,0:T(8,128)(2,1)} %collective-permute-done.28), channel_id=1, source_target_pairs={{0,8},{1,9},{2,10},{3,11},{4,12},{5,13},{6,14},{7,15},{8,0},{9,1},... | collective-permute-start | bytes 1572872 | tf_op jit(solution)/shard_map/ppermute | solution.py:23
  180.2 21.5 %collective-permute-start.33 = (bf16[1,256,1024]{2,1,0:T(8,128)(2,1)}, bf16[1,256,1024]{2,1,0:T(8,128)(2,1)}, u32[]{:S(2)}, u32[]{:S(2)}) collective-permute-start(bf16[1,256,1024]{2,1,0:T(8,128)(2,1)} %collective-permute-done.29), channel_id=1, source_target_pairs={{0,8},{1,9},{2,10},{3,11},{4,12},{5,13},{6,14},{7,15},{8,0},{9,1},... | collective-permute-start | bytes 1572872 | tf_op jit(solution)/shard_map/ppermute | solution.py:23
  183.4 67.1 %all-to-all-start = ((bf16[8,2,32,1024]{3,2,1,0:T(8,128)(2,1)}), bf16[8,2,32,1024]{3,2,1,0:T(8,128)(2,1)S(1)}, u32[]{:S(2)}, u32[]{:S(2)}) async-start(bf16[8,2,32,1024]{3,2,1,0:T(8,128)(2,1)} %copy.59), calls=%async_computation | async-start | bytes 2097152 | tf_op jit(solution)/shard_map/all_to_all | solution.py:88
  191.1 33.0 %collective-permute-start.30 = (bf16[1,256,1024]{2,1,0:T(8,128)(2,1)}, bf16[1,256,1024]{2,1,0:T(8,128)(2,1)S(1)}, u32[]{:S(2)}, u32[]{:S(2)}) collective-permute-start(bf16[1,256,1024]{2,1,0:T(8,128)(2,1)} %collective-permute-done.26), channel_id=1, source_target_pairs={{0,8},{1,9},{2,10},{3,11},{4,12},{5,13},{6,14},{7,15},{8,0},{9,1},... | collective-permute-start | bytes 1572872 | tf_op jit(solution)/shard_map/ppermute | solution.py:23
  191.3 44.1 %collective-permute-start.31 = (bf16[1,256,1024]{2,1,0:T(8,128)(2,1)}, bf16[1,256,1024]{2,1,0:T(8,128)(2,1)S(1)}, u32[]{:S(2)}, u32[]{:S(2)}) collective-permute-start(bf16[1,256,1024]{2,1,0:T(8,128)(2,1)} %collective-permute-done.27), channel_id=1, source_target_pairs={{0,8},{1,9},{2,10},{3,11},{4,12},{5,13},{6,14},{7,15},{8,0},{9,1},... | collective-permute-start | bytes 1572872 | tf_op jit(solution)/shard_map/ppermute | solution.py:23
  195.2 45.0 %collective-permute-start.25 = (bf16[2,256,1024]{2,1,0:T(8,128)(2,1)}, bf16[2,256,1024]{2,1,0:T(8,128)(2,1)S(1)}, u32[]{:S(2)}, u32[]{:S(2)}) collective-permute-start(bf16[2,256,1024]{2,1,0:T(8,128)(2,1)} %collective-permute-done.19), channel_id=1, source_target_pairs={{0,2},{1,3},{2,4},{3,5},{4,6},{5,7},{6,0},{7,1},{8,10},{9,11},{10,... | collective-permute-start | bytes 3145736 | tf_op jit(solution)/shard_map/ppermute | solution.py:23
  201.7 40.8 %collective-permute-start.22 = (bf16[2,256,1024]{2,1,0:T(8,128)(2,1)S(1)}, bf16[2,256,1024]{2,1,0:T(8,128)(2,1)S(1)}, u32[]{:S(2)}, u32[]{:S(2)}) collective-permute-start(bf16[2,256,1024]{2,1,0:T(8,128)(2,1)S(1)} %copy-done.16), channel_id=1, source_target_pairs={{0,6},{1,7},{2,0},{3,1},{4,2},{5,3},{6,4},{7,5},{8,14},{9,15},{10,... | collective-permute-start | bytes 3145736 | tf_op jit(solution)/shard_map/ppermute | solution.py:23
  224.1 22.3 %collective-permute-start.24 = (bf16[2,256,1024]{2,1,0:T(8,128)(2,1)S(1)}, bf16[2,256,1024]{2,1,0:T(8,128)(2,1)S(1)}, u32[]{:S(2)}, u32[]{:S(2)}) collective-permute-start(bf16[2,256,1024]{2,1,0:T(8,128)(2,1)S(1)} %copy-done.16), channel_id=1, source_target_pairs={{0,2},{1,3},{2,4},{3,5},{4,6},{5,7},{6,0},{7,1},{8,10},{9,11},{10,... | collective-permute-start | bytes 3145736 | tf_op jit(solution)/shard_map/ppermute | solution.py:23
  250.4 24.1 %all-to-all-start.1 = ((bf16[8,2,32,1024]{3,2,1,0:T(8,128)(2,1)}), bf16[8,2,32,1024]{3,2,1,0:T(8,128)(2,1)S(1)}, u32[]{:S(2)}, u32[]{:S(2)}) async-start(bf16[8,2,32,1024]{3,2,1,0:T(8,128)(2,1)} %copy.61), calls=%async_computation.1 | async-start | bytes 2097152 | tf_op jit(solution)/shard_map/all_to_all | solution.py:88
  289.7 43.9 %collective-permute-start.36 = (bf16[256,1024]{0,1:T(8,128)(2,1)S(1)}, bf16[256,1024]{0,1:T(8,128)(2,1)S(1)}, u32[]{:S(2)}, u32[]{:S(2)}) collective-permute-start(bf16[256,1024]{0,1:T(8,128)(2,1)S(1)} %fusion.15), channel_id=1, source_target_pairs={{0,0},{1,1},{2,16},{3,17},{4,32},{5,33},{6,48},{7,49},{8,64},{9,65... | collective-permute-start | bytes 1572872 | tf_op jit(solution)/shard_map/ppermute | solution.py:23
  296.1 43.8 %all-to-all-start.2 = ((bf16[8,32,2048]{2,1,0:T(8,128)(2,1)}), bf16[8,32,2048]{2,1,0:T(8,128)(2,1)S(1)}, u32[]{:S(2)}, u32[]{:S(2)}) async-start(bf16[8,32,2048]{2,1,0:T(8,128)(2,1)} %pad_maximum_fusion.4), calls=%async_computation.2 | async-start | bytes 2097152 | tf_op jit(solution)/shard_map/all_to_all | solution.py:165
  (29 other events, 283.8 us)
Sparse Core Ops, SparseCore 0:
  94.9 65.6 all-gather.2

commit v2 on v1

v2 whole, which is shorter than its diff:
```python
import jax
import jax.numpy as jnp
from jax import lax
from jax.experimental import pallas as pl
from jax.experimental.pallas import tpu as pltpu
from jax.sharding import Mesh, PartitionSpec as P

ATILE = 32
AXES = ("grp", "chip", "core")
NZ, NH, NA, NY, NK = 4, 2, 2, 4, 2


def device(z, h, a, y, k):
    return ((z * NH + h) * NA + a) * NY * NK + y * NK + k


def moved(x, where):
    pairs = []
    for z in range(NZ):
        for h in range(NH):
            for a in range(NA):
                for y in range(NY):
                    for k in range(NK):
                        pairs.append((device(z, h, a, y, k), device(*where(z, h, a, y, k))))
    return lax.ppermute(x, AXES, pairs)


def from_next(x):
    return moved(x, lambda z, h, a, y, k: (z, h, a, (y - 1) % NY, k))


def from_prev(x):
    return moved(x, lambda z, h, a, y, k: (z, h, a, (y + 1) % NY, k))


def across_in(x):
    return moved(x, lambda z, h, a, y, k: (z, h, 1 - a, y, k))


def across_out(x):
    return moved(x, lambda z, h, a, y, k: (z, 1 - h, 1 - a, y, k))


def other_core(x):
    return moved(x, lambda z, h, a, y, k: (z, h, a, y, 1 - k))


def mirror(z, h, a, y, k):
    chip, group = a * NY + y, z * NH + h
    return (chip // NH, chip % NH, group // NY, group % NY, k)


def mirrored(x):
    return moved(x, mirror)


def mirrored_cross(x):
    def where(z, h, a, y, k):
        return mirror(z, h, a, y, 1 - k)

    return moved(x, where)


def to_absolute(rel, a, y):
    twice = jnp.concatenate([rel, rel], axis=1)
    turned = lax.dynamic_slice_in_dim(twice, (NY - y) % NY, NY, 1)
    return jnp.where(a == 0, turned, turned[::-1])


def after(x, *earlier):
    return lax.optimization_barrier((x,) + earlier)[0]


def masked_block(keep_ref, slab_ref):
    rows = slab_ref.shape[1]
    keep = keep_ref[...]
    wide = jnp.broadcast_to(keep[:, None, :], (keep.shape[0], ATILE, keep.shape[1]))
    wide = wide.reshape(rows, keep.shape[1]).astype(jnp.bfloat16)
    both = slab_ref[...] * wide[None]
    return both.reshape(slab_ref.shape[0] * rows, keep.shape[1])


def mask_kernel(cols, *refs):
    count = len(refs) // 3
    for at in range(count):
        refs[2 * count + at][...] = masked_block(refs[at], refs[count + at])


def masked_columns(cols, keep, slab, depth, steps):
    aux_dev, rows, nao = slab.shape
    count = nao // (depth * steps)
    keep_spec = [
        pl.BlockSpec((keep.shape[0], depth), lambda s, c, t=t: (0, c[t * steps + s]))
        for t in range(count)
    ]
    slab_spec = [
        pl.BlockSpec((aux_dev, rows, depth), lambda s, c, t=t: (0, 0, c[t * steps + s]))
        for t in range(count)
    ]
    return pl.pallas_call(
        mask_kernel,
        out_shape=[jax.ShapeDtypeStruct((aux_dev * rows, depth * steps), slab.dtype)] * count,
        grid_spec=pltpu.PrefetchScalarGridSpec(
            num_scalar_prefetch=1,
            grid=(steps,),
            in_specs=keep_spec + slab_spec,
            out_specs=[pl.BlockSpec((aux_dev * rows, depth), lambda s, c: (0, s))] * count,
        ),
        compiler_params=pltpu.CompilerParams(vmem_limit_bytes=40 << 20),
        name="masked_columns",
    )(cols, *[keep] * count, *[slab] * count)


def margin_kernel(cols, m1, m2, flag_ref, n1, n2, x1, x2, out_ref, acc):
    step = pl.program_id(0)
    half = pl.num_programs(0) // 2

    def add(c1, c2):
        left = jnp.concatenate([m1[0], m2[0]], axis=1)
        right = jnp.concatenate([c1[0], c2[0]], axis=0)
        acc[...] += jnp.dot(left, right, preferred_element_type=jnp.float32)

    @pl.when(step == 0)
    def _():
        acc[...] = jnp.zeros_like(acc)

    @pl.when(step < half)
    def _():
        add(n1, n2)

    @pl.when(step >= half)
    def _():
        add(x1, x2)

    @pl.when(step == pl.num_programs(0) - 1)
    def _():
        out_ref[...] = (acc[...] * flag_ref[...]).astype(out_ref.dtype)


def margin_env(cols, margin_row, flag, near, near_oth, cross, cross_oth):
    steps, depth, occ = near.shape
    rows = margin_row.shape[1]
    m_spec = [
        pl.BlockSpec(
            (1, rows, depth),
            lambda s, c, t=t: (c[t * 2 * steps + s] // NK, 0, c[t * 2 * steps + s] % NK),
        )
        for t in range(2)
    ]
    n_spec = pl.BlockSpec((1, depth, occ), lambda s, c: (jnp.minimum(s, steps - 1), 0, 0))
    x_spec = pl.BlockSpec((1, depth, occ), lambda s, c: (jnp.maximum(s - steps, 0), 0, 0))
    f_spec = pl.BlockSpec((1, occ), lambda s, c: (0, 0))
    return pl.pallas_call(
        margin_kernel,
        out_shape=jax.ShapeDtypeStruct((rows, occ), jnp.bfloat16),
        grid_spec=pltpu.PrefetchScalarGridSpec(
            num_scalar_prefetch=1,
            grid=(2 * steps,),
            in_specs=m_spec + [f_spec, n_spec, n_spec, x_spec, x_spec],
            out_specs=pl.BlockSpec((rows, occ), lambda s, c: (0, 0)),
            scratch_shapes=[pltpu.VMEM((rows, occ), jnp.float32)],
        ),
        compiler_params=pltpu.CompilerParams(vmem_limit_bytes=40 << 20),
        cost_estimate=pl.CostEstimate(
            flops=8 * rows * occ * depth * steps,
            transcendentals=0,
            bytes_accessed=8 * steps * depth * (rows + occ),
        ),
        name="margin_env",
    )(cols, margin_row, margin_row, flag, near, near_oth, cross, cross_oth)


def pair_kernel(core_ref, mine_ref, mate_ref, *refs):
    blocks, rest = refs[: len(refs) - 3], refs[len(refs) - 3 :]
    base_ref, out_ref, acc = rest
    run_pair(core_ref, mine_ref, mate_ref, blocks, base_ref, out_ref, acc)


def run_pair(core_ref, mine_ref, mate_ref, blocks, base_ref, out_ref, acc):
    step = pl.program_id(0)
    contract = (((1,), (1,)), ((), ()))
    left = jnp.concatenate([mine_ref[0], mate_ref[0]], axis=0)
    for at, block in enumerate(blocks):
        width = block.shape[1]
        cols = slice(at * width, (at + 1) * width)
        part = lax.dot_general(left, block[0], contract, preferred_element_type=jnp.float32)

        @pl.when(step == 0)
        def _():
            acc[:, cols] = part if base_ref is None else base_ref[:, cols] + part

        @pl.when(step > 0)
        def _():
            acc[:, cols] += part

    @pl.when(step == pl.num_programs(0) - 1)
    def _():
        if out_ref.shape == acc.shape:
            out_ref[...] = acc[...]
        else:
            core = core_ref[0]
            rows = mine_ref.shape[1]
            cut = out_ref.shape[:1] + out_ref.shape[2:]
            out_ref[:, core] = acc[:rows].reshape(cut).astype(out_ref.dtype)
            out_ref[:, 1 - core] = acc[rows:].reshape(cut).astype(out_ref.dtype)


def first_pair_kernel(core_ref, mine_ref, mate_ref, *refs):
    run_pair(core_ref, mine_ref, mate_ref, refs[:-2], None, refs[-2], refs[-1])


def pair_tiles(core, mine, mate, blocks, start=0, base=None, cut=True):
    depth, rows, occ = blocks[0].shape
    cols = rows * len(blocks)
    spec = pl.BlockSpec((1, rows, occ), lambda s, c: (s, 0, 0))
    own_spec = pl.BlockSpec((1, rows, occ), lambda s, c: (s + start, 0, 0))
    in_specs = [own_spec, own_spec] + [spec] * len(blocks)
    args = [core.reshape(1), mine, mate, *blocks]
    body = first_pair_kernel
    if base is not None:
        body = pair_kernel
        in_specs.append(pl.BlockSpec((2 * rows, cols), lambda s, c: (0, 0)))
        args.append(base)
    if cut:
        out = jax.ShapeDtypeStruct((8, 2, rows // 8, cols), jnp.bfloat16)
        out_spec = pl.BlockSpec(out.shape, lambda s, c: (0, 0, 0, 0))
    else:
        out = jax.ShapeDtypeStruct((2 * rows, cols), jnp.float32)
        out_spec = pl.BlockSpec(out.shape, lambda s, c: (0, 0))
    return pl.pallas_call(
        body,
        out_shape=out,
        grid_spec=pltpu.PrefetchScalarGridSpec(
            num_scalar_prefetch=1,
            grid=(depth,),
            in_specs=in_specs,
            out_specs=out_spec,
            scratch_shapes=[pltpu.VMEM((2 * rows, cols), jnp.float32)],
        ),
        compiler_params=pltpu.CompilerParams(vmem_limit_bytes=48 << 20),
        cost_estimate=pl.CostEstimate(
            flops=4 * rows * cols * depth * occ,
            transcendentals=0,
            bytes_accessed=2 * depth * occ * (2 * rows + cols) + 4 * rows * cols,
        ),
        name="exchange_tiles",
    )(*args)


def exchanged(cut):
    rows, cols = cut.shape[2:]
    return lax.all_to_all(cut.reshape(16, rows, cols), ("grp", "core"), 0, 0)


def sum_groups(got_ref, first):
    total = got_ref[first].astype(jnp.float32)
    for at in range(1, got_ref.shape[0] // 2):
        total += got_ref[2 * at + first].astype(jnp.float32)
    return total


def rows_times(rows, first, block):
    depth = block.shape[0]
    left = rows[:, first * depth : (first + 1) * depth].astype(jnp.bfloat16)
    return jnp.dot(left, block, preferred_element_type=jnp.float32)


def early_kernel(core_ref, got, near, near_oth, cross, cross_oth, k_ref, b_ref):
    core = core_ref[0]
    total = jnp.zeros(b_ref.shape, jnp.float32)
    for t, (nc, cc) in enumerate(((near, cross), (near_oth, cross_oth))):
        rows = sum_groups(got, core if t == 0 else 1 - core)
        k_ref[t] = rows
        for at, block in enumerate((nc[0], nc[1], nc[2], cc[0], nc[3])):
            total += rows_times(rows, at, block)
    b_ref[...] = total


def late_kernel(scalars, got, k_early, b_early, flag, cross, cross_oth, out_ref):
    core = scalars[0]
    occ = b_early.shape[1]
    depth = cross.shape[1]
    total = b_early[...]
    for t, cc in enumerate((cross, cross_oth)):
        rows = sum_groups(got, core if t == 0 else 1 - core)
        for at, block in enumerate((cc[3], cc[1], cc[2])):
            total += rows_times(rows, at, block)
        tiles = [k_early[t, :, at * depth : (at + 1) * depth] for at in range(5)]
        tiles += [rows[:, at * depth : (at + 1) * depth] for at in range(3)]
        first = occ + t * depth
        for at, place in enumerate((0, 1, 2, 4, 3, 7, 5, 6)):
            hi = tiles[at].astype(jnp.bfloat16)
            lo = (tiles[at] - hi.astype(jnp.float32)).astype(jnp.bfloat16)
            chip = scalars[1 + place]
            out_ref[chip, :, first : first + depth] = hi
            out_ref[chip, :, first + 2 * depth : first + 3 * depth] = lo
    b_rows = (total * flag[...]).astype(jnp.bfloat16)
    for at in range(out_ref.shape[0]):
        out_ref[at, :, :occ] = b_rows


def on_chip(body, name, out_shape, scalars, *args):
    flops = 4 * args[0].shape[1] * args[0].shape[2] * 1024
    return pl.pallas_call(
        body,
        out_shape=out_shape,
        in_specs=[pl.BlockSpec(memory_space=pltpu.SMEM)]
        + [pl.BlockSpec(memory_space=pltpu.VMEM)] * len(args),
        compiler_params=pltpu.CompilerParams(vmem_limit_bytes=40 << 20),
        cost_estimate=pl.CostEstimate(flops=flops, transcendentals=0, bytes_accessed=8 << 20),
        name=name,
    )(scalars, *args)


def early_rows(core, got, near, near_oth, cross, cross_oth):
    rows, cols = got.shape[1:]
    occ = near.shape[2]
    shapes = [
        jax.ShapeDtypeStruct((2, rows, cols), jnp.float32),
        jax.ShapeDtypeStruct((rows, occ), jnp.float32),
    ]
    args = (got, near, near_oth, cross, cross_oth)
    return on_chip(early_kernel, "early_rows", shapes, core.reshape(1), *args)


def late_rows(scalars, got, k_early, b_early, flag, cross, cross_oth):
    rows, occ = b_early.shape
    shape = jax.ShapeDtypeStruct((8, rows, occ + 4 * cross.shape[1]), jnp.bfloat16)
    args = (got, k_early, b_early, flag, cross, cross_oth)
    return on_chip(late_kernel, "late_rows", shape, scalars, *args)


def on_device(slab, block_mask, orbitals, margin, env_flag):
    aux_dev, ao_dev, nao = slab.shape
    occ = orbitals.shape[1]
    chip, core = lax.axis_index("chip"), lax.axis_index("core")
    a, y = chip // NY, chip % NY
    hb = ao_dev // 2
    flag = env_flag.astype(jnp.float32)[None, :]

    margin_row = lax.all_gather(margin, "grp", axis=0)
    order = (y + jnp.array([0, 1, NY - 1, 2], jnp.int32)) % NY
    near_cols = ((a * NY + order) * NK).astype(jnp.int32)
    cross_cols = (((1 - a) * NY + order) * NK).astype(jnp.int32)
    near_cols = jnp.concatenate([near_cols + core, near_cols + 1 - core])
    cross_cols = jnp.concatenate([cross_cols + core, cross_cols + 1 - core])
    keep = jnp.repeat(block_mask[0], ATILE, axis=1).astype(jnp.float32)
    masked = masked_columns(jnp.concatenate([near_cols, cross_cols]), keep, slab, ao_dev, NY)

    def product(left, right):
        return jnp.dot(left, right.reshape(-1, occ), preferred_element_type=jnp.float32)

    def cross_over(t):
        return [across_in(t[:hb]), across_out(t[hb:])]

    nxt, prv, *own_x, masked = lax.optimization_barrier(
        (from_next(orbitals), from_prev(orbitals), *cross_over(orbitals), masked)
    )
    far_lo, far_hi, *side_x = lax.optimization_barrier(
        (from_next(nxt[:hb]), from_prev(prv[hb:]), *cross_over(nxt), *cross_over(prv))
    )
    near = jnp.concatenate([orbitals, nxt, prv, far_lo, far_hi]).reshape(NY, ao_dev, occ)
    base = product(masked[0], near)
    near_oth, far_lo_x, far_hi_x, base = lax.optimization_barrier(
        (other_core(near), across_in(far_lo), across_out(far_hi), base)
    )
    cross = jnp.concatenate([*own_x, *side_x, far_lo_x, far_hi_x]).reshape(NY, ao_dev, occ)
    base += product(masked[1], near_oth)
    cross_oth, base = lax.optimization_barrier((other_core(cross), base))
    part = base + product(masked[2], cross) + product(masked[3], cross_oth)
    part = part.astype(jnp.bfloat16).reshape(aux_dev, ao_dev, occ)
    mid = aux_dev // 2

    x, n, p = across_in(part), from_next(part), from_prev(part)
    mate = other_core(part)
    gcols = jnp.concatenate([near_cols[:4], cross_cols[:4], near_cols[4:], cross_cols[4:]])
    a_rows = margin_env(gcols, margin_row, flag, after(near, mate), near_oth, cross, cross_oth)
    f, g = from_next(n[:mid]), from_prev(p[mid:])
    f, g, x, a_rows = lax.optimization_barrier((f, g, x, a_rows))
    xn, xp, xf = from_next(x), from_prev(x), across_in(f)
    xg = across_in(after(g, xf))

    far = jnp.concatenate([f, g])
    part_e, mate_e, _ = lax.optimization_barrier((part, mate, xf))
    early = pair_tiles(core, part_e, mate_e, [part, n, p, x, far])
    early = exchanged(early)
    k_early, b_early = early_rows(core, early, near, near_oth, cross, cross_oth)

    xfar = jnp.concatenate([xf, xg])
    late = pair_tiles(core, part, mate, [xfar, xn, xp])
    a_own = mirrored(after(a_rows, xn, xp))
    late, b_early, k_early, a_own = lax.optimization_barrier((late, b_early, k_early, a_own))
    late = exchanged(late)
    a_oth = other_core(a_own)
    places = jnp.concatenate([near_cols[:4], cross_cols[:4]]) // NK
    scalars = jnp.concatenate([core.reshape(1), places]).astype(jnp.int32)
    packed = late_rows(scalars, late, k_early, b_early, flag, cross, cross_oth)
    got = lax.all_to_all(packed, "grp", 0, 0).reshape(ao_dev, -1)
    b_all = got[:, :occ]
    k_tile = got[:, occ : occ + 512].astype(jnp.float32) + got[:, occ + 512 :].astype(jnp.float32)
    contract = (((1,), (1,)), ((), ()))
    z_own = lax.dot_general(b_all, a_own, contract, preferred_element_type=jnp.float32)
    z_oth = lax.dot_general(b_all, a_oth, contract, preferred_element_type=jnp.float32)
    t_own = mirrored(z_own.astype(jnp.bfloat16))
    t_oth = mirrored_cross(z_oth.astype(jnp.bfloat16))
    out_own = k_tile[:, :256] - z_own - t_own.astype(jnp.float32).T
    out_oth = k_tile[:, 256:] - z_oth - t_oth.astype(jnp.float32).T
    straight = jnp.concatenate([out_own, out_oth], axis=1)
    swapped = jnp.concatenate([out_oth, out_own], axis=1)
    return jnp.where(core == 0, straight, swapped)


def solution(mesh):
    fine = Mesh(mesh.devices.reshape(8, NA * NY, NK), AXES)
    blk = ("chip", "core")
    placed = (P("grp", blk, None), P("grp", blk, None), P(blk, None), P(blk, "grp"), P())
    return jax.shard_map(
        on_device, mesh=fine, in_specs=placed, out_specs=P(blk, "grp"), check_vma=False
    )
```

time: 372 us -> 311 us (0.84); the launches traced: 364 us -> 308 us
  Pallas kernels: 0 us -> 44.8 us
  matrix products: 60.9 us -> 18.4 us
  other arithmetic: 31.7 us -> 9.53 us
  local copies, waits for them, and re-layouts: 40 us -> 19.4 us
  starting transfers between devices: 80 us -> 66.2 us
    pallas_call x0 -> x6, Pallas kernels: none -> 44.8 us  [the longest x2 26.4 us: pair_tiles(): pl.pallas_call(body, out_shape=out, grid_spec=pltpu.PrefetchScalarGridSpe...]
    dot_general x20 -> x4, matrix products: 60.2 us -> 16.7 us  [product(): jnp.dot(left, right.reshape(-1, occ), preferred_element_type=jnp.float32)]
    ppermute x40 -> x28, waiting for transfers between devices: 134 us -> 111 us  [moved(): return lax.ppermute(x, AXES, pairs)]
    all_to_all x3, waiting for transfers between devices: 3.07 us -> 25.1 us  [the longest x1 12.7 us: on_device(): got = lax.all_to_all(packed, 'grp', 0, 0).reshape(ao_dev, -1)]
    ppermute x40 -> x28, starting transfers between devices: 58.3 us -> 42.1 us  [moved(): return lax.ppermute(x, AXES, pairs)]
    reshape x2 -> x0, local copies, waits for them, and re-layouts: 11.8 us -> none  [the longest x1 11.4 us: on_device(): whole_c = whole_c.reshape(nao, occ)]
    unnamed x44 -> x65, local copies, waits for them, and re-layouts: 5.27 us -> 16.1 us
    slice x8 -> x5, local copies, waits for them, and re-layouts: 10.7 us -> 2.54 us  [the longest x2 1.41 us: on_device(): f, g = (from_next(n[:mid]), from_prev(p[mid:]))]
  transfers between devices with their start and end apart: 44 -> 32, of which waited for: 15 -> 15; matrix products, arithmetic and copies ran while one was open for 33% -> 10% of each run, Pallas kernels for 0% -> 13%
where the time goes in v2:
time: 311 us; the launch traced here: 308 us
  waiting for transfers between devices  136 us (44%)
  starting transfers between devices  66.2 us (21%)
  Pallas kernels  44.8 us (14%)
  local copies, waits for them, and re-layouts  19.4 us (6%)
  matrix products  18.4 us (6%)
  between operations  13.9 us (4%)
  other arithmetic  9.53 us (3%)
    ppermute x28, waiting for transfers between devices, moved(): return lax.ppermute(x, AXES, pairs)  111 us
    ppermute x28, starting transfers between devices, moved(): return lax.ppermute(x, AXES, pairs)  42.1 us
    pallas_call x2, Pallas kernels, pair_tiles(): pl.pallas_call(body, out_shape=out, grid_spec=pltpu.PrefetchScalarGridSpe...  26.4 us
    all_to_all x2, starting transfers between devices, exchanged(): return lax.all_to_all(cut.reshape(16, rows, cols), ('grp', 'core'), 0, 0)  18.7 us
    dot_general x4, matrix products, product(): jnp.dot(left, right.reshape(-1, occ), preferred_element_type=jnp.float32)  16.7 us
    unnamed x65, local copies, waits for them, and re-layouts  16.1 us
    all_to_all x1, waiting for transfers between devices, on_device(): got = lax.all_to_all(packed, 'grp', 0, 0).reshape(ao_dev, -1)  12.7 us
    all_to_all x2, waiting for transfers between devices, exchanged(): return lax.all_to_all(cut.reshape(16, rows, cols), ('grp', 'core'), 0, 0)  12.4 us
  transfers between devices with their start and end apart: 32, of which 15 were waited for; matrix products, arithmetic and copies ran while one was open for 10% of the time, Pallas kernels for 13%

profile of v2, /device:TPU:7, one launch (start us, length us, event | category | flops | bytes accessed | tf_op | source)
XLA Modules:
  0.0 308.1 jit_solution(11144993630652528764)
XLA Ops:
  12.5 5.4 %masked_columns.1 = (bf16[1024,1024]{1,0:T(8,128)(2,1)S(1)}, bf16[1024,1024]{1,0:T(8,128)(2,1)S(1)}, bf16[1024,1024]{1,0:T(8,128)(2,1)S(1)}, bf16[1024,1024]{1,0:T(8,128)(2,1)S(1)}) custom-call(s32[16]{0:T(128)S(1)} %get-tuple-element.94.cols, f32[8,4096]{1,0:T(8,128)S(1)} %convert_element_type.29.refs_0_.refs_1_.refs_2_.refs_3_, ...), custom_call_target="tpu_custom_call" | custom-call | tf_op jit(solution)/shard_map/masked_columns/pallas_call | solution.py:100
  26.2 2.4 collective-permute-done.7
  28.7 5.3 %collective-permute-done.8 = bf16[128,1024]{1,0:T(8,128)(2,1)S(1)} collective-permute-done((bf16[128,1024]{1,0:T(8,128)(2,1)S(1)}, bf16[128,1024]{1,0:T(8,128)(2,1)S(1)}, u32[]{:S(2)}, u32[]{:S(2)}) %collective-permute-start.8) | collective-permute-done | bytes 262176 | tf_op jit(solution)/shard_map/ppermute | solution.py:25
  34.2 5.3 %collective-permute-start.10 = (bf16[4,256,1024]{2,1,0:T(8,128)(2,1)S(1)}, bf16[4,256,1024]{2,1,0:T(8,128)(2,1)S(1)}, u32[]{:S(2)}, u32[]{:S(2)}) collective-permute-start(bf16[4,256,1024]{2,1,0:T(8,128)(2,1)S(1)} %bitcast.31), channel_id=1, source_target_pairs={{0,1},{1,0},{2,3},{3,2},{4,5},{5,4},{6,7},{7,6},{8,9},{9,8},{10,11... | collective-permute-start | bytes 6291464 | tf_op jit(solution)/shard_map/ppermute | solution.py:25
  39.7 4.3 %fusion.12 = f32[1024,1024]{1,0:T(8,128)} fusion(bf16[1024,1024]{1,0:T(8,128)(2,1)S(1)} %get-tuple-element.58, bf16[1024,1024]{1,0:T(8,128)(2,1)S(1)} %constant_dynamic-update-slice_fusion), kind=kOutput, calls=%fused_computation.50 | convolution fusion | flops 2147483648 | bytes 8388608 | tf_op jit(solution)/shard_map/dot_general | solution.py:351
  44.2 3.4 %collective-permute-done.11 = bf16[128,1024]{1,0:T(8,128)(2,1)S(1)} collective-permute-done((bf16[128,1024]{1,0:T(8,128)(2,1)S(1)}, bf16[128,1024]{1,0:T(8,128)(2,1)S(1)}, u32[]{:S(2)}, u32[]{:S(2)}) %collective-permute-start.11) | collective-permute-done | bytes 262176 | tf_op jit(solution)/shard_map/ppermute | solution.py:25
  51.0 4.7 %fusion.13 = f32[1024,1024]{1,0:T(8,128)S(1)} fusion(bf16[1024,1024]{1,0:T(8,128)(2,1)} %copy-done.16, bf16[1024,1024]{1,0:T(8,128)(2,1)} %bitcast.34), kind=kOutput, calls=%fused_computation.51 | convolution fusion | flops 2147483648 | bytes 8388608 | tf_op jit(solution)/shard_map/dot_general | solution.py:351
  57.3 2.3 fusion.14
  59.6 5.3 %add_convert_fusion = bf16[1024,1024]{1,0:T(8,128)(2,1)} fusion(f32[1024,1024]{1,0:T(8,128)S(1)} %add.71, f32[1024,1024]{1,0:T(8,128)S(1)} %fusion.14, bf16[1024,1024]{1,0:T(8,128)(2,1)S(1)} %copy-done.13, bf16[1024,1024]{1,0:T(8,128)(2,1)} %bitcast.5), kind=kOutput, calls=%fused_computation | convolution fusion | flops 2150629376 | bytes 14680064 | tf_op jit(solution)/shard_map/dot_general | solution.py:351
  68.4 45.3 %collective-permute-done.17.refs_2_ = bf16[4,256,1024]{2,1,0:T(8,128)(2,1)S(1)} collective-permute-done((bf16[4,256,1024]{2,1,0:T(8,128)(2,1)}, bf16[4,256,1024]{2,1,0:T(8,128)(2,1)S(1)}, u32[]{:S(2)}, u32[]{:S(2)}) %collective-permute-start.17) | collective-permute-done | bytes 2097184 | tf_op jit(solution)/shard_map/ppermute | solution.py:25
  115.3 2.3 collective-permute-start.16
  123.7 7.1 %margin_env.1 = bf16[256,1024]{1,0:T(8,128)(2,1)S(1)} custom-call(s32[16]{0:T(128)S(1)} %get-tuple-element.93.cols, bf16[8,256,512]{2,1,0:T(8,128)(2,1)S(1)} %bitcast.35, bf16[8,256,512]{2,1,0:T(8,128)(2,1)S(1)} %bitcast.36, f32[1,1024]{1,0:T(1,128)S(1)} %bitcast.39, bf16[4,256,1024]{2,1,0:T(8,128)(2,1)S(1)} %bitcast.32, ...), custom_call_target="tpu_custom_call" | custom-call | flops 2147483648 | bytes 10485760 | tf_op jit(solution)/shard_map/margin_env/pallas_call | solution.py:153
  130.8 8.2 %collective-permute-done.18 = bf16[2,256,1024]{2,1,0:T(8,128)(2,1)} collective-permute-done((bf16[2,256,1024]{2,1,0:T(8,128)(2,1)S(1)}, bf16[2,256,1024]{2,1,0:T(8,128)(2,1)}, u32[]{:S(2)}, u32[]{:S(2)}) %collective-permute-start.18) | collective-permute-done | bytes 1048608 | tf_op jit(solution)/shard_map/ppermute | solution.py:25
  140.3 2.8 collective-permute-start.22
  143.1 3.1 pad_maximum_fusion.1.refs_4_
  146.2 16.4 %collective-permute-done.20 = bf16[2,256,1024]{2,1,0:T(8,128)(2,1)S(1)} collective-permute-done((bf16[2,256,1024]{2,1,0:T(8,128)(2,1)}, bf16[2,256,1024]{2,1,0:T(8,128)(2,1)S(1)}, u32[]{:S(2)}, u32[]{:S(2)}) %collective-permute-start.20) | collective-permute-done | bytes 1048608 | tf_op jit(solution)/shard_map/ppermute | solution.py:25
  162.8 16.5 %exchange_tiles.3 = bf16[8,2,32,1280]{3,2,1,0:T(8,128)(2,1)S(1)} custom-call(s32[1]{0:T(128)} %bitcast.core_ref, bf16[4,256,1024]{2,1,0:T(8,128)(2,1)} %bitcast.6.mine_ref.refs_0_, bf16[4,256,1024]{2,1,0:T(8,128)(2,1)S(1)} %copy-done.18, bf16[4,256,1024]{2,1,0:T(8,128)(2,1)} %bitcast.6.mine_ref.refs_0_, bf16[4,256,1024]{2,1,0:T(8,128)(2,1)} %copy-done.24, ...), custom_call_target="tpu_custom_call" | custom-call | flops 5368709120 | bytes 15990784 | tf_op jit(solution)/shard_map/exchange_tiles/pallas_call | solution.py:230
  180.5 10.8 %all-to-all-start = ((bf16[16,32,1280]{2,1,0:T(8,128)(2,1)}), bf16[16,32,1280]{2,1,0:T(8,128)(2,1)S(1)}, u32[]{:S(2)}, u32[]{:S(2)}) async-start(bf16[16,32,1280]{2,1,0:T(8,128)(2,1)} %bitcast.37), calls=%async_computation | async-start | bytes 2621440 | tf_op jit(solution)/shard_map/all_to_all | solution.py:252
  191.3 6.0 %collective-permute-start.24 = (bf16[256,1024]{1,0:T(8,128)(2,1)}, bf16[256,1024]{1,0:T(8,128)(2,1)}, u32[]{:S(2)}, u32[]{:S(2)}) collective-permute-start(bf16[256,1024]{1,0:T(8,128)(2,1)} %copy-done.9), channel_id=1, source_target_pairs={{0,0},{1,1},{2,16},{3,17},{4,32},{5,33},{6,48},{7,49},{8,64},{9,65... | collective-permute-start | bytes 1572872 | tf_op jit(solution)/shard_map/ppermute | solution.py:25
  197.2 3.2 %pad_maximum_fusion.refs_0_ = bf16[4,256,1024]{2,1,0:T(8,128)(2,1)} fusion(bf16[2,256,1024]{2,1,0:T(8,128)(2,1)} %collective-permute-done.21, bf16[2,256,1024]{2,1,0:T(8,128)(2,1)} %copy-done.22), kind=kLoop, calls=%fused_computation.1 | loop fusion | flops 1048576 | bytes 4194304 | tf_op jit(solution)/shard_map/concatenate | solution.py:389
  200.4 9.9 %exchange_tiles.2 = bf16[8,2,32,768]{3,2,1,0:T(8,128)(2,1)S(1)} custom-call(s32[1]{0:T(128)} %bitcast.core_ref, bf16[4,256,1024]{2,1,0:T(8,128)(2,1)} %bitcast.6.mine_ref.refs_0_, bf16[4,256,1024]{2,1,0:T(8,128)(2,1)S(1)} %copy-done.19, bf16[4,256,1024]{2,1,0:T(8,128)(2,1)} %pad_maximum_fusion.refs_0_, ...), custom_call_target="tpu_custom_call" | custom-call | flops 3221225472 | bytes 11272192 | tf_op jit(solution)/shard_map/exchange_tiles/pallas_call | solution.py:230
  214.4 2.6 early_rows.1
  217.8 16.3 %collective-permute-done.24 = bf16[256,1024]{1,0:T(8,128)(2,1)} collective-permute-done((bf16[256,1024]{1,0:T(8,128)(2,1)}, bf16[256,1024]{1,0:T(8,128)(2,1)}, u32[]{:S(2)}, u32[]{:S(2)}) %collective-permute-start.24) | collective-permute-done | bytes 524320 | tf_op jit(solution)/shard_map/ppermute | solution.py:25
  234.1 7.9 %all-to-all-start.1 = ((bf16[16,32,768]{2,1,0:T(8,128)(2,1)}), bf16[16,32,768]{2,1,0:T(8,128)(2,1)S(1)}, u32[]{:S(2)}, u32[]{:S(2)}) async-start(bf16[16,32,768]{2,1,0:T(8,128)(2,1)} %bitcast.38), calls=%async_computation.1 | async-start | bytes 1572864 | tf_op jit(solution)/shard_map/all_to_all | solution.py:252
  242.2 12.4 %all-to-all-done.1.got = bf16[16,32,768]{2,1,0:T(8,128)(2,1)S(1)} async-done(((bf16[16,32,768]{2,1,0:T(8,128)(2,1)}), bf16[16,32,768]{2,1,0:T(8,128)(2,1)S(1)}, u32[]{:S(2)}, u32[]{:S(2)}) %all-to-all-start.1) | async-done | bytes 786464 | tf_op jit(solution)/shard_map/all_to_all | solution.py:252
  255.5 3.3 %late_rows.1 = bf16[8,32,2048]{2,1,0:T(8,128)(2,1)} custom-call(s32[9]{0:T(128)S(1)} %pad_add_fusion.1.scalars, bf16[16,32,768]{2,1,0:T(8,128)(2,1)S(1)} %all-to-all-done.1.got, f32[2,32,1280]{2,1,0:T(8,128)S(1)} %copy-done.11, f32[32,1024]{1,0:T(8,128)S(1)} %get-tuple-element.81.b_early, f32[1,1024]{1,0:T(1,128)S(1)} %bitcast.40, ...), custom_call_target="tpu_custom_call" | custom-call | flops 100663296 | bytes 8388608 | tf_op jit(solution)/shard_map/late_rows/pallas_call | solution.py:304
  258.8 5.5 %all-to-all-start.2 = ((bf16[8,32,2048]{2,1,0:T(8,128)(2,1)}), bf16[8,32,2048]{2,1,0:T(8,128)(2,1)S(1)}, u32[]{:S(2)}, u32[]{:S(2)}) async-start(bf16[8,32,2048]{2,1,0:T(8,128)(2,1)} %late_rows.1), calls=%async_computation.2 | async-start | bytes 2097152 | tf_op jit(solution)/shard_map/all_to_all | solution.py:398
  265.5 12.7 %all-to-all-done.2 = bf16[8,32,2048]{2,1,0:T(8,128)(2,1)S(1)} async-done(((bf16[8,32,2048]{2,1,0:T(8,128)(2,1)}), bf16[8,32,2048]{2,1,0:T(8,128)(2,1)S(1)}, u32[]{:S(2)}, u32[]{:S(2)}) %all-to-all-start.2) | async-done | bytes 1048608 | tf_op jit(solution)/shard_map/all_to_all | solution.py:398
  279.6 6.9 %collective-permute-start.25 = (bf16[256,256]{0,1:T(8,128)(2,1)S(1)}, bf16[256,256]{0,1:T(8,128)(2,1)S(1)}, u32[]{:S(2)}, u32[]{:S(2)}) collective-permute-start(bf16[256,256]{0,1:T(8,128)(2,1)S(1)} %get-tuple-element.98), channel_id=1, source_target_pairs={{0,0},{1,1},{2,16},{3,17},{4,32},{5,33},{6,48},{7,49},{8,64},{9,65... | collective-permute-start | bytes 393224 | tf_op jit(solution)/shard_map/ppermute | solution.py:25
  286.9 3.2 %collective-permute-start.27 = (bf16[256,256]{0,1:T(8,128)(2,1)S(1)}, bf16[256,256]{0,1:T(8,128)(2,1)S(1)}, u32[]{:S(2)}, u32[]{:S(2)}) collective-permute-start(bf16[256,256]{0,1:T(8,128)(2,1)S(1)} %get-tuple-element.100), channel_id=1, source_target_pairs={{0,1},{1,0},{2,17},{3,16},{4,33},{5,32},{6,49},{7,48},{8,65},{9,64... | collective-permute-start | bytes 393224 | tf_op jit(solution)/shard_map/ppermute | solution.py:25
  290.3 4.0 %collective-permute-done.25 = bf16[256,256]{0,1:T(8,128)(2,1)S(1)} collective-permute-done((bf16[256,256]{0,1:T(8,128)(2,1)S(1)}, bf16[256,256]{0,1:T(8,128)(2,1)S(1)}, u32[]{:S(2)}, u32[]{:S(2)}) %collective-permute-start.25) | collective-permute-done | bytes 131104 | tf_op jit(solution)/shard_map/ppermute | solution.py:25
  294.3 6.1 %collective-permute-done.27 = bf16[256,256]{0,1:T(8,128)(2,1)S(1)} collective-permute-done((bf16[256,256]{0,1:T(8,128)(2,1)S(1)}, bf16[256,256]{0,1:T(8,128)(2,1)S(1)}, u32[]{:S(2)}, u32[]{:S(2)}) %collective-permute-start.27) | collective-permute-done | bytes 131104 | tf_op jit(solution)/shard_map/ppermute | solution.py:25
  (134 shorter events, 43.7 us)
Async XLA Ops:
  6.5 112.4 %all-gather.3.cloned.1.call-start = ((), (), s32[]{:S(2)}) async-start(), calls=%async_computation.3 | async-start | bytes 2359296 | tf_op jit(solution)/shard_map/all_gather | solution.py:341
  6.5 14.3 %collective-permute-start.1 = (bf16[256,1024]{1,0:T(8,128)(2,1)}, bf16[256,1024]{1,0:T(8,128)(2,1)S(1)}, u32[]{:S(2)}, u32[]{:S(2)}) collective-permute-start(bf16[256,1024]{1,0:T(8,128)(2,1)} %param.8), channel_id=1, source_target_pairs={{0,2},{1,3},{2,4},{3,5},{4,6},{5,7},{6,0},{7,1},{8,10},{9,11},{10,... | collective-permute-start | bytes 1572872 | tf_op jit(solution)/shard_map/ppermute | solution.py:25
  7.8 13.1 %collective-permute-start = (bf16[256,1024]{1,0:T(8,128)(2,1)}, bf16[256,1024]{1,0:T(8,128)(2,1)S(1)}, u32[]{:S(2)}, u32[]{:S(2)}) collective-permute-start(bf16[256,1024]{1,0:T(8,128)(2,1)} %param.8), channel_id=1, source_target_pairs={{0,6},{1,7},{2,0},{3,1},{4,2},{5,3},{6,4},{7,5},{8,14},{9,15},{10,... | collective-permute-start | bytes 1572872 | tf_op jit(solution)/shard_map/ppermute | solution.py:25
  10.3 8.9 %collective-permute-start.3 = (bf16[128,1024]{1,0:T(8,128)(2,1)S(1)}, bf16[128,1024]{1,0:T(8,128)(2,1)S(1)}, u32[]{:S(2)}, u32[]{:S(2)}) collective-permute-start(bf16[128,1024]{1,0:T(8,128)(2,1)S(1)} %get-tuple-element.91), channel_id=1, source_target_pairs={{0,24},{1,25},{2,26},{3,27},{4,28},{5,29},{6,30},{7,31},{8,16},{9,... | collective-permute-start | bytes 786440 | tf_op jit(solution)/shard_map/ppermute | solution.py:25
  10.6 8.6 %collective-permute-start.2 = (bf16[128,1024]{1,0:T(8,128)(2,1)S(1)}, bf16[128,1024]{1,0:T(8,128)(2,1)S(1)}, u32[]{:S(2)}, u32[]{:S(2)}) collective-permute-start(bf16[128,1024]{1,0:T(8,128)(2,1)S(1)} %get-tuple-element.92), channel_id=1, source_target_pairs={{0,8},{1,9},{2,10},{3,11},{4,12},{5,13},{6,14},{7,15},{8,0},{9,1},... | collective-permute-start | bytes 786440 | tf_op jit(solution)/shard_map/ppermute | solution.py:25
  20.9 7.6 %collective-permute-start.7 = (bf16[128,1024]{1,0:T(8,128)(2,1)S(1)}, bf16[128,1024]{1,0:T(8,128)(2,1)S(1)}, u32[]{:S(2)}, u32[]{:S(2)}) collective-permute-start(bf16[128,1024]{1,0:T(8,128)(2,1)S(1)} %get-tuple-element.89), channel_id=1, source_target_pairs={{0,24},{1,25},{2,26},{3,27},{4,28},{5,29},{6,30},{7,31},{8,16},{9,... | collective-permute-start | bytes 786440 | tf_op jit(solution)/shard_map/ppermute | solution.py:25
  21.3 7.4 %collective-permute-start.6 = (bf16[128,1024]{1,0:T(8,128)(2,1)S(1)}, bf16[128,1024]{1,0:T(8,128)(2,1)S(1)}, u32[]{:S(2)}, u32[]{:S(2)}) collective-permute-start(bf16[128,1024]{1,0:T(8,128)(2,1)S(1)} %get-tuple-element.90), channel_id=1, source_target_pairs={{0,8},{1,9},{2,10},{3,11},{4,12},{5,13},{6,14},{7,15},{8,0},{9,1},... | collective-permute-start | bytes 786440 | tf_op jit(solution)/shard_map/ppermute | solution.py:25
  22.1 6.6 %collective-permute-start.4 = (bf16[128,1024]{1,0:T(8,128)(2,1)S(1)}, bf16[128,1024]{1,0:T(8,128)(2,1)S(1)}, u32[]{:S(2)}, u32[]{:S(2)}) collective-permute-start(bf16[128,1024]{1,0:T(8,128)(2,1)S(1)} %get-tuple-element.90), channel_id=1, source_target_pairs={{0,6},{1,7},{2,0},{3,1},{4,2},{5,3},{6,4},{7,5},{8,14},{9,15},{10,... | collective-permute-start | bytes 786440 | tf_op jit(solution)/shard_map/ppermute | solution.py:25
  24.2 9.9 %collective-permute-start.9 = (bf16[128,1024]{1,0:T(8,128)(2,1)S(1)}, bf16[128,1024]{1,0:T(8,128)(2,1)S(1)}, u32[]{:S(2)}, u32[]{:S(2)}) collective-permute-start(bf16[128,1024]{1,0:T(8,128)(2,1)S(1)} %get-tuple-element.88), channel_id=1, source_target_pairs={{0,24},{1,25},{2,26},{3,27},{4,28},{5,29},{6,30},{7,31},{8,16},{9,... | collective-permute-start | bytes 786440 | tf_op jit(solution)/shard_map/ppermute | solution.py:25
  26.2 8.0 %collective-permute-start.5 = (bf16[128,1024]{1,0:T(8,128)(2,1)S(1)}, bf16[128,1024]{1,0:T(8,128)(2,1)S(1)}, u32[]{:S(2)}, u32[]{:S(2)}) collective-permute-start(bf16[128,1024]{1,0:T(8,128)(2,1)S(1)} %get-tuple-element.88), channel_id=1, source_target_pairs={{0,2},{1,3},{2,4},{3,5},{4,6},{5,7},{6,0},{7,1},{8,10},{9,11},{10,... | collective-permute-start | bytes 786440 | tf_op jit(solution)/shard_map/ppermute | solution.py:25
  28.5 5.5 %collective-permute-start.8 = (bf16[128,1024]{1,0:T(8,128)(2,1)S(1)}, bf16[128,1024]{1,0:T(8,128)(2,1)S(1)}, u32[]{:S(2)}, u32[]{:S(2)}) collective-permute-start(bf16[128,1024]{1,0:T(8,128)(2,1)S(1)} %get-tuple-element.87), channel_id=1, source_target_pairs={{0,8},{1,9},{2,10},{3,11},{4,12},{5,13},{6,14},{7,15},{8,0},{9,1},... | collective-permute-start | bytes 786440 | tf_op jit(solution)/shard_map/ppermute | solution.py:25
  34.2 14.6 %collective-permute-start.10 = (bf16[4,256,1024]{2,1,0:T(8,128)(2,1)S(1)}, bf16[4,256,1024]{2,1,0:T(8,128)(2,1)S(1)}, u32[]{:S(2)}, u32[]{:S(2)}) collective-permute-start(bf16[4,256,1024]{2,1,0:T(8,128)(2,1)S(1)} %bitcast.31), channel_id=1, source_target_pairs={{0,1},{1,0},{2,3},{3,2},{4,5},{5,4},{6,7},{7,6},{8,9},{9,8},{10,11... | collective-permute-start | bytes 6291464 | tf_op jit(solution)/shard_map/ppermute | solution.py:25
  39.5 8.0 %collective-permute-start.11 = (bf16[128,1024]{1,0:T(8,128)(2,1)S(1)}, bf16[128,1024]{1,0:T(8,128)(2,1)S(1)}, u32[]{:S(2)}, u32[]{:S(2)}) collective-permute-start(bf16[128,1024]{1,0:T(8,128)(2,1)S(1)} %collective-permute-done.4), channel_id=1, source_target_pairs={{0,8},{1,9},{2,10},{3,11},{4,12},{5,13},{6,14},{7,15},{8,0},{9,1},... | collective-permute-start | bytes 786440 | tf_op jit(solution)/shard_map/ppermute | solution.py:25
  39.6 9.2 %collective-permute-start.12 = (bf16[128,1024]{1,0:T(8,128)(2,1)S(1)}, bf16[128,1024]{1,0:T(8,128)(2,1)S(1)}, u32[]{:S(2)}, u32[]{:S(2)}) collective-permute-start(bf16[128,1024]{1,0:T(8,128)(2,1)S(1)} %collective-permute-done.5), channel_id=1, source_target_pairs={{0,24},{1,25},{2,26},{3,27},{4,28},{5,29},{6,30},{7,31},{8,16},{9,... | collective-permute-start | bytes 786440 | tf_op jit(solution)/shard_map/ppermute | solution.py:25
  50.1 9.5 %collective-permute-start.13 = (bf16[4,256,1024]{2,1,0:T(8,128)(2,1)S(1)}, bf16[4,256,1024]{2,1,0:T(8,128)(2,1)}, u32[]{:S(2)}, u32[]{:S(2)}) collective-permute-start(bf16[4,256,1024]{2,1,0:T(8,128)(2,1)S(1)} %bitcast.27), channel_id=1, source_target_pairs={{0,1},{1,0},{2,3},{3,2},{4,5},{5,4},{6,7},{7,6},{8,9},{9,8},{10,11... | collective-permute-start | bytes 6291464 | tf_op jit(solution)/shard_map/ppermute | solution.py:25
  65.0 48.7 %collective-permute-start.17 = (bf16[4,256,1024]{2,1,0:T(8,128)(2,1)}, bf16[4,256,1024]{2,1,0:T(8,128)(2,1)S(1)}, u32[]{:S(2)}, u32[]{:S(2)}) collective-permute-start(bf16[4,256,1024]{2,1,0:T(8,128)(2,1)} %bitcast.6.mine_ref.refs_0_), channel_id=1, source_target_pairs={{0,2},{1,3},{2,4},{3,5},{4,6},{5,7},{6,0},{7,1},{8,10},{9,11},{10,... | collective-permute-start | bytes 6291464 | tf_op jit(solution)/shard_map/ppermute | solution.py:25
  66.3 47.7 %collective-permute-start.15 = (bf16[4,256,1024]{2,1,0:T(8,128)(2,1)}, bf16[4,256,1024]{2,1,0:T(8,128)(2,1)S(1)}, u32[]{:S(2)}, u32[]{:S(2)}) collective-permute-start(bf16[4,256,1024]{2,1,0:T(8,128)(2,1)} %bitcast.6.mine_ref.refs_0_), channel_id=1, source_target_pairs={{0,6},{1,7},{2,0},{3,1},{4,2},{5,3},{6,4},{7,5},{8,14},{9,15},{10,... | collective-permute-start | bytes 6291464 | tf_op jit(solution)/shard_map/ppermute | solution.py:25
  67.7 50.0 %collective-permute-start.14 = (bf16[4,256,1024]{2,1,0:T(8,128)(2,1)}, bf16[4,256,1024]{2,1,0:T(8,128)(2,1)S(1)}, u32[]{:S(2)}, u32[]{:S(2)}) collective-permute-start(bf16[4,256,1024]{2,1,0:T(8,128)(2,1)} %bitcast.6.mine_ref.refs_0_), channel_id=1, source_target_pairs={{0,1},{1,0},{2,3},{3,2},{4,5},{5,4},{6,7},{7,6},{8,9},{9,8},{10,11... | collective-permute-start | bytes 6291464 | tf_op jit(solution)/shard_map/ppermute | solution.py:25
  68.2 62.6 %collective-permute-start.19 = (bf16[4,256,1024]{2,1,0:T(8,128)(2,1)}, bf16[4,256,1024]{2,1,0:T(8,128)(2,1)}, u32[]{:S(2)}, u32[]{:S(2)}) collective-permute-start(bf16[4,256,1024]{2,1,0:T(8,128)(2,1)} %bitcast.6.mine_ref.refs_0_), channel_id=1, source_target_pairs={{0,8},{1,9},{2,10},{3,11},{4,12},{5,13},{6,14},{7,15},{8,0},{9,1},... | collective-permute-start | bytes 6291464 | tf_op jit(solution)/shard_map/ppermute | solution.py:25
  113.7 25.3 %collective-permute-start.18 = (bf16[2,256,1024]{2,1,0:T(8,128)(2,1)S(1)}, bf16[2,256,1024]{2,1,0:T(8,128)(2,1)}, u32[]{:S(2)}, u32[]{:S(2)}) collective-permute-start(bf16[2,256,1024]{2,1,0:T(8,128)(2,1)S(1)} %slice.55), channel_id=1, source_target_pairs={{0,2},{1,3},{2,4},{3,5},{4,6},{5,7},{6,0},{7,1},{8,10},{9,11},{10,... | collective-permute-start | bytes 3145736 | tf_op jit(solution)/shard_map/ppermute | solution.py:25
  115.3 24.1 %collective-permute-start.16 = (bf16[2,256,1024]{2,1,0:T(8,128)(2,1)}, bf16[2,256,1024]{2,1,0:T(8,128)(2,1)}, u32[]{:S(2)}, u32[]{:S(2)}) collective-permute-start(bf16[2,256,1024]{2,1,0:T(8,128)(2,1)} %slice.54), channel_id=1, source_target_pairs={{0,6},{1,7},{2,0},{3,1},{4,2},{5,3},{6,4},{7,5},{8,14},{9,15},{10,... | collective-permute-start | bytes 3145736 | tf_op jit(solution)/shard_map/ppermute | solution.py:25
  139.4 23.1 %collective-permute-start.20 = (bf16[2,256,1024]{2,1,0:T(8,128)(2,1)}, bf16[2,256,1024]{2,1,0:T(8,128)(2,1)S(1)}, u32[]{:S(2)}, u32[]{:S(2)}) collective-permute-start(bf16[2,256,1024]{2,1,0:T(8,128)(2,1)} %collective-permute-done.16), channel_id=1, source_target_pairs={{0,8},{1,9},{2,10},{3,11},{4,12},{5,13},{6,14},{7,15},{8,0},{9,1},... | collective-permute-start | bytes 3145736 | tf_op jit(solution)/shard_map/ppermute | solution.py:25
  139.7 51.5 %collective-permute-start.23 = (bf16[4,256,1024]{2,1,0:T(8,128)(2,1)}, bf16[4,256,1024]{2,1,0:T(8,128)(2,1)}, u32[]{:S(2)}, u32[]{:S(2)}) collective-permute-start(bf16[4,256,1024]{2,1,0:T(8,128)(2,1)} %collective-permute-done.19.refs_3_), channel_id=1, source_target_pairs={{0,2},{1,3},{2,4},{3,5},{4,6},{5,7},{6,0},{7,1},{8,10},{9,11},{10,... | collective-permute-start | bytes 6291464 | tf_op jit(solution)/shard_map/ppermute | solution.py:25
  140.3 50.9 %collective-permute-start.22 = (bf16[4,256,1024]{2,1,0:T(8,128)(2,1)}, bf16[4,256,1024]{2,1,0:T(8,128)(2,1)}, u32[]{:S(2)}, u32[]{:S(2)}) collective-permute-start(bf16[4,256,1024]{2,1,0:T(8,128)(2,1)} %collective-permute-done.19.refs_3_), channel_id=1, source_target_pairs={{0,6},{1,7},{2,0},{3,1},{4,2},{5,3},{6,4},{7,5},{8,14},{9,15},{10,... | collective-permute-start | bytes 6291464 | tf_op jit(solution)/shard_map/ppermute | solution.py:25
  162.6 34.7 %collective-permute-start.21 = (bf16[2,256,1024]{2,1,0:T(8,128)(2,1)}, bf16[2,256,1024]{2,1,0:T(8,128)(2,1)}, u32[]{:S(2)}, u32[]{:S(2)}) collective-permute-start(bf16[2,256,1024]{2,1,0:T(8,128)(2,1)} %collective-permute-done.18), channel_id=1, source_target_pairs={{0,8},{1,9},{2,10},{3,11},{4,12},{5,13},{6,14},{7,15},{8,0},{9,1},... | collective-permute-start | bytes 3145736 | tf_op jit(solution)/shard_map/ppermute | solution.py:25
  180.5 30.8 %all-to-all-start = ((bf16[16,32,1280]{2,1,0:T(8,128)(2,1)}), bf16[16,32,1280]{2,1,0:T(8,128)(2,1)S(1)}, u32[]{:S(2)}, u32[]{:S(2)}) async-start(bf16[16,32,1280]{2,1,0:T(8,128)(2,1)} %bitcast.37), calls=%async_computation | async-start | bytes 2621440 | tf_op jit(solution)/shard_map/all_to_all | solution.py:252
  191.3 42.8 %collective-permute-start.24 = (bf16[256,1024]{1,0:T(8,128)(2,1)}, bf16[256,1024]{1,0:T(8,128)(2,1)}, u32[]{:S(2)}, u32[]{:S(2)}) collective-permute-start(bf16[256,1024]{1,0:T(8,128)(2,1)} %copy-done.9), channel_id=1, source_target_pairs={{0,0},{1,1},{2,16},{3,17},{4,32},{5,33},{6,48},{7,49},{8,64},{9,65... | collective-permute-start | bytes 1572872 | tf_op jit(solution)/shard_map/ppermute | solution.py:25
  234.1 20.5 %all-to-all-start.1 = ((bf16[16,32,768]{2,1,0:T(8,128)(2,1)}), bf16[16,32,768]{2,1,0:T(8,128)(2,1)S(1)}, u32[]{:S(2)}, u32[]{:S(2)}) async-start(bf16[16,32,768]{2,1,0:T(8,128)(2,1)} %bitcast.38), calls=%async_computation.1 | async-start | bytes 1572864 | tf_op jit(solution)/shard_map/all_to_all | solution.py:252
  258.8 19.4 %all-to-all-start.2 = ((bf16[8,32,2048]{2,1,0:T(8,128)(2,1)}), bf16[8,32,2048]{2,1,0:T(8,128)(2,1)S(1)}, u32[]{:S(2)}, u32[]{:S(2)}) async-start(bf16[8,32,2048]{2,1,0:T(8,128)(2,1)} %late_rows.1), calls=%async_computation.2 | async-start | bytes 2097152 | tf_op jit(solution)/shard_map/all_to_all | solution.py:398
  264.3 22.3 %collective-permute-start.26 = (bf16[256,1024]{1,0:T(8,128)(2,1)}, bf16[256,1024]{1,0:T(8,128)(2,1)S(1)}, u32[]{:S(2)}, u32[]{:S(2)}) collective-permute-start(bf16[256,1024]{1,0:T(8,128)(2,1)} %collective-permute-done.24), channel_id=1, source_target_pairs={{0,1},{1,0},{2,3},{3,2},{4,5},{5,4},{6,7},{7,6},{8,9},{9,8},{10,11... | collective-permute-start | bytes 1572872 | tf_op jit(solution)/shard_map/ppermute | solution.py:25
  279.6 14.7 %collective-permute-start.25 = (bf16[256,256]{0,1:T(8,128)(2,1)S(1)}, bf16[256,256]{0,1:T(8,128)(2,1)S(1)}, u32[]{:S(2)}, u32[]{:S(2)}) collective-permute-start(bf16[256,256]{0,1:T(8,128)(2,1)S(1)} %get-tuple-element.98), channel_id=1, source_target_pairs={{0,0},{1,1},{2,16},{3,17},{4,32},{5,33},{6,48},{7,49},{8,64},{9,65... | collective-permute-start | bytes 393224 | tf_op jit(solution)/shard_map/ppermute | solution.py:25
  286.9 13.4 %collective-permute-start.27 = (bf16[256,256]{0,1:T(8,128)(2,1)S(1)}, bf16[256,256]{0,1:T(8,128)(2,1)S(1)}, u32[]{:S(2)}, u32[]{:S(2)}) collective-permute-start(bf16[256,256]{0,1:T(8,128)(2,1)S(1)} %get-tuple-element.100), channel_id=1, source_target_pairs={{0,1},{1,0},{2,17},{3,16},{4,33},{5,32},{6,49},{7,48},{8,65},{9,64... | collective-permute-start | bytes 393224 | tf_op jit(solution)/shard_map/ppermute | solution.py:25
  (27 other events, 199.4 us)
Sparse Core Ops, SparseCore 0:
  51.1 65.2 all-gather.2

commit v3 on v2

v3 whole, which is shorter than its diff:
```python
import jax
import jax.numpy as jnp
from jax import lax
from jax.experimental import pallas as pl
from jax.experimental.pallas import tpu as pltpu
from jax.sharding import Mesh, PartitionSpec as P

ATILE = 32
AXES = ("grp", "chip", "core")
NZ, NH, NA, NY, NK = 4, 2, 2, 4, 2


def device(z, h, a, y, k):
    return ((z * NH + h) * NA + a) * NY * NK + y * NK + k


def moved(x, where):
    pairs = []
    for z in range(NZ):
        for h in range(NH):
            for a in range(NA):
                for y in range(NY):
                    for k in range(NK):
                        pairs.append((device(z, h, a, y, k), device(*where(z, h, a, y, k))))
    return lax.ppermute(x, AXES, pairs)


def from_next(x):
    return moved(x, lambda z, h, a, y, k: (z, h, a, (y - 1) % NY, k))


def from_prev(x):
    return moved(x, lambda z, h, a, y, k: (z, h, a, (y + 1) % NY, k))


def across_in(x):
    return moved(x, lambda z, h, a, y, k: (z, h, 1 - a, y, k))


def across_out(x):
    return moved(x, lambda z, h, a, y, k: (z, 1 - h, 1 - a, y, k))


def other_core(x):
    return moved(x, lambda z, h, a, y, k: (z, h, a, y, 1 - k))


def mirror(z, h, a, y, k):
    chip, group = a * NY + y, z * NH + h
    return (chip // NH, chip % NH, group // NY, group % NY, k)


def mirrored(x):
    return moved(x, mirror)


def mirrored_cross(x):
    def where(z, h, a, y, k):
        return mirror(z, h, a, y, 1 - k)

    return moved(x, where)


def to_absolute(rel, a, y):
    twice = jnp.concatenate([rel, rel], axis=1)
    turned = lax.dynamic_slice_in_dim(twice, (NY - y) % NY, NY, 1)
    return jnp.where(a == 0, turned, turned[::-1])


def after(x, *earlier):
    return lax.optimization_barrier((x,) + earlier)[0]


def masked_block(keep_ref, slab_ref):
    rows = slab_ref.shape[1]
    keep = keep_ref[...]
    wide = jnp.broadcast_to(keep[:, None, :], (keep.shape[0], ATILE, keep.shape[1]))
    wide = wide.reshape(rows, keep.shape[1]).astype(jnp.bfloat16)
    both = slab_ref[...] * wide[None]
    return both.reshape(slab_ref.shape[0] * rows, keep.shape[1])


def mask_kernel(cols, *refs):
    count = len(refs) // 3
    for at in range(count):
        refs[2 * count + at][...] = masked_block(refs[at], refs[count + at])


def masked_columns(cols, keep, slab, depth, steps):
    aux_dev, rows, nao = slab.shape
    count = nao // (depth * steps)
    keep_spec = [
        pl.BlockSpec((keep.shape[0], depth), lambda s, c, t=t: (0, c[t * steps + s]))
        for t in range(count)
    ]
    slab_spec = [
        pl.BlockSpec((aux_dev, rows, depth), lambda s, c, t=t: (0, 0, c[t * steps + s]))
        for t in range(count)
    ]
    return pl.pallas_call(
        mask_kernel,
        out_shape=[jax.ShapeDtypeStruct((aux_dev * rows, depth * steps), slab.dtype)] * count,
        grid_spec=pltpu.PrefetchScalarGridSpec(
            num_scalar_prefetch=1,
            grid=(steps,),
            in_specs=keep_spec + slab_spec,
            out_specs=[pl.BlockSpec((aux_dev * rows, depth), lambda s, c: (0, s))] * count,
        ),
        compiler_params=pltpu.CompilerParams(vmem_limit_bytes=40 << 20),
        name="masked_columns",
    )(cols, *[keep] * count, *[slab] * count)


def tiles_kernel(core_ref, *refs):
    pieces, out_ref = refs[:-1], refs[-1]
    rows = pieces[0].shape[1]
    contract = (((1,), (1,)), ((), ()))
    packs = []
    open_pack = []
    for piece in pieces:
        open_pack += [piece[at] for at in range(piece.shape[0])]
        if len(open_pack) == pieces[0].shape[0]:
            packs.append(jnp.concatenate(open_pack, axis=1))
            open_pack = []
    left = jnp.concatenate(packs[:2], axis=0)
    core = core_ref[0]
    for at, right in enumerate(packs[2:]):
        tile = lax.dot_general(left, right, contract, preferred_element_type=jnp.float32)
        tile = tile.astype(out_ref.dtype)
        cut = (out_ref.shape[0], out_ref.shape[2], rows)
        cols = slice(at * rows, (at + 1) * rows)
        out_ref[:, core, :, cols] = tile[:rows].reshape(cut)
        out_ref[:, 1 - core, :, cols] = tile[rows:].reshape(cut)


def pair_tiles(core, *pieces):
    depth, rows, occ = pieces[0].shape
    cols = rows * (sum(p.shape[0] for p in pieces) // depth - 2)
    specs = [pl.BlockSpec(p.shape, lambda s, c: (0, 0, 0)) for p in pieces]
    out = jax.ShapeDtypeStruct((8, 2, rows // 8, cols), jnp.bfloat16)
    return pl.pallas_call(
        tiles_kernel,
        out_shape=out,
        grid_spec=pltpu.PrefetchScalarGridSpec(
            num_scalar_prefetch=1,
            grid=(1,),
            in_specs=specs,
            out_specs=pl.BlockSpec(out.shape, lambda s, c: (0, 0, 0, 0)),
        ),
        compiler_params=pltpu.CompilerParams(vmem_limit_bytes=56 << 20),
        cost_estimate=pl.CostEstimate(
            flops=4 * rows * cols * depth * occ,
            transcendentals=0,
            bytes_accessed=2 * depth * occ * (2 * rows + cols) + 4 * rows * cols,
        ),
        name="exchange_tiles",
    )(core.reshape(1), *pieces)


def exchanged(cut):
    rows, cols = cut.shape[2:]
    return lax.all_to_all(cut.reshape(16, rows, cols), ("grp", "core"), 0, 0)


def sum_groups(got_ref, first):
    total = got_ref[first].astype(jnp.float32)
    for at in range(1, got_ref.shape[0] // 2):
        total += got_ref[2 * at + first].astype(jnp.float32)
    return total


def rows_times(rows, first, block):
    depth = block.shape[0]
    left = rows[:, first * depth : (first + 1) * depth].astype(jnp.bfloat16)
    return jnp.dot(left, block, preferred_element_type=jnp.float32)


def early_kernel(core_ref, got, near, near_oth, cross, cross_oth, k_ref, b_ref):
    core = core_ref[0]
    total = jnp.zeros(b_ref.shape, jnp.float32)
    for t, (nc, cc) in enumerate(((near, cross), (near_oth, cross_oth))):
        rows = sum_groups(got, core if t == 0 else 1 - core)
        k_ref[t] = rows
        for at, block in enumerate((nc[0], nc[1], nc[2], cc[0])):
            total += rows_times(rows, at, block)
    b_ref[...] = total


def late_kernel(scalars, got, k_early, b_early, flag, cross, cross_oth, far, out_ref):
    core = scalars[0]
    occ = b_early.shape[1]
    depth = cross.shape[1]
    total = b_early[...]
    tiles = []
    for t, cc in enumerate((cross, cross_oth)):
        rows = sum_groups(got, core if t == 0 else 1 - core)
        for at, block in enumerate((far[t], cc[3], cc[1], cc[2])):
            total += rows_times(rows, at, block)
        mine = [k_early[t, :, at * depth : (at + 1) * depth] for at in range(4)]
        tiles.append(mine + [rows[:, at * depth : (at + 1) * depth] for at in range(4)])
    for t in range(2):
        first = occ + t * depth
        for at, place in enumerate((0, 1, 2, 4, 3, 7, 5, 6)):
            tile = jnp.where(core == t, tiles[0][at], tiles[1][at])
            hi = tile.astype(jnp.bfloat16)
            lo = (tile - hi.astype(jnp.float32)).astype(jnp.bfloat16)
            chip = scalars[1 + place]
            out_ref[chip, :, first : first + depth] = hi
            out_ref[chip, :, first + 2 * depth : first + 3 * depth] = lo
    b_rows = (total * flag[...]).astype(jnp.bfloat16)
    for at in range(out_ref.shape[0]):
        out_ref[at, :, :occ] = b_rows


def on_chip(body, name, out_shape, scalars, *args):
    flops = 4 * args[0].shape[1] * args[0].shape[2] * 1024
    outs = out_shape if isinstance(out_shape, list) else [out_shape]

    def whole(array):
        zeros = (0,) * len(array.shape)
        return pl.BlockSpec(array.shape, lambda s, c: zeros)

    got = pl.pallas_call(
        body,
        out_shape=outs,
        grid_spec=pltpu.PrefetchScalarGridSpec(
            num_scalar_prefetch=1,
            grid=(1,),
            in_specs=[whole(a) for a in args],
            out_specs=[whole(o) for o in outs],
        ),
        compiler_params=pltpu.CompilerParams(vmem_limit_bytes=48 << 20),
        cost_estimate=pl.CostEstimate(flops=flops, transcendentals=0, bytes_accessed=8 << 20),
        name=name,
    )(scalars, *args)
    return got if isinstance(out_shape, list) else got[0]


def early_rows(core, got, near, near_oth, cross, cross_oth):
    rows, cols = got.shape[1:]
    occ = near.shape[2]
    shapes = [
        jax.ShapeDtypeStruct((2, rows, cols), jnp.float32),
        jax.ShapeDtypeStruct((rows, occ), jnp.float32),
    ]
    args = (got, near, near_oth, cross, cross_oth)
    return on_chip(early_kernel, "early_rows", shapes, core.reshape(1), *args)


def late_rows(scalars, got, k_early, b_early, flag, cross, cross_oth, far):
    rows, occ = b_early.shape
    shape = jax.ShapeDtypeStruct((8, rows, occ + 4 * cross.shape[1]), jnp.bfloat16)
    args = (got, k_early, b_early, flag, cross, cross_oth, far)
    return on_chip(late_kernel, "late_rows", shape, scalars, *args)


def on_device(slab, block_mask, orbitals, margin, env_flag):
    aux_dev, ao_dev, nao = slab.shape
    occ = orbitals.shape[1]
    chip, core = lax.axis_index("chip"), lax.axis_index("core")
    a, y = chip // NY, chip % NY
    hb = ao_dev // 2
    flag = env_flag.astype(jnp.float32)[None, :]

    a_part = lax.dot_general(
        margin, orbitals, (((0,), (0,)), ((), ())), preferred_element_type=jnp.float32
    )
    a_low, a_high = a_part[:ao_dev], a_part[ao_dev:]
    a_send = other_core(jnp.where(core == 0, a_high, a_low).astype(jnp.bfloat16))
    a_part = jnp.where(core == 0, a_low, a_high) + a_send.astype(jnp.float32)
    a_part = a_part.astype(jnp.bfloat16).reshape(8, 32, occ)
    order = (y + jnp.array([0, 1, NY - 1, 2], jnp.int32)) % NY
    near_cols = ((a * NY + order) * NK).astype(jnp.int32)
    cross_cols = (((1 - a) * NY + order) * NK).astype(jnp.int32)
    near_cols = jnp.concatenate([near_cols + core, near_cols + 1 - core])
    cross_cols = jnp.concatenate([cross_cols + core, cross_cols + 1 - core])
    keep = jnp.repeat(block_mask[0], ATILE, axis=1).astype(jnp.float32)
    masked = masked_columns(jnp.concatenate([near_cols, cross_cols]), keep, slab, ao_dev, NY)

    def product(left, right):
        return jnp.dot(left, right.reshape(-1, occ), preferred_element_type=jnp.float32)

    def cross_over(t):
        return [across_in(t[:hb]), across_out(t[hb:])]

    nxt, prv, *own_x, masked = lax.optimization_barrier(
        (from_next(orbitals), from_prev(orbitals), *cross_over(orbitals), masked)
    )
    far_lo, far_hi, a_part, *side_x = lax.optimization_barrier(
        (from_next(nxt[:hb]), from_prev(prv[hb:]), a_part, *cross_over(nxt), *cross_over(prv))
    )
    near = jnp.concatenate([orbitals, nxt, prv, far_lo, far_hi]).reshape(NY, ao_dev, occ)
    base = product(masked[0], near)
    near_oth, far_lo_x, far_hi_x, base = lax.optimization_barrier(
        (other_core(near), across_in(far_lo), across_out(far_hi), base)
    )
    cross = jnp.concatenate([*own_x, *side_x, far_lo_x, far_hi_x]).reshape(NY, ao_dev, occ)
    base += product(masked[1], near_oth)
    cross_oth, base = lax.optimization_barrier((other_core(cross), base))
    part = base + product(masked[2], cross) + product(masked[3], cross_oth)
    part = part.astype(jnp.bfloat16).reshape(aux_dev, ao_dev, occ)
    mid = aux_dev // 2

    x, n, p = across_in(part), from_next(part), from_prev(part)
    mate = other_core(part)
    a_got = lax.all_to_all(after(a_part, mate), "chip", 0, 0)
    a_slice = (a_got.astype(jnp.float32).sum(0) * flag).astype(jnp.bfloat16)
    a_slice = jnp.broadcast_to(a_slice[None], (8,) + a_slice.shape)
    a_own = lax.all_to_all(a_slice, "chip", 0, 0).reshape(ao_dev, occ)
    f, g = from_next(n[:mid]), from_prev(p[mid:])
    early = pair_tiles(core, part, mate, part, n, p, x)
    f, g, x, early, a_own = lax.optimization_barrier((f, g, x, early, a_own))
    a_oth = other_core(a_own)
    xn, xp = from_next(x), from_prev(x)
    xf, xg = across_in(f), across_in(g)
    early = exchanged(early)
    k_early, b_early = early_rows(core, early, near, near_oth, cross, cross_oth)

    late = exchanged(pair_tiles(core, part, mate, f, g, xf, xg, xn, xp))
    places = jnp.concatenate([near_cols[:4], cross_cols[:4]]) // NK
    scalars = jnp.concatenate([core.reshape(1), places]).astype(jnp.int32)
    far_c = jnp.stack([near[3], near_oth[3]])
    packed = late_rows(scalars, late, k_early, b_early, flag, cross, cross_oth, far_c)
    got = lax.all_to_all(packed, "grp", 0, 0).reshape(ao_dev, -1)
    b_all = got[:, :occ]
    k_tile = got[:, occ : occ + 512].astype(jnp.float32) + got[:, occ + 512 :].astype(jnp.float32)
    contract = (((1,), (1,)), ((), ()))
    z_own = lax.dot_general(b_all, a_own, contract, preferred_element_type=jnp.float32)
    z_oth = lax.dot_general(b_all, a_oth, contract, preferred_element_type=jnp.float32)
    t_own = mirrored(z_own.astype(jnp.bfloat16)).astype(jnp.float32).T + z_own
    t_oth = mirrored_cross(z_oth.astype(jnp.bfloat16)).astype(jnp.float32).T + z_oth
    low, high = jnp.where(core == 0, t_own, t_oth), jnp.where(core == 0, t_oth, t_own)
    return k_tile - jnp.concatenate([low, high], axis=1)


def solution(mesh):
    fine = Mesh(mesh.devices.reshape(8, NA * NY, NK), AXES)
    blk = ("chip", "core")
    placed = (P("grp", blk, None), P("grp", blk, None), P(blk, None), P(blk, "grp"), P())
    return jax.shard_map(
        on_device, mesh=fine, in_specs=placed, out_specs=P(blk, "grp"), check_vma=False
    )
```

time: 311 us -> 277 us (0.89)
  between operations: 13.9 us -> 0.46 us
  Pallas kernels: 44.8 us -> 33.5 us
  starting transfers between devices: 66.2 us -> 74.1 us
  matrix products: 18.4 us -> 13 us
  local copies, waits for them, and re-layouts: 19.4 us -> 14.1 us
  other arithmetic: 9.53 us -> 5.5 us
    ppermute x28, waiting for transfers between devices: 111 us -> 95.5 us  [moved(): return lax.ppermute(x, AXES, pairs)]
    all_to_all x0 -> x2, waiting for transfers between devices: none -> 12.3 us  [the longest x1 10.9 us: on_device(): a_own = lax.all_to_all(a_slice, 'chip', 0, 0).reshape(ao_dev, occ)]
    unnamed x65 -> x55, local copies, waits for them, and re-layouts: 16.1 us -> 4.77 us
    pallas_call x5 -> x4, Pallas kernels: 39.3 us -> 28.1 us  [the longest x2 20.5 us: pair_tiles(): pl.pallas_call(tiles_kernel, out_shape=out, grid_spec=pltpu.PrefetchScala...]
    all_to_all x0 -> x2, starting transfers between devices: none -> 8.22 us  [the longest x1 4.18 us: on_device(): a_own = lax.all_to_all(a_slice, 'chip', 0, 0).reshape(ao_dev, occ)]
    concatenate x3 -> x1, other arithmetic: 6.3 us -> 0.08 us  [on_device(): jnp.concatenate([near_cols, cross_cols])]
    dot_general x4, matrix products: 16.7 us -> 10.8 us  [product(): jnp.dot(left, right.reshape(-1, occ), preferred_element_type=jnp.float32)]
    ppermute x28, starting transfers between devices: 42.1 us -> 38.3 us  [moved(): return lax.ppermute(x, AXES, pairs)]
  transfers between devices with their start and end apart: 32 -> 33, of which waited for: 15 -> 21; matrix products, arithmetic and copies ran while one was open for 10% -> 9% of each run, Pallas kernels for 13% -> 11%
where the time goes in v3:
time: 277 us
  waiting for transfers between devices  136 us (49%)
  starting transfers between devices  74.1 us (27%)
  Pallas kernels  33.5 us (12%)
  local copies, waits for them, and re-layouts  14.1 us (5%)
  matrix products  13 us (5%)
  other arithmetic  5.5 us (2%)
    ppermute x28, waiting for transfers between devices, moved(): return lax.ppermute(x, AXES, pairs)  95.5 us
    ppermute x28, starting transfers between devices, moved(): return lax.ppermute(x, AXES, pairs)  38.3 us
    all_to_all x2, starting transfers between devices, exchanged(): return lax.all_to_all(cut.reshape(16, rows, cols), ('grp', 'core'), 0, 0)  22 us
    pallas_call x2, Pallas kernels, pair_tiles(): pl.pallas_call(tiles_kernel, out_shape=out, grid_spec=pltpu.PrefetchScala...  20.5 us
    all_to_all x2, waiting for transfers between devices, exchanged(): return lax.all_to_all(cut.reshape(16, rows, cols), ('grp', 'core'), 0, 0)  15.3 us
    all_to_all x1, waiting for transfers between devices, on_device(): got = lax.all_to_all(packed, 'grp', 0, 0).reshape(ao_dev, -1)  12.7 us
    all_to_all x1, waiting for transfers between devices, on_device(): a_own = lax.all_to_all(a_slice, 'chip', 0, 0).reshape(ao_dev, occ)  10.9 us
    dot_general x4, matrix products, product(): jnp.dot(left, right.reshape(-1, occ), preferred_element_type=jnp.float32)  10.8 us
  transfers between devices with their start and end apart: 33, of which 21 were waited for; matrix products, arithmetic and copies ran while one was open for 9% of the time, Pallas kernels for 11%

profile of v3, /device:TPU:7, one launch (start us, length us, event | category | flops | bytes accessed | tf_op | source)
XLA Modules:
  0.0 276.6 jit_solution(12983133705786534062)
XLA Ops:
  0.0 2.7 collective-permute-start
  10.5 5.4 %masked_columns.1 = (bf16[1024,1024]{1,0:T(8,128)(2,1)S(1)}, bf16[1024,1024]{1,0:T(8,128)(2,1)S(1)}, bf16[1024,1024]{1,0:T(8,128)(2,1)S(1)}, bf16[1024,1024]{1,0:T(8,128)(2,1)S(1)}) custom-call(s32[16]{0:T(128)S(1)} %pad_add_fusion.2.cols, f32[8,4096]{1,0:T(8,128)S(1)} %convert_element_type.48.refs_0_.refs_1_.refs_2_.refs_3_, ...), custom_call_target="tpu_custom_call" | custom-call | tf_op jit(solution)/shard_map/masked_columns/pallas_call | solution.py:100
  19.4 2.7 collective-permute-start.4
  30.3 3.7 %collective-permute-done.9 = bf16[128,1024]{1,0:T(8,128)(2,1)S(1)} collective-permute-done((bf16[128,1024]{1,0:T(8,128)(2,1)S(1)}, bf16[128,1024]{1,0:T(8,128)(2,1)S(1)}, u32[]{:S(2)}, u32[]{:S(2)}) %collective-permute-start.9) | collective-permute-done | bytes 262176 | tf_op jit(solution)/shard_map/ppermute | solution.py:25
  34.1 2.5 collective-permute-start.11
  40.3 2.3 fusion.12
  42.8 3.5 %collective-permute-done.12 = bf16[128,1024]{1,0:T(8,128)(2,1)S(1)} collective-permute-done((bf16[128,1024]{1,0:T(8,128)(2,1)S(1)}, bf16[128,1024]{1,0:T(8,128)(2,1)S(1)}, u32[]{:S(2)}, u32[]{:S(2)}) %collective-permute-start.12) | collective-permute-done | bytes 262176 | tf_op jit(solution)/shard_map/ppermute | solution.py:25
  54.6 3.7 %add_convert_fusion = bf16[1024,1024]{1,0:T(8,128)(2,1)} fusion(f32[1024,1024]{1,0:T(8,128)S(1)} %add.81, f32[1024,1024]{1,0:T(8,128)S(1)} %fusion.14, bf16[1024,1024]{1,0:T(8,128)(2,1)S(1)} %get-tuple-element.60, bf16[1024,1024]{1,0:T(8,128)(2,1)S(1)} %bitcast.47), kind=kOutput, calls=%fused_computation | convolution fusion | flops 2150629376 | bytes 14680064 | tf_op jit(solution)/shard_map/dot_general | solution.py:281
  61.1 2.4 collective-permute-done.15.refs_1_
  63.5 4.0 %all-to-all-start = ((bf16[8,32,1024]{2,1,0:T(8,128)(2,1)}), bf16[8,32,1024]{2,1,0:T(8,128)(2,1)S(1)}, u32[]{:S(2)}, u32[]{:S(2)}) async-start(bf16[8,32,1024]{2,1,0:T(8,128)(2,1)} %bitcast.2), calls=%async_computation | async-start | bytes 1048576 | tf_op jit(solution)/shard_map/all_to_all | solution.py:306
  67.6 39.4 %collective-permute-done.16.refs_3_ = bf16[4,256,1024]{2,1,0:T(8,128)(2,1)} collective-permute-done((bf16[4,256,1024]{2,1,0:T(8,128)(2,1)}, bf16[4,256,1024]{2,1,0:T(8,128)(2,1)}, u32[]{:S(2)}, u32[]{:S(2)}) %collective-permute-start.16) | collective-permute-done | bytes 2097184 | tf_op jit(solution)/shard_map/ppermute | solution.py:25
  108.3 2.9 %collective-permute-start.17 = (bf16[2,256,1024]{2,1,0:T(8,128)(2,1)S(1)}, bf16[2,256,1024]{2,1,0:T(8,128)(2,1)}, u32[]{:S(2)}, u32[]{:S(2)}) collective-permute-start(bf16[2,256,1024]{2,1,0:T(8,128)(2,1)S(1)} %slice.66), channel_id=1, source_target_pairs={{0,6},{1,7},{2,0},{3,1},{4,2},{5,3},{6,4},{7,5},{8,14},{9,15},{10,... | collective-permute-start | bytes 3145736 | tf_op jit(solution)/shard_map/ppermute | solution.py:25
  115.1 4.2 %all-to-all-start.1 = ((bf16[8,32,1024]{2,1,0:T(8,128)(2,1)}), bf16[8,32,1024]{2,1,0:T(8,128)(2,1)S(1)}, u32[]{:S(2)}, u32[]{:S(2)}) async-start(bf16[8,32,1024]{2,1,0:T(8,128)(2,1)} %broadcast_in_dim.13), calls=%async_computation.1 | async-start | bytes 1048576 | tf_op jit(solution)/shard_map/all_to_all | solution.py:309
  119.3 10.2 %exchange_tiles.2 = bf16[8,2,32,1024]{3,2,1,0:T(8,128)(2,1)} custom-call(s32[1]{0:T(128)} %bitcast.core_ref, bf16[4,256,1024]{2,1,0:T(8,128)(2,1)} %bitcast.7.refs_0_.refs_2_, bf16[4,256,1024]{2,1,0:T(8,128)(2,1)} %collective-permute-done.15.refs_1_, bf16[4,256,1024]{2,1,0:T(8,128)(2,1)} %bitcast.7.refs_0_.refs_2_, ...), custom_call_target="tpu_custom_call" | custom-call | flops 4294967296 | bytes 13631488 | tf_op jit(solution)/shard_map/exchange_tiles/pallas_call | solution.py:141
  129.6 10.9 %all-to-all-done.1 = bf16[8,32,1024]{2,1,0:T(8,128)(2,1)S(1)} async-done(((bf16[8,32,1024]{2,1,0:T(8,128)(2,1)}), bf16[8,32,1024]{2,1,0:T(8,128)(2,1)S(1)}, u32[]{:S(2)}, u32[]{:S(2)}) %all-to-all-start.1) | async-done | bytes 524320 | tf_op jit(solution)/shard_map/all_to_all | solution.py:309
  140.5 2.7 collective-permute-start.23
  144.7 12.8 %all-to-all-start.3 = ((bf16[16,32,1024]{2,1,0:T(8,128)(2,1)}), bf16[16,32,1024]{2,1,0:T(8,128)(2,1)S(1)}, u32[]{:S(2)}, u32[]{:S(2)}) async-start(bf16[16,32,1024]{2,1,0:T(8,128)(2,1)} %bitcast.53), calls=%async_computation.3 | async-start | bytes 2097152 | tf_op jit(solution)/shard_map/all_to_all | solution.py:162
  157.5 6.5 %collective-permute-done.21.refs_4_ = bf16[2,256,1024]{2,1,0:T(8,128)(2,1)S(1)} collective-permute-done((bf16[2,256,1024]{2,1,0:T(8,128)(2,1)}, bf16[2,256,1024]{2,1,0:T(8,128)(2,1)S(1)}, u32[]{:S(2)}, u32[]{:S(2)}) %collective-permute-start.21) | collective-permute-done | bytes 1048608 | tf_op jit(solution)/shard_map/ppermute | solution.py:25
  164.0 22.5 %collective-permute-done.22.refs_5_ = bf16[2,256,1024]{2,1,0:T(8,128)(2,1)} collective-permute-done((bf16[2,256,1024]{2,1,0:T(8,128)(2,1)}, bf16[2,256,1024]{2,1,0:T(8,128)(2,1)}, u32[]{:S(2)}, u32[]{:S(2)}) %collective-permute-start.22) | collective-permute-done | bytes 1048608 | tf_op jit(solution)/shard_map/ppermute | solution.py:25
  186.5 3.1 %collective-permute-done.24.refs_7_ = bf16[4,256,1024]{2,1,0:T(8,128)(2,1)} collective-permute-done((bf16[4,256,1024]{2,1,0:T(8,128)(2,1)}, bf16[4,256,1024]{2,1,0:T(8,128)(2,1)}, u32[]{:S(2)}, u32[]{:S(2)}) %collective-permute-start.24) | collective-permute-done | bytes 2097184 | tf_op jit(solution)/shard_map/ppermute | solution.py:25
  189.6 10.2 %exchange_tiles.3 = bf16[8,2,32,1024]{3,2,1,0:T(8,128)(2,1)} custom-call(s32[1]{0:T(128)} %bitcast.core_ref, bf16[4,256,1024]{2,1,0:T(8,128)(2,1)} %bitcast.7.refs_0_.refs_2_, bf16[4,256,1024]{2,1,0:T(8,128)(2,1)} %collective-permute-done.15.refs_1_, bf16[2,256,1024]{2,1,0:T(8,128)(2,1)} %collective-permute-done.17.refs_2_, ...), custom_call_target="tpu_custom_call" | custom-call | flops 4294967296 | bytes 13631488 | tf_op jit(solution)/shard_map/exchange_tiles/pallas_call | solution.py:141
  199.8 5.6 %all-to-all-done.3.got = bf16[16,32,1024]{2,1,0:T(8,128)(2,1)S(1)} async-done(((bf16[16,32,1024]{2,1,0:T(8,128)(2,1)}), bf16[16,32,1024]{2,1,0:T(8,128)(2,1)S(1)}, u32[]{:S(2)}, u32[]{:S(2)}) %all-to-all-start.3) | async-done | bytes 1048608 | tf_op jit(solution)/shard_map/all_to_all | solution.py:162
  205.5 9.3 %all-to-all-start.2 = ((bf16[16,32,1024]{2,1,0:T(8,128)(2,1)}), bf16[16,32,1024]{2,1,0:T(8,128)(2,1)}, u32[]{:S(2)}, u32[]{:S(2)}) async-start(bf16[16,32,1024]{2,1,0:T(8,128)(2,1)} %bitcast.54), calls=%async_computation.2 | async-start | bytes 2097152 | tf_op jit(solution)/shard_map/all_to_all | solution.py:162
  217.3 3.2 %early_rows.1 = (f32[2,32,1024]{2,1,0:T(8,128)S(1)}, f32[32,1024]{1,0:T(8,128)S(1)}) custom-call(s32[1]{0:T(128)} %bitcast.core_ref, bf16[16,32,1024]{2,1,0:T(8,128)(2,1)S(1)} %all-to-all-done.3.got, bf16[4,256,1024]{2,1,0:T(8,128)(2,1)S(1)} %bitcast.45, bf16[4,256,1024]{2,1,0:T(8,128)(2,1)S(1)} %copy-done.6, bf16[4,256,1024]{2,1,0:T(8,128)(2,1)} %bitcast.41, ...), custom_call_target="tpu_custom_call" | custom-call | flops 134217728 | bytes 8388608 | tf_op jit(solution)/shard_map/early_rows/pallas_call | solution.py:223
  220.5 9.7 %all-to-all-done.2.got = bf16[16,32,1024]{2,1,0:T(8,128)(2,1)} async-done(((bf16[16,32,1024]{2,1,0:T(8,128)(2,1)}), bf16[16,32,1024]{2,1,0:T(8,128)(2,1)}, u32[]{:S(2)}, u32[]{:S(2)}) %all-to-all-start.2) | async-done | bytes 1048608 | tf_op jit(solution)/shard_map/all_to_all | solution.py:162
  231.4 4.4 %late_rows.1 = bf16[8,32,2048]{2,1,0:T(8,128)(2,1)} custom-call(s32[9]{0:T(128)S(1)} %pad_add_fusion.1.scalars, bf16[16,32,1024]{2,1,0:T(8,128)(2,1)} %all-to-all-done.2.got, f32[2,32,1024]{2,1,0:T(8,128)S(1)} %get-tuple-element.68.k_early, f32[32,1024]{1,0:T(8,128)S(1)} %get-tuple-element.69.b_early, f32[1,1024]{1,0:T(1,128)S(1)} %bitcast.46, ...), custom_call_target="tpu_custom_call" | custom-call | flops 134217728 | bytes 8388608 | tf_op jit(solution)/shard_map/late_rows/pallas_call | solution.py:223
  235.8 5.6 %all-to-all-start.4 = ((bf16[8,32,2048]{2,1,0:T(8,128)(2,1)}), bf16[8,32,2048]{2,1,0:T(8,128)(2,1)S(1)}, u32[]{:S(2)}, u32[]{:S(2)}) async-start(bf16[8,32,2048]{2,1,0:T(8,128)(2,1)} %late_rows.1), calls=%async_computation.4 | async-start | bytes 2097152 | tf_op jit(solution)/shard_map/all_to_all | solution.py:324
  242.6 12.7 %all-to-all-done.4 = bf16[8,32,2048]{2,1,0:T(8,128)(2,1)S(1)} async-done(((bf16[8,32,2048]{2,1,0:T(8,128)(2,1)}), bf16[8,32,2048]{2,1,0:T(8,128)(2,1)S(1)}, u32[]{:S(2)}, u32[]{:S(2)}) %all-to-all-start.4) | async-done | bytes 1048608 | tf_op jit(solution)/shard_map/all_to_all | solution.py:324
  256.1 3.5 %collective-permute-start.27 = (bf16[256,256]{1,0:T(8,128)(2,1)S(1)}, bf16[256,256]{1,0:T(8,128)(2,1)S(1)}, u32[]{:S(2)}, u32[]{:S(2)}) collective-permute-start(bf16[256,256]{1,0:T(8,128)(2,1)S(1)} %copy.15), channel_id=1, source_target_pairs={{0,1},{1,0},{2,17},{3,16},{4,33},{5,32},{6,49},{7,48},{8,65},{9,64... | collective-permute-start | bytes 393224 | tf_op jit(solution)/shard_map/ppermute | solution.py:25
  259.7 6.2 %collective-permute-start.25 = (bf16[256,256]{1,0:T(8,128)(2,1)S(1)}, bf16[256,256]{1,0:T(8,128)(2,1)S(1)}, u32[]{:S(2)}, u32[]{:S(2)}) collective-permute-start(bf16[256,256]{1,0:T(8,128)(2,1)S(1)} %copy.14), channel_id=1, source_target_pairs={{0,0},{1,1},{2,16},{3,17},{4,32},{5,33},{6,48},{7,49},{8,64},{9,65... | collective-permute-start | bytes 393224 | tf_op jit(solution)/shard_map/ppermute | solution.py:25
  266.3 3.1 %collective-permute-done.27 = bf16[256,256]{1,0:T(8,128)(2,1)S(1)} collective-permute-done((bf16[256,256]{1,0:T(8,128)(2,1)S(1)}, bf16[256,256]{1,0:T(8,128)(2,1)S(1)}, u32[]{:S(2)}, u32[]{:S(2)}) %collective-permute-start.27) | collective-permute-done | bytes 131104 | tf_op jit(solution)/shard_map/ppermute | solution.py:25
  269.4 6.1 %collective-permute-done.25 = bf16[256,256]{1,0:T(8,128)(2,1)S(1)} collective-permute-done((bf16[256,256]{1,0:T(8,128)(2,1)S(1)}, bf16[256,256]{1,0:T(8,128)(2,1)S(1)}, u32[]{:S(2)}, u32[]{:S(2)}) %collective-permute-start.25) | collective-permute-done | bytes 131104 | tf_op jit(solution)/shard_map/ppermute | solution.py:25
  (132 shorter events, 48.3 us)
Async XLA Ops:
  0.0 16.1 %collective-permute-start = (bf16[256,1024]{1,0:T(8,128)(2,1)}, bf16[256,1024]{1,0:T(8,128)(2,1)S(1)}, u32[]{:S(2)}, u32[]{:S(2)}) collective-permute-start(bf16[256,1024]{1,0:T(8,128)(2,1)} %param.8), channel_id=1, source_target_pairs={{0,6},{1,7},{2,0},{3,1},{4,2},{5,3},{6,4},{7,5},{8,14},{9,15},{10,... | collective-permute-start | bytes 1572872 | tf_op jit(solution)/shard_map/ppermute | solution.py:25
  2.7 14.0 %collective-permute-start.1 = (bf16[256,1024]{1,0:T(8,128)(2,1)}, bf16[256,1024]{1,0:T(8,128)(2,1)}, u32[]{:S(2)}, u32[]{:S(2)}) collective-permute-start(bf16[256,1024]{1,0:T(8,128)(2,1)} %param.8), channel_id=1, source_target_pairs={{0,2},{1,3},{2,4},{3,5},{4,6},{5,7},{6,0},{7,1},{8,10},{9,11},{10,... | collective-permute-start | bytes 1572872 | tf_op jit(solution)/shard_map/ppermute | solution.py:25
  4.6 11.4 %collective-permute-start.2 = (bf16[128,1024]{1,0:T(8,128)(2,1)}, bf16[128,1024]{1,0:T(8,128)(2,1)}, u32[]{:S(2)}, u32[]{:S(2)}) collective-permute-start(bf16[128,1024]{1,0:T(8,128)(2,1)} %get-tuple-element.82), channel_id=1, source_target_pairs={{0,8},{1,9},{2,10},{3,11},{4,12},{5,13},{6,14},{7,15},{8,0},{9,1},... | collective-permute-start | bytes 786440 | tf_op jit(solution)/shard_map/ppermute | solution.py:25
  5.2 10.9 %collective-permute-start.3 = (bf16[128,1024]{1,0:T(8,128)(2,1)}, bf16[128,1024]{1,0:T(8,128)(2,1)}, u32[]{:S(2)}, u32[]{:S(2)}) collective-permute-start(bf16[128,1024]{1,0:T(8,128)(2,1)} %get-tuple-element.81), channel_id=1, source_target_pairs={{0,24},{1,25},{2,26},{3,27},{4,28},{5,29},{6,30},{7,31},{8,16},{9,... | collective-permute-start | bytes 786440 | tf_op jit(solution)/shard_map/ppermute | solution.py:25
  8.5 14.7 %collective-permute-start.6 = (bf16[256,1024]{1,0:T(8,128)(2,1)}, bf16[256,1024]{1,0:T(8,128)(2,1)}, u32[]{:S(2)}, u32[]{:S(2)}) collective-permute-start(bf16[256,1024]{1,0:T(8,128)(2,1)} %select_convert_fusion), channel_id=1, source_target_pairs={{0,1},{1,0},{2,3},{3,2},{4,5},{5,4},{6,7},{7,6},{8,9},{9,8},{10,11... | collective-permute-start | bytes 1572872 | tf_op jit(solution)/shard_map/ppermute | solution.py:25
  17.8 7.2 %collective-permute-start.10 = (bf16[128,1024]{1,0:T(8,128)(2,1)S(1)}, bf16[128,1024]{1,0:T(8,128)(2,1)S(1)}, u32[]{:S(2)}, u32[]{:S(2)}) collective-permute-start(bf16[128,1024]{1,0:T(8,128)(2,1)S(1)} %get-tuple-element.78), channel_id=1, source_target_pairs={{0,24},{1,25},{2,26},{3,27},{4,28},{5,29},{6,30},{7,31},{8,16},{9,... | collective-permute-start | bytes 786440 | tf_op jit(solution)/shard_map/ppermute | solution.py:25
  19.0 8.5 %collective-permute-start.5 = (bf16[128,1024]{1,0:T(8,128)(2,1)S(1)}, bf16[128,1024]{1,0:T(8,128)(2,1)S(1)}, u32[]{:S(2)}, u32[]{:S(2)}) collective-permute-start(bf16[128,1024]{1,0:T(8,128)(2,1)S(1)} %get-tuple-element.78), channel_id=1, source_target_pairs={{0,2},{1,3},{2,4},{3,5},{4,6},{5,7},{6,0},{7,1},{8,10},{9,11},{10,... | collective-permute-start | bytes 786440 | tf_op jit(solution)/shard_map/ppermute | solution.py:25
  19.4 8.2 %collective-permute-start.4 = (bf16[128,1024]{1,0:T(8,128)(2,1)S(1)}, bf16[128,1024]{1,0:T(8,128)(2,1)S(1)}, u32[]{:S(2)}, u32[]{:S(2)}) collective-permute-start(bf16[128,1024]{1,0:T(8,128)(2,1)S(1)} %get-tuple-element.80), channel_id=1, source_target_pairs={{0,6},{1,7},{2,0},{3,1},{4,2},{5,3},{6,4},{7,5},{8,14},{9,15},{10,... | collective-permute-start | bytes 786440 | tf_op jit(solution)/shard_map/ppermute | solution.py:25
  22.1 6.3 %collective-permute-start.7 = (bf16[128,1024]{1,0:T(8,128)(2,1)S(1)}, bf16[128,1024]{1,0:T(8,128)(2,1)S(1)}, u32[]{:S(2)}, u32[]{:S(2)}) collective-permute-start(bf16[128,1024]{1,0:T(8,128)(2,1)S(1)} %get-tuple-element.80), channel_id=1, source_target_pairs={{0,8},{1,9},{2,10},{3,11},{4,12},{5,13},{6,14},{7,15},{8,0},{9,1},... | collective-permute-start | bytes 786440 | tf_op jit(solution)/shard_map/ppermute | solution.py:25
  23.2 7.1 %collective-permute-start.8 = (bf16[128,1024]{1,0:T(8,128)(2,1)S(1)}, bf16[128,1024]{1,0:T(8,128)(2,1)S(1)}, u32[]{:S(2)}, u32[]{:S(2)}) collective-permute-start(bf16[128,1024]{1,0:T(8,128)(2,1)S(1)} %get-tuple-element.79), channel_id=1, source_target_pairs={{0,24},{1,25},{2,26},{3,27},{4,28},{5,29},{6,30},{7,31},{8,16},{9,... | collective-permute-start | bytes 786440 | tf_op jit(solution)/shard_map/ppermute | solution.py:25
  25.0 9.0 %collective-permute-start.9 = (bf16[128,1024]{1,0:T(8,128)(2,1)S(1)}, bf16[128,1024]{1,0:T(8,128)(2,1)S(1)}, u32[]{:S(2)}, u32[]{:S(2)}) collective-permute-start(bf16[128,1024]{1,0:T(8,128)(2,1)S(1)} %get-tuple-element.77), channel_id=1, source_target_pairs={{0,8},{1,9},{2,10},{3,11},{4,12},{5,13},{6,14},{7,15},{8,0},{9,1},... | collective-permute-start | bytes 786440 | tf_op jit(solution)/shard_map/ppermute | solution.py:25
  34.1 13.3 %collective-permute-start.11 = (bf16[4,256,1024]{2,1,0:T(8,128)(2,1)S(1)}, bf16[4,256,1024]{2,1,0:T(8,128)(2,1)S(1)}, u32[]{:S(2)}, u32[]{:S(2)}) collective-permute-start(bf16[4,256,1024]{2,1,0:T(8,128)(2,1)S(1)} %bitcast.44), channel_id=1, source_target_pairs={{0,1},{1,0},{2,3},{3,2},{4,5},{5,4},{6,7},{7,6},{8,9},{9,8},{10,11... | collective-permute-start | bytes 6291464 | tf_op jit(solution)/shard_map/ppermute | solution.py:25
  38.5 7.8 %collective-permute-start.12 = (bf16[128,1024]{1,0:T(8,128)(2,1)S(1)}, bf16[128,1024]{1,0:T(8,128)(2,1)S(1)}, u32[]{:S(2)}, u32[]{:S(2)}) collective-permute-start(bf16[128,1024]{1,0:T(8,128)(2,1)S(1)} %collective-permute-done.4), channel_id=1, source_target_pairs={{0,8},{1,9},{2,10},{3,11},{4,12},{5,13},{6,14},{7,15},{8,0},{9,1},... | collective-permute-start | bytes 786440 | tf_op jit(solution)/shard_map/ppermute | solution.py:25
  38.6 8.8 %collective-permute-start.13 = (bf16[128,1024]{1,0:T(8,128)(2,1)S(1)}, bf16[128,1024]{1,0:T(8,128)(2,1)S(1)}, u32[]{:S(2)}, u32[]{:S(2)}) collective-permute-start(bf16[128,1024]{1,0:T(8,128)(2,1)S(1)} %collective-permute-done.5), channel_id=1, source_target_pairs={{0,24},{1,25},{2,26},{3,27},{4,28},{5,29},{6,30},{7,31},{8,16},{9,... | collective-permute-start | bytes 786440 | tf_op jit(solution)/shard_map/ppermute | solution.py:25
  47.4 7.1 %collective-permute-start.14 = (bf16[4,256,1024]{2,1,0:T(8,128)(2,1)S(1)}, bf16[4,256,1024]{2,1,0:T(8,128)(2,1)S(1)}, u32[]{:S(2)}, u32[]{:S(2)}) collective-permute-start(bf16[4,256,1024]{2,1,0:T(8,128)(2,1)S(1)} %bitcast.40), channel_id=1, source_target_pairs={{0,1},{1,0},{2,3},{3,2},{4,5},{5,4},{6,7},{7,6},{8,9},{9,8},{10,11... | collective-permute-start | bytes 6291464 | tf_op jit(solution)/shard_map/ppermute | solution.py:25
  59.4 47.6 %collective-permute-start.16 = (bf16[4,256,1024]{2,1,0:T(8,128)(2,1)}, bf16[4,256,1024]{2,1,0:T(8,128)(2,1)}, u32[]{:S(2)}, u32[]{:S(2)}) collective-permute-start(bf16[4,256,1024]{2,1,0:T(8,128)(2,1)} %bitcast.7.refs_0_.refs_2_), channel_id=1, source_target_pairs={{0,6},{1,7},{2,0},{3,1},{4,2},{5,3},{6,4},{7,5},{8,14},{9,15},{10,... | collective-permute-start | bytes 6291464 | tf_op jit(solution)/shard_map/ppermute | solution.py:25
  61.0 50.5 %collective-permute-start.18 = (bf16[4,256,1024]{2,1,0:T(8,128)(2,1)}, bf16[4,256,1024]{2,1,0:T(8,128)(2,1)}, u32[]{:S(2)}, u32[]{:S(2)}) collective-permute-start(bf16[4,256,1024]{2,1,0:T(8,128)(2,1)} %bitcast.7.refs_0_.refs_2_), channel_id=1, source_target_pairs={{0,2},{1,3},{2,4},{3,5},{4,6},{5,7},{6,0},{7,1},{8,10},{9,11},{10,... | collective-permute-start | bytes 6291464 | tf_op jit(solution)/shard_map/ppermute | solution.py:25
  61.0 58.3 %collective-permute-start.20 = (bf16[4,256,1024]{2,1,0:T(8,128)(2,1)}, bf16[4,256,1024]{2,1,0:T(8,128)(2,1)}, u32[]{:S(2)}, u32[]{:S(2)}) collective-permute-start(bf16[4,256,1024]{2,1,0:T(8,128)(2,1)} %bitcast.7.refs_0_.refs_2_), channel_id=1, source_target_pairs={{0,8},{1,9},{2,10},{3,11},{4,12},{5,13},{6,14},{7,15},{8,0},{9,1},... | collective-permute-start | bytes 6291464 | tf_op jit(solution)/shard_map/ppermute | solution.py:25
  63.5 50.7 %all-to-all-start = ((bf16[8,32,1024]{2,1,0:T(8,128)(2,1)}), bf16[8,32,1024]{2,1,0:T(8,128)(2,1)S(1)}, u32[]{:S(2)}, u32[]{:S(2)}) async-start(bf16[8,32,1024]{2,1,0:T(8,128)(2,1)} %bitcast.2), calls=%async_computation | async-start | bytes 1048576 | tf_op jit(solution)/shard_map/all_to_all | solution.py:306
  108.3 32.3 %collective-permute-start.17 = (bf16[2,256,1024]{2,1,0:T(8,128)(2,1)S(1)}, bf16[2,256,1024]{2,1,0:T(8,128)(2,1)}, u32[]{:S(2)}, u32[]{:S(2)}) collective-permute-start(bf16[2,256,1024]{2,1,0:T(8,128)(2,1)S(1)} %slice.66), channel_id=1, source_target_pairs={{0,6},{1,7},{2,0},{3,1},{4,2},{5,3},{6,4},{7,5},{8,14},{9,15},{10,... | collective-permute-start | bytes 3145736 | tf_op jit(solution)/shard_map/ppermute | solution.py:25
  112.7 27.8 %collective-permute-start.19 = (bf16[2,256,1024]{2,1,0:T(8,128)(2,1)S(1)}, bf16[2,256,1024]{2,1,0:T(8,128)(2,1)}, u32[]{:S(2)}, u32[]{:S(2)}) collective-permute-start(bf16[2,256,1024]{2,1,0:T(8,128)(2,1)S(1)} %slice.67), channel_id=1, source_target_pairs={{0,2},{1,3},{2,4},{3,5},{4,6},{5,7},{6,0},{7,1},{8,10},{9,11},{10,... | collective-permute-start | bytes 3145736 | tf_op jit(solution)/shard_map/ppermute | solution.py:25
  115.1 25.4 %all-to-all-start.1 = ((bf16[8,32,1024]{2,1,0:T(8,128)(2,1)}), bf16[8,32,1024]{2,1,0:T(8,128)(2,1)S(1)}, u32[]{:S(2)}, u32[]{:S(2)}) async-start(bf16[8,32,1024]{2,1,0:T(8,128)(2,1)} %broadcast_in_dim.13), calls=%async_computation.1 | async-start | bytes 1048576 | tf_op jit(solution)/shard_map/all_to_all | solution.py:309
  140.5 46.0 %collective-permute-start.23 = (bf16[4,256,1024]{2,1,0:T(8,128)(2,1)}, bf16[4,256,1024]{2,1,0:T(8,128)(2,1)}, u32[]{:S(2)}, u32[]{:S(2)}) collective-permute-start(bf16[4,256,1024]{2,1,0:T(8,128)(2,1)} %collective-permute-done.20.refs_5_), channel_id=1, source_target_pairs={{0,6},{1,7},{2,0},{3,1},{4,2},{5,3},{6,4},{7,5},{8,14},{9,15},{10,... | collective-permute-start | bytes 6291464 | tf_op jit(solution)/shard_map/ppermute | solution.py:25
  143.3 46.3 %collective-permute-start.24 = (bf16[4,256,1024]{2,1,0:T(8,128)(2,1)}, bf16[4,256,1024]{2,1,0:T(8,128)(2,1)}, u32[]{:S(2)}, u32[]{:S(2)}) collective-permute-start(bf16[4,256,1024]{2,1,0:T(8,128)(2,1)} %collective-permute-done.20.refs_5_), channel_id=1, source_target_pairs={{0,2},{1,3},{2,4},{3,5},{4,6},{5,7},{6,0},{7,1},{8,10},{9,11},{10,... | collective-permute-start | bytes 6291464 | tf_op jit(solution)/shard_map/ppermute | solution.py:25
  143.3 20.7 %collective-permute-start.21 = (bf16[2,256,1024]{2,1,0:T(8,128)(2,1)}, bf16[2,256,1024]{2,1,0:T(8,128)(2,1)S(1)}, u32[]{:S(2)}, u32[]{:S(2)}) collective-permute-start(bf16[2,256,1024]{2,1,0:T(8,128)(2,1)} %collective-permute-done.17.refs_2_), channel_id=1, source_target_pairs={{0,8},{1,9},{2,10},{3,11},{4,12},{5,13},{6,14},{7,15},{8,0},{9,1},... | collective-permute-start | bytes 3145736 | tf_op jit(solution)/shard_map/ppermute | solution.py:25
  143.4 43.0 %collective-permute-start.22 = (bf16[2,256,1024]{2,1,0:T(8,128)(2,1)}, bf16[2,256,1024]{2,1,0:T(8,128)(2,1)}, u32[]{:S(2)}, u32[]{:S(2)}) collective-permute-start(bf16[2,256,1024]{2,1,0:T(8,128)(2,1)} %collective-permute-done.19.refs_3_), channel_id=1, source_target_pairs={{0,8},{1,9},{2,10},{3,11},{4,12},{5,13},{6,14},{7,15},{8,0},{9,1},... | collective-permute-start | bytes 3145736 | tf_op jit(solution)/shard_map/ppermute | solution.py:25
  144.7 60.7 %all-to-all-start.3 = ((bf16[16,32,1024]{2,1,0:T(8,128)(2,1)}), bf16[16,32,1024]{2,1,0:T(8,128)(2,1)S(1)}, u32[]{:S(2)}, u32[]{:S(2)}) async-start(bf16[16,32,1024]{2,1,0:T(8,128)(2,1)} %bitcast.53), calls=%async_computation.3 | async-start | bytes 2097152 | tf_op jit(solution)/shard_map/all_to_all | solution.py:162
  205.5 24.7 %all-to-all-start.2 = ((bf16[16,32,1024]{2,1,0:T(8,128)(2,1)}), bf16[16,32,1024]{2,1,0:T(8,128)(2,1)}, u32[]{:S(2)}, u32[]{:S(2)}) async-start(bf16[16,32,1024]{2,1,0:T(8,128)(2,1)} %bitcast.54), calls=%async_computation.2 | async-start | bytes 2097152 | tf_op jit(solution)/shard_map/all_to_all | solution.py:162
  235.8 19.5 %all-to-all-start.4 = ((bf16[8,32,2048]{2,1,0:T(8,128)(2,1)}), bf16[8,32,2048]{2,1,0:T(8,128)(2,1)S(1)}, u32[]{:S(2)}, u32[]{:S(2)}) async-start(bf16[8,32,2048]{2,1,0:T(8,128)(2,1)} %late_rows.1), calls=%async_computation.4 | async-start | bytes 2097152 | tf_op jit(solution)/shard_map/all_to_all | solution.py:324
  241.4 14.2 %collective-permute-start.26 = (bf16[256,1024]{1,0:T(8,128)(2,1)S(1)}, bf16[256,1024]{1,0:T(8,128)(2,1)S(1)}, u32[]{:S(2)}, u32[]{:S(2)}) collective-permute-start(bf16[256,1024]{1,0:T(8,128)(2,1)S(1)} %bitcast.51), channel_id=1, source_target_pairs={{0,1},{1,0},{2,3},{3,2},{4,5},{5,4},{6,7},{7,6},{8,9},{9,8},{10,11... | collective-permute-start | bytes 1572872 | tf_op jit(solution)/shard_map/ppermute | solution.py:25
  256.1 13.3 %collective-permute-start.27 = (bf16[256,256]{1,0:T(8,128)(2,1)S(1)}, bf16[256,256]{1,0:T(8,128)(2,1)S(1)}, u32[]{:S(2)}, u32[]{:S(2)}) collective-permute-start(bf16[256,256]{1,0:T(8,128)(2,1)S(1)} %copy.15), channel_id=1, source_target_pairs={{0,1},{1,0},{2,17},{3,16},{4,33},{5,32},{6,49},{7,48},{8,65},{9,64... | collective-permute-start | bytes 393224 | tf_op jit(solution)/shard_map/ppermute | solution.py:25
  259.7 15.7 %collective-permute-start.25 = (bf16[256,256]{1,0:T(8,128)(2,1)S(1)}, bf16[256,256]{1,0:T(8,128)(2,1)S(1)}, u32[]{:S(2)}, u32[]{:S(2)}) collective-permute-start(bf16[256,256]{1,0:T(8,128)(2,1)S(1)} %copy.14), channel_id=1, source_target_pairs={{0,0},{1,1},{2,16},{3,17},{4,32},{5,33},{6,48},{7,49},{8,64},{9,65... | collective-permute-start | bytes 393224 | tf_op jit(solution)/shard_map/ppermute | solution.py:25
  (22 other events, 268.9 us)

commit v4 on v3

--- a/solution.py
+++ b/solution.py
@@ -181,23 +181,23 @@
     for t, (nc, cc) in enumerate(((near, cross), (near_oth, cross_oth))):
         rows = sum_groups(got, core if t == 0 else 1 - core)
         k_ref[t] = rows
-        for at, block in enumerate((nc[0], nc[1], nc[2], cc[0])):
+        for at, block in enumerate((nc[0], nc[1], nc[2], cc[1], cc[0])):
             total += rows_times(rows, at, block)
     b_ref[...] = total
 
 
-def late_kernel(scalars, got, k_early, b_early, flag, cross, cross_oth, far, out_ref):
+def late_kernel(scalars, got, k_early, b_early, flag, rest, rest_oth, out_ref):
     core = scalars[0]
     occ = b_early.shape[1]
-    depth = cross.shape[1]
+    depth = rest.shape[1]
     total = b_early[...]
     tiles = []
-    for t, cc in enumerate((cross, cross_oth)):
+    for t, cc in enumerate((rest, rest_oth)):
         rows = sum_groups(got, core if t == 0 else 1 - core)
-        for at, block in enumerate((far[t], cc[3], cc[1], cc[2])):
+        for at, block in enumerate((cc[4], cc[2], cc[3])):
             total += rows_times(rows, at, block)
-        mine = [k_early[t, :, at * depth : (at + 1) * depth] for at in range(4)]
-        tiles.append(mine + [rows[:, at * depth : (at + 1) * depth] for at in range(4)])
+        mine = [k_early[t, :, at * depth : (at + 1) * depth] for at in range(5)]
+        tiles.append(mine + [rows[:, at * depth : (at + 1) * depth] for at in range(3)])
     for t in range(2):
         first = occ + t * depth
         for at, place in enumerate((0, 1, 2, 4, 3, 7, 5, 6)):
@@ -247,10 +247,10 @@
     return on_chip(early_kernel, "early_rows", shapes, core.reshape(1), *args)
 
 
-def late_rows(scalars, got, k_early, b_early, flag, cross, cross_oth, far):
+def late_rows(scalars, got, k_early, b_early, flag, rest, rest_oth):
     rows, occ = b_early.shape
-    shape = jax.ShapeDtypeStruct((8, rows, occ + 4 * cross.shape[1]), jnp.bfloat16)
-    args = (got, k_early, b_early, flag, cross, cross_oth, far)
+    shape = jax.ShapeDtypeStruct((8, rows, occ + 4 * rest.shape[1]), jnp.bfloat16)
+    args = (got, k_early, b_early, flag, rest, rest_oth)
     return on_chip(late_kernel, "late_rows", shape, scalars, *args)
 
 
@@ -266,16 +266,13 @@
         margin, orbitals, (((0,), (0,)), ((), ())), preferred_element_type=jnp.float32
     )
     a_low, a_high = a_part[:ao_dev], a_part[ao_dev:]
-    a_send = other_core(jnp.where(core == 0, a_high, a_low).astype(jnp.bfloat16))
-    a_part = jnp.where(core == 0, a_low, a_high) + a_send.astype(jnp.float32)
-    a_part = a_part.astype(jnp.bfloat16).reshape(8, 32, occ)
+    a_send = other_core(jnp.where(core == 0, a_high, a_low))
     order = (y + jnp.array([0, 1, NY - 1, 2], jnp.int32)) % NY
-    near_cols = ((a * NY + order) * NK).astype(jnp.int32)
-    cross_cols = (((1 - a) * NY + order) * NK).astype(jnp.int32)
-    near_cols = jnp.concatenate([near_cols + core, near_cols + 1 - core])
-    cross_cols = jnp.concatenate([cross_cols + core, cross_cols + 1 - core])
+    sides = jnp.concatenate([a * NY + order, (1 - a) * NY + order]).astype(jnp.int32)
+    cols = jnp.concatenate([sides * NK + core, sides * NK + 1 - core])
     keep = jnp.repeat(block_mask[0], ATILE, axis=1).astype(jnp.float32)
-    masked = masked_columns(jnp.concatenate([near_cols, cross_cols]), keep, slab, ao_dev, NY)
+    own_m, oth_m = masked_columns(cols, keep, slab, ao_dev, NA * NY)
+    wide = 3 * ao_dev
 
     def product(left, right):
         return jnp.dot(left, right.reshape(-1, occ), preferred_element_type=jnp.float32)
@@ -283,44 +280,55 @@
     def cross_over(t):
         return [across_in(t[:hb]), across_out(t[hb:])]
 
-    nxt, prv, *own_x, masked = lax.optimization_barrier(
-        (from_next(orbitals), from_prev(orbitals), *cross_over(orbitals), masked)
+    nxt, prv, *own_x, own_m, oth_m = lax.optimization_barrier(
+        (from_next(orbitals), from_prev(orbitals), *cross_over(orbitals), own_m, oth_m)
     )
-    far_lo, far_hi, a_part, *side_x = lax.optimization_barrier(
-        (from_next(nxt[:hb]), from_prev(prv[hb:]), a_part, *cross_over(nxt), *cross_over(prv))
+    near = jnp.concatenate([orbitals, nxt, prv]).reshape(3, ao_dev, occ)
+    base = product(own_m[:, :wide], near)
+    far_lo, far_hi, side_in, side_out, near, base, a_send = lax.optimization_barrier(
+        (
+            from_next(nxt[:hb]),
+            from_prev(prv[hb:]),
+            across_in(jnp.concatenate([nxt[:hb], prv[:hb]])),
+            across_out(jnp.concatenate([nxt[hb:], prv[hb:]])),
+            near,
+            base,
+            a_send,
+        )
     )
-    near = jnp.concatenate([orbitals, nxt, prv, far_lo, far_hi]).reshape(NY, ao_dev, occ)
-    base = product(masked[0], near)
-    near_oth, far_lo_x, far_hi_x, base = lax.optimization_barrier(
-        (other_core(near), across_in(far_lo), across_out(far_hi), base)
-    )
-    cross = jnp.concatenate([*own_x, *side_x, far_lo_x, far_hi_x]).reshape(NY, ao_dev, occ)
-    base += product(masked[1], near_oth)
-    cross_oth, base = lax.optimization_barrier((other_core(cross), base))
-    part = base + product(masked[2], cross) + product(masked[3], cross_oth)
+    side_x = [side_in[:hb], side_out[:hb], side_in[hb:], side_out[hb:]]
+    far_x = [across_in(far_lo), across_out(far_hi)]
+    near_oth = other_core(near)
+    base += product(oth_m[:, :wide], near_oth)
+    *far_x, base = lax.optimization_barrier((*far_x, base))
+    rest = jnp.concatenate([far_lo, far_hi, *own_x, *side_x, *far_x]).reshape(5, ao_dev, occ)
+    rest_oth = other_core(rest)
+    base += product(own_m[:, wide:], rest)
+    rest_oth, base = lax.optimization_barrier((rest_oth, base))
+    part = base + product(oth_m[:, wide:], rest_oth)
     part = part.astype(jnp.bfloat16).reshape(aux_dev, ao_dev, occ)
     mid = aux_dev // 2
 
     x, n, p = across_in(part), from_next(part), from_prev(part)
     mate = other_core(part)
-    a_got = lax.all_to_all(after(a_part, mate), "chip", 0, 0)
+    a_send = after(a_send, mate)
+    a_part = jnp.where(core == 0, a_low, a_high) + a_send
+    a_part = a_part.astype(jnp.bfloat16).reshape(8, 32, occ)
+    a_got = lax.all_to_all(a_part, "chip", 0, 0)
     a_slice = (a_got.astype(jnp.float32).sum(0) * flag).astype(jnp.bfloat16)
     a_slice = jnp.broadcast_to(a_slice[None], (8,) + a_slice.shape)
     a_own = lax.all_to_all(a_slice, "chip", 0, 0).reshape(ao_dev, occ)
     f, g = from_next(n[:mid]), from_prev(p[mid:])
-    early = pair_tiles(core, part, mate, part, n, p, x)
-    f, g, x, early, a_own = lax.optimization_barrier((f, g, x, early, a_own))
+    f, g, x, a_own = lax.optimization_barrier((f, g, x, a_own))
     a_oth = other_core(a_own)
     xn, xp = from_next(x), from_prev(x)
     xf, xg = across_in(f), across_in(g)
-    early = exchanged(early)
-    k_early, b_early = early_rows(core, early, near, near_oth, cross, cross_oth)
-
-    late = exchanged(pair_tiles(core, part, mate, f, g, xf, xg, xn, xp))
-    places = jnp.concatenate([near_cols[:4], cross_cols[:4]]) // NK
-    scalars = jnp.concatenate([core.reshape(1), places]).astype(jnp.int32)
-    far_c = jnp.stack([near[3], near_oth[3]])
-    packed = late_rows(scalars, late, k_early, b_early, flag, cross, cross_oth, far_c)
+    early = exchanged(pair_tiles(core, part, mate, part, n, p, x, f, g))
+    k_early, b_early = early_rows(core, early, near, near_oth, rest[:2], rest_oth[:2])
+
+    late = exchanged(pair_tiles(core, part, mate, xf, xg, xn, xp))
+    scalars = jnp.concatenate([core.reshape(1), sides]).astype(jnp.int32)
+    packed = late_rows(scalars, late, k_early, b_early, flag, rest, rest_oth)
     got = lax.all_to_all(packed, "grp", 0, 0).reshape(ao_dev, -1)
     b_all = got[:, :occ]
     k_tile = got[:, occ : occ + 512].astype(jnp.float32) + got[:, occ + 512 :].astype(jnp.float32)

time: 277 us -> 274 us (0.989)
  starting transfers between devices: 74.1 us -> 67.7 us
  other arithmetic: 5.5 us -> 8.98 us
    ppermute x28 -> x26, waiting for transfers between devices: 95.5 us -> 83.4 us  [moved(): return lax.ppermute(x, AXES, pairs)]
    all_to_all x1, waiting for transfers between devices: 10.9 us -> 20.1 us  [on_device(): a_own = lax.all_to_all(a_slice, 'chip', 0, 0).reshape(ao_dev, occ)]
    ppermute x28 -> x26, starting transfers between devices: 38.3 us -> 34.7 us  [moved(): return lax.ppermute(x, AXES, pairs)]
    all_to_all x2, starting transfers between devices: 22 us -> 19.2 us  [exchanged(): return lax.all_to_all(cut.reshape(16, rows, cols), ('grp', 'core'), 0, 0)]
  transfers between devices with their start and end apart: 33 -> 31, of which waited for: 21 -> 18; matrix products, arithmetic and copies ran while one was open for 9% -> 10% of each run, Pallas kernels for 11% -> 11%
where the time goes in v4:
time: 274 us; the launch traced here: 272 us
  waiting for transfers between devices  135 us (49%)
  starting transfers between devices  67.7 us (25%)
  Pallas kernels  33.7 us (12%)
  local copies, waits for them, and re-layouts  14.6 us (5%)
  matrix products  11.5 us (4%)
  other arithmetic  8.98 us (3%)
    ppermute x26, waiting for transfers between devices, moved(): return lax.ppermute(x, AXES, pairs)  83.4 us
    ppermute x26, starting transfers between devices, moved(): return lax.ppermute(x, AXES, pairs)  34.7 us
    pallas_call x2, Pallas kernels, pair_tiles(): pl.pallas_call(tiles_kernel, out_shape=out, grid_spec=pltpu.PrefetchScala...  20.4 us
    all_to_all x1, waiting for transfers between devices, on_device(): a_own = lax.all_to_all(a_slice, 'chip', 0, 0).reshape(ao_dev, occ)  20.1 us
    all_to_all x2, starting transfers between devices, exchanged(): return lax.all_to_all(cut.reshape(16, rows, cols), ('grp', 'core'), 0, 0)  19.2 us
    all_to_all x2, waiting for transfers between devices, exchanged(): return lax.all_to_all(cut.reshape(16, rows, cols), ('grp', 'core'), 0, 0)  16.8 us
    all_to_all x1, waiting for transfers between devices, on_device(): got = lax.all_to_all(packed, 'grp', 0, 0).reshape(ao_dev, -1)  12.7 us
    dot_general x4, matrix products, product(): jnp.dot(left, right.reshape(-1, occ), preferred_element_type=jnp.float32)  9.33 us
  transfers between devices with their start and end apart: 31, of which 18 were waited for; matrix products, arithmetic and copies ran while one was open for 10% of the time, Pallas kernels for 11%

profile of v4, /device:TPU:7, one launch (start us, length us, event | category | flops | bytes accessed | tf_op | source)
XLA Modules:
  0.0 271.6 jit_solution(16052671221022538331)
XLA Ops:
  0.0 2.7 %collective-permute-start = (bf16[256,1024]{1,0:T(8,128)(2,1)}, bf16[256,1024]{1,0:T(8,128)(2,1)S(1)}, u32[]{:S(2)}, u32[]{:S(2)}) collective-permute-start(bf16[256,1024]{1,0:T(8,128)(2,1)} %param.8), channel_id=1, source_target_pairs={{0,6},{1,7},{2,0},{3,1},{4,2},{5,3},{6,4},{7,5},{8,14},{9,15},{10,... | collective-permute-start | bytes 1572872 | tf_op jit(solution)/shard_map/ppermute | solution.py:25
  10.8 6.9 %masked_columns.1 = (bf16[1024,2048]{1,0:T(8,128)(2,1)S(1)}, bf16[1024,2048]{1,0:T(8,128)(2,1)S(1)}) custom-call(s32[16]{0:T(128)S(1)} %pad_add_fusion.1.cols, f32[8,4096]{1,0:T(8,128)S(1)} %convert_element_type.42.refs_0_.refs_1_, f32[8,4096]{1,0:T(8,128)S(1)} %convert_element_type.42.refs_0_.refs_1_, bf16[4,256,4096]{2,1,0:T(8,128)(2,1)} %refs_3_.1, ...), custom_call_target="tpu_custom_call" | custom-call | tf_op jit(solution)/shard_map/masked_columns/pallas_call | solution.py:100
  21.2 2.7 collective-permute-start.4
  26.9 2.3 collective-permute-done.4
  29.3 4.3 %collective-permute-done.7 = bf16[256,1024]{1,0:T(8,128)(2,1)S(1)} collective-permute-done((bf16[256,1024]{1,0:T(8,128)(2,1)S(1)}, bf16[256,1024]{1,0:T(8,128)(2,1)S(1)}, u32[]{:S(2)}, u32[]{:S(2)}) %collective-permute-start.7) | collective-permute-done | bytes 524320 | tf_op jit(solution)/shard_map/ppermute | solution.py:25
  33.6 3.3 %collective-permute-done.6 = bf16[256,1024]{1,0:T(8,128)(2,1)S(1)} collective-permute-done((bf16[256,1024]{1,0:T(8,128)(2,1)S(1)}, bf16[256,1024]{1,0:T(8,128)(2,1)S(1)}, u32[]{:S(2)}, u32[]{:S(2)}) %collective-permute-start.6) | collective-permute-done | bytes 524320 | tf_op jit(solution)/shard_map/ppermute | solution.py:25
  44.1 3.3 %collective-permute-done.10 = bf16[128,1024]{1,0:T(8,128)(2,1)S(1)} collective-permute-done((bf16[128,1024]{1,0:T(8,128)(2,1)S(1)}, bf16[128,1024]{1,0:T(8,128)(2,1)S(1)}, u32[]{:S(2)}, u32[]{:S(2)}) %collective-permute-start.10) | collective-permute-done | bytes 262176 | tf_op jit(solution)/shard_map/ppermute | solution.py:25
  48.6 2.9 %fusion.2 = f32[1024,1024]{1,0:T(8,128)S(1)} fusion(bf16[1280,1024]{1,0:T(8,128)(2,1)S(1)} %constant_dynamic-update-slice_fusion.3, bf16[1024,2048]{1,0:T(8,128)(2,1)S(1)} %get-tuple-element.36), kind=kOutput, calls=%fused_computation.3 | convolution fusion | flops 2684354560 | bytes 9437184 | tf_op jit(solution)/shard_map/dot_general | solution.py:278
  53.2 2.9 %fusion = f32[1024,1024]{1,0:T(8,128)S(1)} fusion(bf16[1280,1024]{1,0:T(8,128)(2,1)S(1)} %bitcast.44, bf16[1024,2048]{1,0:T(8,128)(2,1)S(1)} %get-tuple-element.44), kind=kOutput, calls=%fused_computation.1 | convolution fusion | flops 2684354560 | bytes 9437184 | tf_op jit(solution)/shard_map/dot_general | solution.py:278
  59.9 2.7 collective-permute-done.13.refs_1_
  64.8 4.0 %all-to-all-start = ((bf16[8,32,1024]{2,1,0:T(8,128)(2,1)}), bf16[8,32,1024]{2,1,0:T(8,128)(2,1)S(1)}, u32[]{:S(2)}, u32[]{:S(2)}) async-start(bf16[8,32,1024]{2,1,0:T(8,128)(2,1)} %bitcast.7), calls=%async_computation | async-start | bytes 1048576 | tf_op jit(solution)/shard_map/all_to_all | solution.py:317
  68.8 37.0 %collective-permute-done.14.refs_3_ = bf16[4,256,1024]{2,1,0:T(8,128)(2,1)} collective-permute-done((bf16[4,256,1024]{2,1,0:T(8,128)(2,1)}, bf16[4,256,1024]{2,1,0:T(8,128)(2,1)}, u32[]{:S(2)}, u32[]{:S(2)}) %collective-permute-start.14) | collective-permute-done | bytes 2097184 | tf_op jit(solution)/shard_map/ppermute | solution.py:25
  107.1 2.7 %collective-permute-start.15 = (bf16[2,256,1024]{2,1,0:T(8,128)(2,1)S(1)}, bf16[2,256,1024]{2,1,0:T(8,128)(2,1)}, u32[]{:S(2)}, u32[]{:S(2)}) collective-permute-start(bf16[2,256,1024]{2,1,0:T(8,128)(2,1)S(1)} %slice.98), channel_id=1, source_target_pairs={{0,6},{1,7},{2,0},{3,1},{4,2},{5,3},{6,4},{7,5},{8,14},{9,15},{10,... | collective-permute-start | bytes 3145736 | tf_op jit(solution)/shard_map/ppermute | solution.py:25
  113.9 4.4 %all-to-all-start.1 = ((bf16[8,32,1024]{2,1,0:T(8,128)(2,1)}), bf16[8,32,1024]{2,1,0:T(8,128)(2,1)S(1)}, u32[]{:S(2)}, u32[]{:S(2)}) async-start(bf16[8,32,1024]{2,1,0:T(8,128)(2,1)} %broadcast_in_dim.13), calls=%async_computation.1 | async-start | bytes 1048576 | tf_op jit(solution)/shard_map/all_to_all | solution.py:320
  118.3 20.1 %all-to-all-done.1 = bf16[8,32,1024]{2,1,0:T(8,128)(2,1)S(1)} async-done(((bf16[8,32,1024]{2,1,0:T(8,128)(2,1)}), bf16[8,32,1024]{2,1,0:T(8,128)(2,1)S(1)}, u32[]{:S(2)}, u32[]{:S(2)}) %all-to-all-start.1) | async-done | bytes 524320 | tf_op jit(solution)/shard_map/all_to_all | solution.py:320
  138.3 3.5 %collective-permute-start.21 = (bf16[4,256,1024]{2,1,0:T(8,128)(2,1)}, bf16[4,256,1024]{2,1,0:T(8,128)(2,1)}, u32[]{:S(2)}, u32[]{:S(2)}) collective-permute-start(bf16[4,256,1024]{2,1,0:T(8,128)(2,1)} %collective-permute-done.18.refs_5_), channel_id=1, source_target_pairs={{0,6},{1,7},{2,0},{3,1},{4,2},{5,3},{6,4},{7,5},{8,14},{9,15},{10,... | collective-permute-start | bytes 6291464 | tf_op jit(solution)/shard_map/ppermute | solution.py:25
  143.3 11.9 %exchange_tiles.3 = bf16[8,2,32,1280]{3,2,1,0:T(8,128)(2,1)} custom-call(s32[1]{0:T(128)} %bitcast.core_ref, bf16[4,256,1024]{2,1,0:T(8,128)(2,1)} %bitcast.6.refs_0_.refs_2_, bf16[4,256,1024]{2,1,0:T(8,128)(2,1)} %collective-permute-done.13.refs_1_, bf16[4,256,1024]{2,1,0:T(8,128)(2,1)} %bitcast.6.refs_0_.refs_2_, ...), custom_call_target="tpu_custom_call" | custom-call | flops 5368709120 | bytes 15990784 | tf_op jit(solution)/shard_map/exchange_tiles/pallas_call | solution.py:141
  155.3 12.3 %all-to-all-start.3 = ((bf16[16,32,1280]{2,1,0:T(8,128)(2,1)}), bf16[16,32,1280]{2,1,0:T(8,128)(2,1)S(1)}, u32[]{:S(2)}, u32[]{:S(2)}) async-start(bf16[16,32,1280]{2,1,0:T(8,128)(2,1)} %bitcast.48), calls=%async_computation.3 | async-start | bytes 2621440 | tf_op jit(solution)/shard_map/all_to_all | solution.py:162
  167.6 17.9 %collective-permute-done.20.refs_3_ = bf16[2,256,1024]{2,1,0:T(8,128)(2,1)} collective-permute-done((bf16[2,256,1024]{2,1,0:T(8,128)(2,1)}, bf16[2,256,1024]{2,1,0:T(8,128)(2,1)}, u32[]{:S(2)}, u32[]{:S(2)}) %collective-permute-start.20) | collective-permute-done | bytes 1048608 | tf_op jit(solution)/shard_map/ppermute | solution.py:25
  185.6 3.1 %collective-permute-done.22.refs_5_ = bf16[4,256,1024]{2,1,0:T(8,128)(2,1)} collective-permute-done((bf16[4,256,1024]{2,1,0:T(8,128)(2,1)}, bf16[4,256,1024]{2,1,0:T(8,128)(2,1)}, u32[]{:S(2)}, u32[]{:S(2)}) %collective-permute-start.22) | collective-permute-done | bytes 2097184 | tf_op jit(solution)/shard_map/ppermute | solution.py:25
  188.6 8.4 %exchange_tiles.2 = bf16[8,2,32,768]{3,2,1,0:T(8,128)(2,1)} custom-call(s32[1]{0:T(128)} %bitcast.core_ref, bf16[4,256,1024]{2,1,0:T(8,128)(2,1)} %bitcast.6.refs_0_.refs_2_, bf16[4,256,1024]{2,1,0:T(8,128)(2,1)} %collective-permute-done.13.refs_1_, bf16[2,256,1024]{2,1,0:T(8,128)(2,1)} %collective-permute-done.19.refs_2_, ...), custom_call_target="tpu_custom_call" | custom-call | flops 3221225472 | bytes 11272192 | tf_op jit(solution)/shard_map/exchange_tiles/pallas_call | solution.py:141
  197.1 9.3 %all-to-all-done.3.got = bf16[16,32,1280]{2,1,0:T(8,128)(2,1)S(1)} async-done(((bf16[16,32,1280]{2,1,0:T(8,128)(2,1)}), bf16[16,32,1280]{2,1,0:T(8,128)(2,1)S(1)}, u32[]{:S(2)}, u32[]{:S(2)}) %all-to-all-start.3) | async-done | bytes 1310752 | tf_op jit(solution)/shard_map/all_to_all | solution.py:162
  206.4 6.9 %all-to-all-start.2 = ((bf16[16,32,768]{2,1,0:T(8,128)(2,1)}), bf16[16,32,768]{2,1,0:T(8,128)(2,1)S(1)}, u32[]{:S(2)}, u32[]{:S(2)}) async-start(bf16[16,32,768]{2,1,0:T(8,128)(2,1)} %bitcast.49), calls=%async_computation.2 | async-start | bytes 1572864 | tf_op jit(solution)/shard_map/all_to_all | solution.py:162
  215.9 2.4 early_rows.1
  218.3 7.5 %all-to-all-done.2.got = bf16[16,32,768]{2,1,0:T(8,128)(2,1)S(1)} async-done(((bf16[16,32,768]{2,1,0:T(8,128)(2,1)}), bf16[16,32,768]{2,1,0:T(8,128)(2,1)S(1)}, u32[]{:S(2)}, u32[]{:S(2)}) %all-to-all-start.2) | async-done | bytes 786464 | tf_op jit(solution)/shard_map/all_to_all | solution.py:162
  227.5 4.0 %late_rows.1 = bf16[8,32,2048]{2,1,0:T(8,128)(2,1)} custom-call(s32[9]{0:T(128)S(1)} %pad_add_fusion.scalars, bf16[16,32,768]{2,1,0:T(8,128)(2,1)S(1)} %all-to-all-done.2.got, f32[2,32,1280]{2,1,0:T(8,128)S(1)} %get-tuple-element.56.k_early, f32[32,1024]{1,0:T(8,128)S(1)} %get-tuple-element.57.b_early, f32[1,1024]{1,0:T(1,128)S(1)} %bitcast.40, ...), custom_call_target="tpu_custom_call" | custom-call | flops 100663296 | bytes 8388608 | tf_op jit(solution)/shard_map/late_rows/pallas_call | solution.py:223
  231.5 5.4 %all-to-all-start.4 = ((bf16[8,32,2048]{2,1,0:T(8,128)(2,1)}), bf16[8,32,2048]{2,1,0:T(8,128)(2,1)S(1)}, u32[]{:S(2)}, u32[]{:S(2)}) async-start(bf16[8,32,2048]{2,1,0:T(8,128)(2,1)} %late_rows.1), calls=%async_computation.4 | async-start | bytes 2097152 | tf_op jit(solution)/shard_map/all_to_all | solution.py:332
  238.1 12.7 %all-to-all-done.4 = bf16[8,32,2048]{2,1,0:T(8,128)(2,1)S(1)} async-done(((bf16[8,32,2048]{2,1,0:T(8,128)(2,1)}), bf16[8,32,2048]{2,1,0:T(8,128)(2,1)S(1)}, u32[]{:S(2)}, u32[]{:S(2)}) %all-to-all-start.4) | async-done | bytes 1048608 | tf_op jit(solution)/shard_map/all_to_all | solution.py:332
  251.7 4.3 %collective-permute-start.25 = (bf16[256,256]{1,0:T(8,128)(2,1)S(1)}, bf16[256,256]{1,0:T(8,128)(2,1)S(1)}, u32[]{:S(2)}, u32[]{:S(2)}) collective-permute-start(bf16[256,256]{1,0:T(8,128)(2,1)S(1)} %copy.15), channel_id=1, source_target_pairs={{0,1},{1,0},{2,17},{3,16},{4,33},{5,32},{6,49},{7,48},{8,65},{9,64... | collective-permute-start | bytes 393224 | tf_op jit(solution)/shard_map/ppermute | solution.py:25
  256.1 5.4 %collective-permute-start.23 = (bf16[256,256]{1,0:T(8,128)(2,1)S(1)}, bf16[256,256]{1,0:T(8,128)(2,1)S(1)}, u32[]{:S(2)}, u32[]{:S(2)}) collective-permute-start(bf16[256,256]{1,0:T(8,128)(2,1)S(1)} %copy.14), channel_id=1, source_target_pairs={{0,0},{1,1},{2,16},{3,17},{4,32},{5,33},{6,48},{7,49},{8,64},{9,65... | collective-permute-start | bytes 393224 | tf_op jit(solution)/shard_map/ppermute | solution.py:25
  261.8 3.6 %collective-permute-done.25 = bf16[256,256]{1,0:T(8,128)(2,1)S(1)} collective-permute-done((bf16[256,256]{1,0:T(8,128)(2,1)S(1)}, bf16[256,256]{1,0:T(8,128)(2,1)S(1)}, u32[]{:S(2)}, u32[]{:S(2)}) %collective-permute-start.25) | collective-permute-done | bytes 131104 | tf_op jit(solution)/shard_map/ppermute | solution.py:25
  265.5 5.0 %collective-permute-done.23 = bf16[256,256]{1,0:T(8,128)(2,1)S(1)} collective-permute-done((bf16[256,256]{1,0:T(8,128)(2,1)S(1)}, bf16[256,256]{1,0:T(8,128)(2,1)S(1)}, u32[]{:S(2)}, u32[]{:S(2)}) %collective-permute-start.23) | collective-permute-done | bytes 131104 | tf_op jit(solution)/shard_map/ppermute | solution.py:25
  (113 shorter events, 45.2 us)
Async XLA Ops:
  0.0 17.8 %collective-permute-start = (bf16[256,1024]{1,0:T(8,128)(2,1)}, bf16[256,1024]{1,0:T(8,128)(2,1)S(1)}, u32[]{:S(2)}, u32[]{:S(2)}) collective-permute-start(bf16[256,1024]{1,0:T(8,128)(2,1)} %param.8), channel_id=1, source_target_pairs={{0,6},{1,7},{2,0},{3,1},{4,2},{5,3},{6,4},{7,5},{8,14},{9,15},{10,... | collective-permute-start | bytes 1572872 | tf_op jit(solution)/shard_map/ppermute | solution.py:25
  2.7 15.1 %collective-permute-start.1 = (bf16[256,1024]{1,0:T(8,128)(2,1)}, bf16[256,1024]{1,0:T(8,128)(2,1)}, u32[]{:S(2)}, u32[]{:S(2)}) collective-permute-start(bf16[256,1024]{1,0:T(8,128)(2,1)} %param.8), channel_id=1, source_target_pairs={{0,2},{1,3},{2,4},{3,5},{4,6},{5,7},{6,0},{7,1},{8,10},{9,11},{10,... | collective-permute-start | bytes 1572872 | tf_op jit(solution)/shard_map/ppermute | solution.py:25
  4.6 13.2 %collective-permute-start.2 = (bf16[128,1024]{1,0:T(8,128)(2,1)}, bf16[128,1024]{1,0:T(8,128)(2,1)}, u32[]{:S(2)}, u32[]{:S(2)}) collective-permute-start(bf16[128,1024]{1,0:T(8,128)(2,1)} %get-tuple-element.70), channel_id=1, source_target_pairs={{0,8},{1,9},{2,10},{3,11},{4,12},{5,13},{6,14},{7,15},{8,0},{9,1},... | collective-permute-start | bytes 786440 | tf_op jit(solution)/shard_map/ppermute | solution.py:25
  5.2 12.6 %collective-permute-start.3 = (bf16[128,1024]{1,0:T(8,128)(2,1)}, bf16[128,1024]{1,0:T(8,128)(2,1)}, u32[]{:S(2)}, u32[]{:S(2)}) collective-permute-start(bf16[128,1024]{1,0:T(8,128)(2,1)} %get-tuple-element.69), channel_id=1, source_target_pairs={{0,24},{1,25},{2,26},{3,27},{4,28},{5,29},{6,30},{7,31},{8,16},{9,... | collective-permute-start | bytes 786440 | tf_op jit(solution)/shard_map/ppermute | solution.py:25
  8.7 28.2 %collective-permute-start.8 = (f32[256,1024]{1,0:T(8,128)}, f32[256,1024]{1,0:T(8,128)}, u32[]{:S(2)}, u32[]{:S(2)}) collective-permute-start(f32[256,1024]{1,0:T(8,128)} %slice_select_fusion), channel_id=1, source_target_pairs={{0,1},{1,0},{2,3},{3,2},{4,5},{5,4},{6,7},{7,6},{8,9},{9,8},{10,11... | collective-permute-start | bytes 3145736 | tf_op jit(solution)/shard_map/ppermute | solution.py:25
  18.9 10.3 %collective-permute-start.5 = (bf16[128,1024]{1,0:T(8,128)(2,1)S(1)}, bf16[128,1024]{1,0:T(8,128)(2,1)S(1)}, u32[]{:S(2)}, u32[]{:S(2)}) collective-permute-start(bf16[128,1024]{1,0:T(8,128)(2,1)S(1)} %get-tuple-element.68), channel_id=1, source_target_pairs={{0,2},{1,3},{2,4},{3,5},{4,6},{5,7},{6,0},{7,1},{8,10},{9,11},{10,... | collective-permute-start | bytes 786440 | tf_op jit(solution)/shard_map/ppermute | solution.py:25
  19.3 14.3 %collective-permute-start.7 = (bf16[256,1024]{1,0:T(8,128)(2,1)S(1)}, bf16[256,1024]{1,0:T(8,128)(2,1)S(1)}, u32[]{:S(2)}, u32[]{:S(2)}) collective-permute-start(bf16[256,1024]{1,0:T(8,128)(2,1)S(1)} %pad_maximum_fusion.2), channel_id=1, source_target_pairs={{0,24},{1,25},{2,26},{3,27},{4,28},{5,29},{6,30},{7,31},{8,16},{9,... | collective-permute-start | bytes 1572872 | tf_op jit(solution)/shard_map/ppermute | solution.py:25
  21.2 8.0 %collective-permute-start.4 = (bf16[128,1024]{1,0:T(8,128)(2,1)S(1)}, bf16[128,1024]{1,0:T(8,128)(2,1)S(1)}, u32[]{:S(2)}, u32[]{:S(2)}) collective-permute-start(bf16[128,1024]{1,0:T(8,128)(2,1)S(1)} %get-tuple-element.66), channel_id=1, source_target_pairs={{0,6},{1,7},{2,0},{3,1},{4,2},{5,3},{6,4},{7,5},{8,14},{9,15},{10,... | collective-permute-start | bytes 786440 | tf_op jit(solution)/shard_map/ppermute | solution.py:25
  23.9 13.0 %collective-permute-start.6 = (bf16[256,1024]{1,0:T(8,128)(2,1)S(1)}, bf16[256,1024]{1,0:T(8,128)(2,1)S(1)}, u32[]{:S(2)}, u32[]{:S(2)}) collective-permute-start(bf16[256,1024]{1,0:T(8,128)(2,1)S(1)} %pad_maximum_fusion.1), channel_id=1, source_target_pairs={{0,8},{1,9},{2,10},{3,11},{4,12},{5,13},{6,14},{7,15},{8,0},{9,1},... | collective-permute-start | bytes 1572872 | tf_op jit(solution)/shard_map/ppermute | solution.py:25
  36.9 4.5 %collective-permute-start.11 = (bf16[3,256,1024]{2,1,0:T(8,128)(2,1)S(1)}, bf16[3,256,1024]{2,1,0:T(8,128)(2,1)S(1)}, u32[]{:S(2)}, u32[]{:S(2)}) collective-permute-start(bf16[3,256,1024]{2,1,0:T(8,128)(2,1)S(1)} %bitcast.38), channel_id=1, source_target_pairs={{0,1},{1,0},{2,3},{3,2},{4,5},{5,4},{6,7},{7,6},{8,9},{9,8},{10,11... | collective-permute-start | bytes 4718600 | tf_op jit(solution)/shard_map/ppermute | solution.py:25
  38.4 9.1 %collective-permute-start.10 = (bf16[128,1024]{1,0:T(8,128)(2,1)S(1)}, bf16[128,1024]{1,0:T(8,128)(2,1)S(1)}, u32[]{:S(2)}, u32[]{:S(2)}) collective-permute-start(bf16[128,1024]{1,0:T(8,128)(2,1)S(1)} %collective-permute-done.5), channel_id=1, source_target_pairs={{0,24},{1,25},{2,26},{3,27},{4,28},{5,29},{6,30},{7,31},{8,16},{9,... | collective-permute-start | bytes 786440 | tf_op jit(solution)/shard_map/ppermute | solution.py:25
  39.2 8.2 %collective-permute-start.9 = (bf16[128,1024]{1,0:T(8,128)(2,1)S(1)}, bf16[128,1024]{1,0:T(8,128)(2,1)S(1)}, u32[]{:S(2)}, u32[]{:S(2)}) collective-permute-start(bf16[128,1024]{1,0:T(8,128)(2,1)S(1)} %collective-permute-done.4), channel_id=1, source_target_pairs={{0,8},{1,9},{2,10},{3,11},{4,12},{5,13},{6,14},{7,15},{8,0},{9,1},... | collective-permute-start | bytes 786440 | tf_op jit(solution)/shard_map/ppermute | solution.py:25
  47.5 5.7 %collective-permute-start.12 = (bf16[5,256,1024]{2,1,0:T(8,128)(2,1)S(1)}, bf16[5,256,1024]{2,1,0:T(8,128)(2,1)S(1)}, u32[]{:S(2)}, u32[]{:S(2)}) collective-permute-start(bf16[5,256,1024]{2,1,0:T(8,128)(2,1)S(1)} %bitcast.36), channel_id=1, source_target_pairs={{0,1},{1,0},{2,3},{3,2},{4,5},{5,4},{6,7},{7,6},{8,9},{9,8},{10,11... | collective-permute-start | bytes 7864328 | tf_op jit(solution)/shard_map/ppermute | solution.py:25
  58.1 4.5 %collective-permute-start.13 = (bf16[4,256,1024]{2,1,0:T(8,128)(2,1)}, bf16[4,256,1024]{2,1,0:T(8,128)(2,1)}, u32[]{:S(2)}, u32[]{:S(2)}) collective-permute-start(bf16[4,256,1024]{2,1,0:T(8,128)(2,1)} %bitcast.6.refs_0_.refs_2_), channel_id=1, source_target_pairs={{0,1},{1,0},{2,3},{3,2},{4,5},{5,4},{6,7},{7,6},{8,9},{9,8},{10,11... | collective-permute-start | bytes 6291464 | tf_op jit(solution)/shard_map/ppermute | solution.py:25
  58.4 47.4 %collective-permute-start.14 = (bf16[4,256,1024]{2,1,0:T(8,128)(2,1)}, bf16[4,256,1024]{2,1,0:T(8,128)(2,1)}, u32[]{:S(2)}, u32[]{:S(2)}) collective-permute-start(bf16[4,256,1024]{2,1,0:T(8,128)(2,1)} %bitcast.6.refs_0_.refs_2_), channel_id=1, source_target_pairs={{0,6},{1,7},{2,0},{3,1},{4,2},{5,3},{6,4},{7,5},{8,14},{9,15},{10,... | collective-permute-start | bytes 6291464 | tf_op jit(solution)/shard_map/ppermute | solution.py:25
  59.9 50.0 %collective-permute-start.16 = (bf16[4,256,1024]{2,1,0:T(8,128)(2,1)}, bf16[4,256,1024]{2,1,0:T(8,128)(2,1)}, u32[]{:S(2)}, u32[]{:S(2)}) collective-permute-start(bf16[4,256,1024]{2,1,0:T(8,128)(2,1)} %bitcast.6.refs_0_.refs_2_), channel_id=1, source_target_pairs={{0,2},{1,3},{2,4},{3,5},{4,6},{5,7},{6,0},{7,1},{8,10},{9,11},{10,... | collective-permute-start | bytes 6291464 | tf_op jit(solution)/shard_map/ppermute | solution.py:25
  59.9 58.4 %collective-permute-start.18 = (bf16[4,256,1024]{2,1,0:T(8,128)(2,1)}, bf16[4,256,1024]{2,1,0:T(8,128)(2,1)}, u32[]{:S(2)}, u32[]{:S(2)}) collective-permute-start(bf16[4,256,1024]{2,1,0:T(8,128)(2,1)} %bitcast.6.refs_0_.refs_2_), channel_id=1, source_target_pairs={{0,8},{1,9},{2,10},{3,11},{4,12},{5,13},{6,14},{7,15},{8,0},{9,1},... | collective-permute-start | bytes 6291464 | tf_op jit(solution)/shard_map/ppermute | solution.py:25
  64.8 46.5 %copy-start.10 = (s32[1024]{0:T(1024)S(1)}, s32[1024]{0:T(1024)}, u32[]{:S(2)}) copy-start(s32[1024]{0:T(1024)} %param.10) | copy-start | bytes 12292
  64.8 48.1 %all-to-all-start = ((bf16[8,32,1024]{2,1,0:T(8,128)(2,1)}), bf16[8,32,1024]{2,1,0:T(8,128)(2,1)S(1)}, u32[]{:S(2)}, u32[]{:S(2)}) async-start(bf16[8,32,1024]{2,1,0:T(8,128)(2,1)} %bitcast.7), calls=%async_computation | async-start | bytes 1048576 | tf_op jit(solution)/shard_map/all_to_all | solution.py:317
  107.1 31.2 %collective-permute-start.15 = (bf16[2,256,1024]{2,1,0:T(8,128)(2,1)S(1)}, bf16[2,256,1024]{2,1,0:T(8,128)(2,1)}, u32[]{:S(2)}, u32[]{:S(2)}) collective-permute-start(bf16[2,256,1024]{2,1,0:T(8,128)(2,1)S(1)} %slice.98), channel_id=1, source_target_pairs={{0,6},{1,7},{2,0},{3,1},{4,2},{5,3},{6,4},{7,5},{8,14},{9,15},{10,... | collective-permute-start | bytes 3145736 | tf_op jit(solution)/shard_map/ppermute | solution.py:25
  111.2 27.2 %collective-permute-start.17 = (bf16[2,256,1024]{2,1,0:T(8,128)(2,1)S(1)}, bf16[2,256,1024]{2,1,0:T(8,128)(2,1)}, u32[]{:S(2)}, u32[]{:S(2)}) collective-permute-start(bf16[2,256,1024]{2,1,0:T(8,128)(2,1)S(1)} %slice.99), channel_id=1, source_target_pairs={{0,2},{1,3},{2,4},{3,5},{4,6},{5,7},{6,0},{7,1},{8,10},{9,11},{10,... | collective-permute-start | bytes 3145736 | tf_op jit(solution)/shard_map/ppermute | solution.py:25
  113.9 24.4 %all-to-all-start.1 = ((bf16[8,32,1024]{2,1,0:T(8,128)(2,1)}), bf16[8,32,1024]{2,1,0:T(8,128)(2,1)S(1)}, u32[]{:S(2)}, u32[]{:S(2)}) async-start(bf16[8,32,1024]{2,1,0:T(8,128)(2,1)} %broadcast_in_dim.13), calls=%async_computation.1 | async-start | bytes 1048576 | tf_op jit(solution)/shard_map/all_to_all | solution.py:320
  138.3 47.2 %collective-permute-start.21 = (bf16[4,256,1024]{2,1,0:T(8,128)(2,1)}, bf16[4,256,1024]{2,1,0:T(8,128)(2,1)}, u32[]{:S(2)}, u32[]{:S(2)}) collective-permute-start(bf16[4,256,1024]{2,1,0:T(8,128)(2,1)} %collective-permute-done.18.refs_5_), channel_id=1, source_target_pairs={{0,6},{1,7},{2,0},{3,1},{4,2},{5,3},{6,4},{7,5},{8,14},{9,15},{10,... | collective-permute-start | bytes 6291464 | tf_op jit(solution)/shard_map/ppermute | solution.py:25
  141.9 46.8 %collective-permute-start.22 = (bf16[4,256,1024]{2,1,0:T(8,128)(2,1)}, bf16[4,256,1024]{2,1,0:T(8,128)(2,1)}, u32[]{:S(2)}, u32[]{:S(2)}) collective-permute-start(bf16[4,256,1024]{2,1,0:T(8,128)(2,1)} %collective-permute-done.18.refs_5_), channel_id=1, source_target_pairs={{0,2},{1,3},{2,4},{3,5},{4,6},{5,7},{6,0},{7,1},{8,10},{9,11},{10,... | collective-permute-start | bytes 6291464 | tf_op jit(solution)/shard_map/ppermute | solution.py:25
  141.9 25.7 %collective-permute-start.19 = (bf16[2,256,1024]{2,1,0:T(8,128)(2,1)}, bf16[2,256,1024]{2,1,0:T(8,128)(2,1)}, u32[]{:S(2)}, u32[]{:S(2)}) collective-permute-start(bf16[2,256,1024]{2,1,0:T(8,128)(2,1)} %collective-permute-done.15.refs_6_), channel_id=1, source_target_pairs={{0,8},{1,9},{2,10},{3,11},{4,12},{5,13},{6,14},{7,15},{8,0},{9,1},... | collective-permute-start | bytes 3145736 | tf_op jit(solution)/shard_map/ppermute | solution.py:25
  141.9 43.6 %collective-permute-start.20 = (bf16[2,256,1024]{2,1,0:T(8,128)(2,1)}, bf16[2,256,1024]{2,1,0:T(8,128)(2,1)}, u32[]{:S(2)}, u32[]{:S(2)}) collective-permute-start(bf16[2,256,1024]{2,1,0:T(8,128)(2,1)} %collective-permute-done.17.refs_7_), channel_id=1, source_target_pairs={{0,8},{1,9},{2,10},{3,11},{4,12},{5,13},{6,14},{7,15},{8,0},{9,1},... | collective-permute-start | bytes 3145736 | tf_op jit(solution)/shard_map/ppermute | solution.py:25
  155.3 51.1 %all-to-all-start.3 = ((bf16[16,32,1280]{2,1,0:T(8,128)(2,1)}), bf16[16,32,1280]{2,1,0:T(8,128)(2,1)S(1)}, u32[]{:S(2)}, u32[]{:S(2)}) async-start(bf16[16,32,1280]{2,1,0:T(8,128)(2,1)} %bitcast.48), calls=%async_computation.3 | async-start | bytes 2621440 | tf_op jit(solution)/shard_map/all_to_all | solution.py:162
  206.4 19.4 %all-to-all-start.2 = ((bf16[16,32,768]{2,1,0:T(8,128)(2,1)}), bf16[16,32,768]{2,1,0:T(8,128)(2,1)S(1)}, u32[]{:S(2)}, u32[]{:S(2)}) async-start(bf16[16,32,768]{2,1,0:T(8,128)(2,1)} %bitcast.49), calls=%async_computation.2 | async-start | bytes 1572864 | tf_op jit(solution)/shard_map/all_to_all | solution.py:162
  231.5 19.3 %all-to-all-start.4 = ((bf16[8,32,2048]{2,1,0:T(8,128)(2,1)}), bf16[8,32,2048]{2,1,0:T(8,128)(2,1)S(1)}, u32[]{:S(2)}, u32[]{:S(2)}) async-start(bf16[8,32,2048]{2,1,0:T(8,128)(2,1)} %late_rows.1), calls=%async_computation.4 | async-start | bytes 2097152 | tf_op jit(solution)/shard_map/all_to_all | solution.py:332
  236.9 14.3 %collective-permute-start.24 = (bf16[256,1024]{1,0:T(8,128)(2,1)S(1)}, bf16[256,1024]{1,0:T(8,128)(2,1)S(1)}, u32[]{:S(2)}, u32[]{:S(2)}) collective-permute-start(bf16[256,1024]{1,0:T(8,128)(2,1)S(1)} %bitcast.45), channel_id=1, source_target_pairs={{0,1},{1,0},{2,3},{3,2},{4,5},{5,4},{6,7},{7,6},{8,9},{9,8},{10,11... | collective-permute-start | bytes 1572872 | tf_op jit(solution)/shard_map/ppermute | solution.py:25
  251.7 13.8 %collective-permute-start.25 = (bf16[256,256]{1,0:T(8,128)(2,1)S(1)}, bf16[256,256]{1,0:T(8,128)(2,1)S(1)}, u32[]{:S(2)}, u32[]{:S(2)}) collective-permute-start(bf16[256,256]{1,0:T(8,128)(2,1)S(1)} %copy.15), channel_id=1, source_target_pairs={{0,1},{1,0},{2,17},{3,16},{4,33},{5,32},{6,49},{7,48},{8,65},{9,64... | collective-permute-start | bytes 393224 | tf_op jit(solution)/shard_map/ppermute | solution.py:25
  256.1 14.4 %collective-permute-start.23 = (bf16[256,256]{1,0:T(8,128)(2,1)S(1)}, bf16[256,256]{1,0:T(8,128)(2,1)S(1)}, u32[]{:S(2)}, u32[]{:S(2)}) collective-permute-start(bf16[256,256]{1,0:T(8,128)(2,1)S(1)} %copy.14), channel_id=1, source_target_pairs={{0,0},{1,1},{2,16},{3,17},{4,32},{5,33},{6,48},{7,49},{8,64},{9,65... | collective-permute-start | bytes 393224 | tf_op jit(solution)/shard_map/ppermute | solution.py:25
  (11 other events, 56.2 us)

commit v5 on v4

--- a/solution.py
+++ b/solution.py
@@ -81,34 +81,36 @@
 
 
 def mask_kernel(cols, *refs):
-    count = len(refs) // 3
-    for at in range(count):
-        refs[2 * count + at][...] = masked_block(refs[at], refs[count + at])
-
-
-def masked_columns(cols, keep, slab, depth, steps):
+    keeps, slabs, outs = refs[:4], refs[4:8], refs[8:]
+    for at in range(4):
+        depth = slabs[at].shape[2]
+        place = slice((at % 2) * depth, (at % 2 + 1) * depth)
+        outs[at // 2][:, place] = masked_block(keeps[at], slabs[at])
+
+
+def masked_columns(cols, keep, slab, depth):
     aux_dev, rows, nao = slab.shape
-    count = nao // (depth * steps)
+    steps = nao // (4 * depth)
+    firsts = [t * 2 * steps + u for t in range(2) for u in range(2)]
     keep_spec = [
-        pl.BlockSpec((keep.shape[0], depth), lambda s, c, t=t: (0, c[t * steps + s]))
-        for t in range(count)
+        pl.BlockSpec((keep.shape[0], depth), lambda s, c, t=t: (0, c[t + 2 * s])) for t in firsts
     ]
     slab_spec = [
-        pl.BlockSpec((aux_dev, rows, depth), lambda s, c, t=t: (0, 0, c[t * steps + s]))
-        for t in range(count)
+        pl.BlockSpec((aux_dev, rows, depth), lambda s, c, t=t: (0, 0, c[t + 2 * s]))
+        for t in firsts
     ]
     return pl.pallas_call(
         mask_kernel,
-        out_shape=[jax.ShapeDtypeStruct((aux_dev * rows, depth * steps), slab.dtype)] * count,
+        out_shape=[jax.ShapeDtypeStruct((aux_dev * rows, nao // 2), slab.dtype)] * 2,
         grid_spec=pltpu.PrefetchScalarGridSpec(
             num_scalar_prefetch=1,
             grid=(steps,),
             in_specs=keep_spec + slab_spec,
-            out_specs=[pl.BlockSpec((aux_dev * rows, depth), lambda s, c: (0, s))] * count,
+            out_specs=[pl.BlockSpec((aux_dev * rows, 2 * depth), lambda s, c: (0, s))] * 2,
         ),
         compiler_params=pltpu.CompilerParams(vmem_limit_bytes=40 << 20),
         name="masked_columns",
-    )(cols, *[keep] * count, *[slab] * count)
+    )(cols, *[keep] * 4, *[slab] * 4)
 
 
 def tiles_kernel(core_ref, *refs):
@@ -262,8 +264,12 @@
     hb = ao_dev // 2
     flag = env_flag.astype(jnp.float32)[None, :]
 
+    group = lax.axis_index("grp")
+    row = (chip * NK + core) * ao_dev + lax.broadcasted_iota(jnp.int32, margin.shape, 0)
+    col = group * 2 * ao_dev + lax.broadcasted_iota(jnp.int32, margin.shape, 1)
+    margin_off = margin - (row == col).astype(margin.dtype)
     a_part = lax.dot_general(
-        margin, orbitals, (((0,), (0,)), ((), ())), preferred_element_type=jnp.float32
+        margin_off, orbitals, (((0,), (0,)), ((), ())), preferred_element_type=jnp.float32
     )
     a_low, a_high = a_part[:ao_dev], a_part[ao_dev:]
     a_send = other_core(jnp.where(core == 0, a_high, a_low))
@@ -271,7 +277,7 @@
     sides = jnp.concatenate([a * NY + order, (1 - a) * NY + order]).astype(jnp.int32)
     cols = jnp.concatenate([sides * NK + core, sides * NK + 1 - core])
     keep = jnp.repeat(block_mask[0], ATILE, axis=1).astype(jnp.float32)
-    own_m, oth_m = masked_columns(cols, keep, slab, ao_dev, NA * NY)
+    own_m, oth_m = masked_columns(cols, keep, slab, ao_dev)
     wide = 3 * ao_dev
 
     def product(left, right):
@@ -315,7 +321,10 @@
     a_part = jnp.where(core == 0, a_low, a_high) + a_send
     a_part = a_part.astype(jnp.bfloat16).reshape(8, 32, occ)
     a_got = lax.all_to_all(a_part, "chip", 0, 0)
-    a_slice = (a_got.astype(jnp.float32).sum(0) * flag).astype(jnp.bfloat16)
+    hit = (sides == group).astype(jnp.float32)[:, None, None]
+    same = [lax.dynamic_slice_in_dim(t, chip * 32, 32, 1) for t in (near, rest)]
+    same = (jnp.concatenate(same).astype(jnp.float32) * hit).sum(0)
+    a_slice = ((a_got.astype(jnp.float32).sum(0) + same) * flag).astype(jnp.bfloat16)
     a_slice = jnp.broadcast_to(a_slice[None], (8,) + a_slice.shape)
     a_own = lax.all_to_all(a_slice, "chip", 0, 0).reshape(ao_dev, occ)
     f, g = from_next(n[:mid]), from_prev(p[mid:])

time: 274 us -> 274 us (level)
    ppermute x26, waiting for transfers between devices: 83.4 us -> 79.3 us  [moved(): return lax.ppermute(x, AXES, pairs)]
    all_to_all x2, waiting for transfers between devices: 16.8 us -> 20.3 us  [exchanged(): return lax.all_to_all(cut.reshape(16, rows, cols), ('grp', 'core'), 0, 0)]
  transfers between devices with their start and end apart: 31 -> 31, of which waited for: 18 -> 16; matrix products, arithmetic and copies ran while one was open for 10% -> 10% of each run, Pallas kernels for 11% -> 10%
where the time goes in v5:
time: 274 us; the launch traced here: 273 us
  waiting for transfers between devices  134 us (49%)
  starting transfers between devices  68.2 us (25%)
  Pallas kernels  32.2 us (12%)
  local copies, waits for them, and re-layouts  16.3 us (6%)
  matrix products  11.8 us (4%)
  other arithmetic  9.46 us (3%)
    ppermute x26, waiting for transfers between devices, moved(): return lax.ppermute(x, AXES, pairs)  79.3 us
    ppermute x26, starting transfers between devices, moved(): return lax.ppermute(x, AXES, pairs)  32.6 us
    all_to_all x1, waiting for transfers between devices, on_device(): a_own = lax.all_to_all(a_slice, 'chip', 0, 0).reshape(ao_dev, occ)  21.9 us
    all_to_all x2, starting transfers between devices, exchanged(): return lax.all_to_all(cut.reshape(16, rows, cols), ('grp', 'core'), 0, 0)  21.1 us
    pallas_call x2, Pallas kernels, pair_tiles(): pl.pallas_call(tiles_kernel, out_shape=out, grid_spec=pltpu.PrefetchScala...  20.3 us
    all_to_all x2, waiting for transfers between devices, exchanged(): return lax.all_to_all(cut.reshape(16, rows, cols), ('grp', 'core'), 0, 0)  20.3 us
    all_to_all x1, waiting for transfers between devices, on_device(): got = lax.all_to_all(packed, 'grp', 0, 0).reshape(ao_dev, -1)  12.7 us
    dot_general x4, matrix products, product(): jnp.dot(left, right.reshape(-1, occ), preferred_element_type=jnp.float32)  9.37 us
  transfers between devices with their start and end apart: 31, of which 16 were waited for; matrix products, arithmetic and copies ran while one was open for 10% of the time, Pallas kernels for 10%

profile of v5, /device:TPU:7, one launch (start us, length us, event | category | flops | bytes accessed | tf_op | source)
XLA Modules:
  0.0 272.7 jit_solution(6412370709089694607)
XLA Ops:
  0.0 2.7 %collective-permute-start = (bf16[256,1024]{1,0:T(8,128)(2,1)}, bf16[256,1024]{1,0:T(8,128)(2,1)S(1)}, u32[]{:S(2)}, u32[]{:S(2)}) collective-permute-start(bf16[256,1024]{1,0:T(8,128)(2,1)} %param.8), channel_id=1, source_target_pairs={{0,6},{1,7},{2,0},{3,1},{4,2},{5,3},{6,4},{7,5},{8,14},{9,15},{10,... | collective-permute-start | bytes 1572872 | tf_op jit(solution)/shard_map/ppermute | solution.py:25
  11.6 5.2 %masked_columns.1 = (bf16[1024,2048]{1,0:T(8,128)(2,1)S(1)}, bf16[1024,2048]{1,0:T(8,128)(2,1)S(1)}) custom-call(s32[16]{0:T(128)S(1)} %pad_add_fusion.2.cols, f32[8,4096]{1,0:T(8,128)S(1)} %convert_element_type.55.refs_0_.refs_1_.refs_2_.refs_3_, f32[8,4096]{1,0:T(8,128)S(1)} %convert_element_type.55.refs_0_.refs_1_.refs_2_.refs_3_, ...), custom_call_target="tpu_custom_call" | custom-call | tf_op jit(solution)/shard_map/masked_columns/pallas_call | solution.py:102
  19.3 2.7 collective-permute-start.4
  24.0 3.3 %collective-permute-done.4 = bf16[128,1024]{1,0:T(8,128)(2,1)S(1)} collective-permute-done((bf16[128,1024]{1,0:T(8,128)(2,1)S(1)}, bf16[128,1024]{1,0:T(8,128)(2,1)S(1)}, u32[]{:S(2)}, u32[]{:S(2)}) %collective-permute-start.4) | collective-permute-done | bytes 262176 | tf_op jit(solution)/shard_map/ppermute | solution.py:25
  27.3 3.5 %collective-permute-done.7 = bf16[256,1024]{1,0:T(8,128)(2,1)S(1)} collective-permute-done((bf16[256,1024]{1,0:T(8,128)(2,1)S(1)}, bf16[256,1024]{1,0:T(8,128)(2,1)S(1)}, u32[]{:S(2)}, u32[]{:S(2)}) %collective-permute-start.7) | collective-permute-done | bytes 524320 | tf_op jit(solution)/shard_map/ppermute | solution.py:25
  30.8 4.2 %collective-permute-done.6 = bf16[256,1024]{1,0:T(8,128)(2,1)S(1)} collective-permute-done((bf16[256,1024]{1,0:T(8,128)(2,1)S(1)}, bf16[256,1024]{1,0:T(8,128)(2,1)S(1)}, u32[]{:S(2)}, u32[]{:S(2)}) %collective-permute-start.6) | collective-permute-done | bytes 524320 | tf_op jit(solution)/shard_map/ppermute | solution.py:25
  46.7 2.9 %fusion.2 = f32[1024,1024]{1,0:T(8,128)S(1)} fusion(bf16[1280,1024]{1,0:T(8,128)(2,1)S(1)} %constant_dynamic-update-slice_fusion.3, bf16[1024,2048]{1,0:T(8,128)(2,1)S(1)} %get-tuple-element.36), kind=kOutput, calls=%fused_computation.3 | convolution fusion | flops 2684354560 | bytes 9437184 | tf_op jit(solution)/shard_map/dot_general | solution.py:284
  51.2 2.9 %fusion = f32[1024,1024]{1,0:T(8,128)S(1)} fusion(bf16[1280,1024]{1,0:T(8,128)(2,1)S(1)} %bitcast.45, bf16[1024,2048]{1,0:T(8,128)(2,1)S(1)} %get-tuple-element.44), kind=kOutput, calls=%fused_computation.1 | convolution fusion | flops 2684354560 | bytes 9437184 | tf_op jit(solution)/shard_map/dot_general | solution.py:284
  58.1 2.5 collective-permute-done.13.refs_1_
  60.6 3.0 %add_convert_fusion.1 = bf16[256,1024]{1,0:T(8,128)(2,1)} fusion(f32[256,1024]{1,0:T(8,128)} %collective-permute-done.8, f32[512,1024]{1,0:T(8,128)S(1)} %copy-done.5, pred[]{:T(512)S(6)} %eq.23), kind=kLoop, calls=%fused_computation.12 | loop fusion | flops 786432 | bytes 3670017 | tf_op jit(solution)/shard_map/convert_element_type | solution.py:322
  63.6 3.9 %all-to-all-start = ((bf16[8,32,1024]{2,1,0:T(8,128)(2,1)}), bf16[8,32,1024]{2,1,0:T(8,128)(2,1)S(1)}, u32[]{:S(2)}, u32[]{:S(2)}) async-start(bf16[8,32,1024]{2,1,0:T(8,128)(2,1)} %bitcast.48), calls=%async_computation | async-start | bytes 1048576 | tf_op jit(solution)/shard_map/all_to_all | solution.py:323
  68.5 35.6 %collective-permute-done.14.refs_3_ = bf16[4,256,1024]{2,1,0:T(8,128)(2,1)} collective-permute-done((bf16[4,256,1024]{2,1,0:T(8,128)(2,1)}, bf16[4,256,1024]{2,1,0:T(8,128)(2,1)}, u32[]{:S(2)}, u32[]{:S(2)}) %collective-permute-start.14) | collective-permute-done | bytes 2097184 | tf_op jit(solution)/shard_map/ppermute | solution.py:25
  104.0 2.3 slice.98
  106.3 2.6 collective-permute-start.15
  108.9 2.4 slice.99
  112.5 5.1 %all-to-all-start.1 = ((bf16[8,32,1024]{2,1,0:T(8,128)(2,1)}), bf16[8,32,1024]{2,1,0:T(8,128)(2,1)S(1)}, u32[]{:S(2)}, u32[]{:S(2)}) async-start(bf16[8,32,1024]{2,1,0:T(8,128)(2,1)} %broadcast_in_dim.14), calls=%async_computation.1 | async-start | bytes 1048576 | tf_op jit(solution)/shard_map/all_to_all | solution.py:329
  117.6 21.9 %all-to-all-done.1 = bf16[8,32,1024]{2,1,0:T(8,128)(2,1)S(1)} async-done(((bf16[8,32,1024]{2,1,0:T(8,128)(2,1)}), bf16[8,32,1024]{2,1,0:T(8,128)(2,1)S(1)}, u32[]{:S(2)}, u32[]{:S(2)}) %all-to-all-start.1) | async-done | bytes 524320 | tf_op jit(solution)/shard_map/all_to_all | solution.py:329
  142.5 11.9 %exchange_tiles.3 = bf16[8,2,32,1280]{3,2,1,0:T(8,128)(2,1)} custom-call(s32[1]{0:T(128)} %bitcast.core_ref, bf16[4,256,1024]{2,1,0:T(8,128)(2,1)} %bitcast.6.refs_0_.refs_2_, bf16[4,256,1024]{2,1,0:T(8,128)(2,1)} %copy-done.17, bf16[4,256,1024]{2,1,0:T(8,128)(2,1)} %bitcast.6.refs_0_.refs_2_, bf16[4,256,1024]{2,1,0:T(8,128)(2,1)} %collective-permute-done.14.refs_3_, ...), custom_call_target="tpu_custom_call" | custom-call | flops 5368709120 | bytes 15990784 | tf_op jit(solution)/shard_map/exchange_tiles/pallas_call | solution.py:143
  154.4 13.4 %all-to-all-start.3 = ((bf16[16,32,1280]{2,1,0:T(8,128)(2,1)}), bf16[16,32,1280]{2,1,0:T(8,128)(2,1)S(1)}, u32[]{:S(2)}, u32[]{:S(2)}) async-start(bf16[16,32,1280]{2,1,0:T(8,128)(2,1)} %bitcast.50), calls=%async_computation.3 | async-start | bytes 2621440 | tf_op jit(solution)/shard_map/all_to_all | solution.py:164
  167.9 15.6 %collective-permute-done.20.refs_3_ = bf16[2,256,1024]{2,1,0:T(8,128)(2,1)} collective-permute-done((bf16[2,256,1024]{2,1,0:T(8,128)(2,1)}, bf16[2,256,1024]{2,1,0:T(8,128)(2,1)}, u32[]{:S(2)}, u32[]{:S(2)}) %collective-permute-start.20) | collective-permute-done | bytes 1048608 | tf_op jit(solution)/shard_map/ppermute | solution.py:25
  184.5 8.4 %exchange_tiles.2 = bf16[8,2,32,768]{3,2,1,0:T(8,128)(2,1)} custom-call(s32[1]{0:T(128)} %bitcast.core_ref, bf16[4,256,1024]{2,1,0:T(8,128)(2,1)} %bitcast.6.refs_0_.refs_2_, bf16[4,256,1024]{2,1,0:T(8,128)(2,1)} %copy-done.17, bf16[2,256,1024]{2,1,0:T(8,128)(2,1)} %copy-done.18, bf16[2,256,1024]{2,1,0:T(8,128)(2,1)} %collective-permute-done.20.refs_3_, ...), custom_call_target="tpu_custom_call" | custom-call | flops 3221225472 | bytes 11272192 | tf_op jit(solution)/shard_map/exchange_tiles/pallas_call | solution.py:143
  192.9 12.6 %all-to-all-done.3.got = bf16[16,32,1280]{2,1,0:T(8,128)(2,1)S(1)} async-done(((bf16[16,32,1280]{2,1,0:T(8,128)(2,1)}), bf16[16,32,1280]{2,1,0:T(8,128)(2,1)S(1)}, u32[]{:S(2)}, u32[]{:S(2)}) %all-to-all-start.3) | async-done | bytes 1310752 | tf_op jit(solution)/shard_map/all_to_all | solution.py:164
  205.6 7.6 %all-to-all-start.2 = ((bf16[16,32,768]{2,1,0:T(8,128)(2,1)}), bf16[16,32,768]{2,1,0:T(8,128)(2,1)}, u32[]{:S(2)}, u32[]{:S(2)}) async-start(bf16[16,32,768]{2,1,0:T(8,128)(2,1)} %bitcast.51), calls=%async_computation.2 | async-start | bytes 1572864 | tf_op jit(solution)/shard_map/all_to_all | solution.py:164
  215.7 2.4 early_rows.1
  218.2 7.6 %all-to-all-done.2.got = bf16[16,32,768]{2,1,0:T(8,128)(2,1)} async-done(((bf16[16,32,768]{2,1,0:T(8,128)(2,1)}), bf16[16,32,768]{2,1,0:T(8,128)(2,1)}, u32[]{:S(2)}, u32[]{:S(2)}) %all-to-all-start.2) | async-done | bytes 786464 | tf_op jit(solution)/shard_map/all_to_all | solution.py:164
  227.6 4.2 %late_rows.1 = bf16[8,32,2048]{2,1,0:T(8,128)(2,1)} custom-call(s32[9]{0:T(128)S(1)} %pad_add_fusion.scalars, bf16[16,32,768]{2,1,0:T(8,128)(2,1)} %all-to-all-done.2.got, f32[2,32,1280]{2,1,0:T(8,128)S(1)} %get-tuple-element.56.k_early, f32[32,1024]{1,0:T(8,128)S(1)} %get-tuple-element.57.b_early, f32[1,1024]{1,0:T(1,128)S(1)} %bitcast.41, ...), custom_call_target="tpu_custom_call" | custom-call | flops 100663296 | bytes 8388608 | tf_op jit(solution)/shard_map/late_rows/pallas_call | solution.py:225
  231.8 5.5 %all-to-all-start.4 = ((bf16[8,32,2048]{2,1,0:T(8,128)(2,1)}), bf16[8,32,2048]{2,1,0:T(8,128)(2,1)S(1)}, u32[]{:S(2)}, u32[]{:S(2)}) async-start(bf16[8,32,2048]{2,1,0:T(8,128)(2,1)} %late_rows.1), calls=%async_computation.4 | async-start | bytes 2097152 | tf_op jit(solution)/shard_map/all_to_all | solution.py:341
  238.5 12.7 %all-to-all-done.4 = bf16[8,32,2048]{2,1,0:T(8,128)(2,1)S(1)} async-done(((bf16[8,32,2048]{2,1,0:T(8,128)(2,1)}), bf16[8,32,2048]{2,1,0:T(8,128)(2,1)S(1)}, u32[]{:S(2)}, u32[]{:S(2)}) %all-to-all-start.4) | async-done | bytes 1048608 | tf_op jit(solution)/shard_map/all_to_all | solution.py:341
  252.0 4.4 %collective-permute-start.25 = (bf16[256,256]{1,0:T(8,128)(2,1)S(1)}, bf16[256,256]{1,0:T(8,128)(2,1)S(1)}, u32[]{:S(2)}, u32[]{:S(2)}) collective-permute-start(bf16[256,256]{1,0:T(8,128)(2,1)S(1)} %copy.15), channel_id=1, source_target_pairs={{0,1},{1,0},{2,17},{3,16},{4,33},{5,32},{6,49},{7,48},{8,65},{9,64... | collective-permute-start | bytes 393224 | tf_op jit(solution)/shard_map/ppermute | solution.py:25
  256.5 5.3 %collective-permute-start.23 = (bf16[256,256]{1,0:T(8,128)(2,1)S(1)}, bf16[256,256]{1,0:T(8,128)(2,1)S(1)}, u32[]{:S(2)}, u32[]{:S(2)}) collective-permute-start(bf16[256,256]{1,0:T(8,128)(2,1)S(1)} %copy.14), channel_id=1, source_target_pairs={{0,0},{1,1},{2,16},{3,17},{4,32},{5,33},{6,48},{7,49},{8,64},{9,65... | collective-permute-start | bytes 393224 | tf_op jit(solution)/shard_map/ppermute | solution.py:25
  262.2 3.5 %collective-permute-done.25 = bf16[256,256]{1,0:T(8,128)(2,1)S(1)} collective-permute-done((bf16[256,256]{1,0:T(8,128)(2,1)S(1)}, bf16[256,256]{1,0:T(8,128)(2,1)S(1)}, u32[]{:S(2)}, u32[]{:S(2)}) %collective-permute-start.25) | collective-permute-done | bytes 131104 | tf_op jit(solution)/shard_map/ppermute | solution.py:25
  265.7 5.8 %collective-permute-done.23 = bf16[256,256]{1,0:T(8,128)(2,1)S(1)} collective-permute-done((bf16[256,256]{1,0:T(8,128)(2,1)S(1)}, bf16[256,256]{1,0:T(8,128)(2,1)S(1)}, u32[]{:S(2)}, u32[]{:S(2)}) %collective-permute-start.23) | collective-permute-done | bytes 131104 | tf_op jit(solution)/shard_map/ppermute | solution.py:25
  (133 shorter events, 44.3 us)
Async XLA Ops:
  0.0 16.9 %collective-permute-start = (bf16[256,1024]{1,0:T(8,128)(2,1)}, bf16[256,1024]{1,0:T(8,128)(2,1)S(1)}, u32[]{:S(2)}, u32[]{:S(2)}) collective-permute-start(bf16[256,1024]{1,0:T(8,128)(2,1)} %param.8), channel_id=1, source_target_pairs={{0,6},{1,7},{2,0},{3,1},{4,2},{5,3},{6,4},{7,5},{8,14},{9,15},{10,... | collective-permute-start | bytes 1572872 | tf_op jit(solution)/shard_map/ppermute | solution.py:25
  2.7 14.2 %collective-permute-start.1 = (bf16[256,1024]{1,0:T(8,128)(2,1)}, bf16[256,1024]{1,0:T(8,128)(2,1)S(1)}, u32[]{:S(2)}, u32[]{:S(2)}) collective-permute-start(bf16[256,1024]{1,0:T(8,128)(2,1)} %param.8), channel_id=1, source_target_pairs={{0,2},{1,3},{2,4},{3,5},{4,6},{5,7},{6,0},{7,1},{8,10},{9,11},{10,... | collective-permute-start | bytes 1572872 | tf_op jit(solution)/shard_map/ppermute | solution.py:25
  4.6 12.2 %collective-permute-start.2 = (bf16[128,1024]{1,0:T(8,128)(2,1)}, bf16[128,1024]{1,0:T(8,128)(2,1)S(1)}, u32[]{:S(2)}, u32[]{:S(2)}) collective-permute-start(bf16[128,1024]{1,0:T(8,128)(2,1)} %get-tuple-element.72), channel_id=1, source_target_pairs={{0,8},{1,9},{2,10},{3,11},{4,12},{5,13},{6,14},{7,15},{8,0},{9,1},... | collective-permute-start | bytes 786440 | tf_op jit(solution)/shard_map/ppermute | solution.py:25
  5.2 11.7 %collective-permute-start.3 = (bf16[128,1024]{1,0:T(8,128)(2,1)}, bf16[128,1024]{1,0:T(8,128)(2,1)S(1)}, u32[]{:S(2)}, u32[]{:S(2)}) collective-permute-start(bf16[128,1024]{1,0:T(8,128)(2,1)} %get-tuple-element.71), channel_id=1, source_target_pairs={{0,24},{1,25},{2,26},{3,27},{4,28},{5,29},{6,30},{7,31},{8,16},{9,... | collective-permute-start | bytes 786440 | tf_op jit(solution)/shard_map/ppermute | solution.py:25
  9.3 25.6 %collective-permute-start.8 = (f32[256,1024]{1,0:T(8,128)S(1)}, f32[256,1024]{1,0:T(8,128)}, u32[]{:S(2)}, u32[]{:S(2)}) collective-permute-start(f32[256,1024]{1,0:T(8,128)S(1)} %slice_select_fusion), channel_id=1, source_target_pairs={{0,1},{1,0},{2,3},{3,2},{4,5},{5,4},{6,7},{7,6},{8,9},{9,8},{10,11... | collective-permute-start | bytes 3145736 | tf_op jit(solution)/shard_map/ppermute | solution.py:25
  17.0 10.3 %collective-permute-start.5 = (bf16[128,1024]{1,0:T(8,128)(2,1)S(1)}, bf16[128,1024]{1,0:T(8,128)(2,1)S(1)}, u32[]{:S(2)}, u32[]{:S(2)}) collective-permute-start(bf16[128,1024]{1,0:T(8,128)(2,1)S(1)} %get-tuple-element.70), channel_id=1, source_target_pairs={{0,2},{1,3},{2,4},{3,5},{4,6},{5,7},{6,0},{7,1},{8,10},{9,11},{10,... | collective-permute-start | bytes 786440 | tf_op jit(solution)/shard_map/ppermute | solution.py:25
  17.4 13.4 %collective-permute-start.7 = (bf16[256,1024]{1,0:T(8,128)(2,1)S(1)}, bf16[256,1024]{1,0:T(8,128)(2,1)S(1)}, u32[]{:S(2)}, u32[]{:S(2)}) collective-permute-start(bf16[256,1024]{1,0:T(8,128)(2,1)S(1)} %pad_maximum_fusion.2), channel_id=1, source_target_pairs={{0,24},{1,25},{2,26},{3,27},{4,28},{5,29},{6,30},{7,31},{8,16},{9,... | collective-permute-start | bytes 1572872 | tf_op jit(solution)/shard_map/ppermute | solution.py:25
  19.3 8.0 %collective-permute-start.4 = (bf16[128,1024]{1,0:T(8,128)(2,1)S(1)}, bf16[128,1024]{1,0:T(8,128)(2,1)S(1)}, u32[]{:S(2)}, u32[]{:S(2)}) collective-permute-start(bf16[128,1024]{1,0:T(8,128)(2,1)S(1)} %get-tuple-element.68), channel_id=1, source_target_pairs={{0,6},{1,7},{2,0},{3,1},{4,2},{5,3},{6,4},{7,5},{8,14},{9,15},{10,... | collective-permute-start | bytes 786440 | tf_op jit(solution)/shard_map/ppermute | solution.py:25
  22.0 12.9 %collective-permute-start.6 = (bf16[256,1024]{1,0:T(8,128)(2,1)S(1)}, bf16[256,1024]{1,0:T(8,128)(2,1)S(1)}, u32[]{:S(2)}, u32[]{:S(2)}) collective-permute-start(bf16[256,1024]{1,0:T(8,128)(2,1)S(1)} %pad_maximum_fusion.1), channel_id=1, source_target_pairs={{0,8},{1,9},{2,10},{3,11},{4,12},{5,13},{6,14},{7,15},{8,0},{9,1},... | collective-permute-start | bytes 1572872 | tf_op jit(solution)/shard_map/ppermute | solution.py:25
  34.9 4.5 %collective-permute-start.11 = (bf16[3,256,1024]{2,1,0:T(8,128)(2,1)S(1)}, bf16[3,256,1024]{2,1,0:T(8,128)(2,1)S(1)}, u32[]{:S(2)}, u32[]{:S(2)}) collective-permute-start(bf16[3,256,1024]{2,1,0:T(8,128)(2,1)S(1)} %bitcast.38), channel_id=1, source_target_pairs={{0,1},{1,0},{2,3},{3,2},{4,5},{5,4},{6,7},{7,6},{8,9},{9,8},{10,11... | collective-permute-start | bytes 4718600 | tf_op jit(solution)/shard_map/ppermute | solution.py:25
  36.4 9.1 %collective-permute-start.10 = (bf16[128,1024]{1,0:T(8,128)(2,1)S(1)}, bf16[128,1024]{1,0:T(8,128)(2,1)S(1)}, u32[]{:S(2)}, u32[]{:S(2)}) collective-permute-start(bf16[128,1024]{1,0:T(8,128)(2,1)S(1)} %collective-permute-done.5), channel_id=1, source_target_pairs={{0,24},{1,25},{2,26},{3,27},{4,28},{5,29},{6,30},{7,31},{8,16},{9,... | collective-permute-start | bytes 786440 | tf_op jit(solution)/shard_map/ppermute | solution.py:25
  37.3 8.2 %collective-permute-start.9 = (bf16[128,1024]{1,0:T(8,128)(2,1)S(1)}, bf16[128,1024]{1,0:T(8,128)(2,1)S(1)}, u32[]{:S(2)}, u32[]{:S(2)}) collective-permute-start(bf16[128,1024]{1,0:T(8,128)(2,1)S(1)} %collective-permute-done.4), channel_id=1, source_target_pairs={{0,8},{1,9},{2,10},{3,11},{4,12},{5,13},{6,14},{7,15},{8,0},{9,1},... | collective-permute-start | bytes 786440 | tf_op jit(solution)/shard_map/ppermute | solution.py:25
  45.6 65.7 %copy-start = (bf16[1280,1024]{1,0:T(8,128)(2,1)}, bf16[1280,1024]{1,0:T(8,128)(2,1)S(1)}, u32[]{:S(2)}) copy-start(bf16[1280,1024]{1,0:T(8,128)(2,1)S(1)} %constant_dynamic-update-slice_fusion.3) | copy-start | bytes 7864324
  45.6 5.7 %collective-permute-start.12 = (bf16[5,256,1024]{2,1,0:T(8,128)(2,1)S(1)}, bf16[5,256,1024]{2,1,0:T(8,128)(2,1)S(1)}, u32[]{:S(2)}, u32[]{:S(2)}) collective-permute-start(bf16[5,256,1024]{2,1,0:T(8,128)(2,1)S(1)} %bitcast.35), channel_id=1, source_target_pairs={{0,1},{1,0},{2,3},{3,2},{4,5},{5,4},{6,7},{7,6},{8,9},{9,8},{10,11... | collective-permute-start | bytes 7864328 | tf_op jit(solution)/shard_map/ppermute | solution.py:25
  56.2 4.4 %collective-permute-start.13 = (bf16[4,256,1024]{2,1,0:T(8,128)(2,1)}, bf16[4,256,1024]{2,1,0:T(8,128)(2,1)S(1)}, u32[]{:S(2)}, u32[]{:S(2)}) collective-permute-start(bf16[4,256,1024]{2,1,0:T(8,128)(2,1)} %bitcast.6.refs_0_.refs_2_), channel_id=1, source_target_pairs={{0,1},{1,0},{2,3},{3,2},{4,5},{5,4},{6,7},{7,6},{8,9},{9,8},{10,11... | collective-permute-start | bytes 6291464 | tf_op jit(solution)/shard_map/ppermute | solution.py:25
  56.6 47.4 %collective-permute-start.14 = (bf16[4,256,1024]{2,1,0:T(8,128)(2,1)}, bf16[4,256,1024]{2,1,0:T(8,128)(2,1)}, u32[]{:S(2)}, u32[]{:S(2)}) collective-permute-start(bf16[4,256,1024]{2,1,0:T(8,128)(2,1)} %bitcast.6.refs_0_.refs_2_), channel_id=1, source_target_pairs={{0,6},{1,7},{2,0},{3,1},{4,2},{5,3},{6,4},{7,5},{8,14},{9,15},{10,... | collective-permute-start | bytes 6291464 | tf_op jit(solution)/shard_map/ppermute | solution.py:25
  58.0 50.9 %collective-permute-start.16 = (bf16[4,256,1024]{2,1,0:T(8,128)(2,1)}, bf16[4,256,1024]{2,1,0:T(8,128)(2,1)}, u32[]{:S(2)}, u32[]{:S(2)}) collective-permute-start(bf16[4,256,1024]{2,1,0:T(8,128)(2,1)} %bitcast.6.refs_0_.refs_2_), channel_id=1, source_target_pairs={{0,2},{1,3},{2,4},{3,5},{4,6},{5,7},{6,0},{7,1},{8,10},{9,11},{10,... | collective-permute-start | bytes 6291464 | tf_op jit(solution)/shard_map/ppermute | solution.py:25
  58.1 59.5 %collective-permute-start.18 = (bf16[4,256,1024]{2,1,0:T(8,128)(2,1)}, bf16[4,256,1024]{2,1,0:T(8,128)(2,1)}, u32[]{:S(2)}, u32[]{:S(2)}) collective-permute-start(bf16[4,256,1024]{2,1,0:T(8,128)(2,1)} %bitcast.6.refs_0_.refs_2_), channel_id=1, source_target_pairs={{0,8},{1,9},{2,10},{3,11},{4,12},{5,13},{6,14},{7,15},{8,0},{9,1},... | collective-permute-start | bytes 6291464 | tf_op jit(solution)/shard_map/ppermute | solution.py:25
  63.6 47.9 %all-to-all-start = ((bf16[8,32,1024]{2,1,0:T(8,128)(2,1)}), bf16[8,32,1024]{2,1,0:T(8,128)(2,1)S(1)}, u32[]{:S(2)}, u32[]{:S(2)}) async-start(bf16[8,32,1024]{2,1,0:T(8,128)(2,1)} %bitcast.48), calls=%async_computation | async-start | bytes 1048576 | tf_op jit(solution)/shard_map/all_to_all | solution.py:323
  106.3 33.2 %collective-permute-start.15 = (bf16[2,256,1024]{2,1,0:T(8,128)(2,1)}, bf16[2,256,1024]{2,1,0:T(8,128)(2,1)}, u32[]{:S(2)}, u32[]{:S(2)}) collective-permute-start(bf16[2,256,1024]{2,1,0:T(8,128)(2,1)} %slice.98), channel_id=1, source_target_pairs={{0,6},{1,7},{2,0},{3,1},{4,2},{5,3},{6,4},{7,5},{8,14},{9,15},{10,... | collective-permute-start | bytes 3145736 | tf_op jit(solution)/shard_map/ppermute | solution.py:25
  111.3 28.2 %collective-permute-start.17 = (bf16[2,256,1024]{2,1,0:T(8,128)(2,1)}, bf16[2,256,1024]{2,1,0:T(8,128)(2,1)}, u32[]{:S(2)}, u32[]{:S(2)}) collective-permute-start(bf16[2,256,1024]{2,1,0:T(8,128)(2,1)} %slice.99), channel_id=1, source_target_pairs={{0,2},{1,3},{2,4},{3,5},{4,6},{5,7},{6,0},{7,1},{8,10},{9,11},{10,... | collective-permute-start | bytes 3145736 | tf_op jit(solution)/shard_map/ppermute | solution.py:25
  112.5 27.0 %all-to-all-start.1 = ((bf16[8,32,1024]{2,1,0:T(8,128)(2,1)}), bf16[8,32,1024]{2,1,0:T(8,128)(2,1)S(1)}, u32[]{:S(2)}, u32[]{:S(2)}) async-start(bf16[8,32,1024]{2,1,0:T(8,128)(2,1)} %broadcast_in_dim.14), calls=%async_computation.1 | async-start | bytes 1048576 | tf_op jit(solution)/shard_map/all_to_all | solution.py:329
  139.5 44.0 %collective-permute-start.21 = (bf16[4,256,1024]{2,1,0:T(8,128)(2,1)}, bf16[4,256,1024]{2,1,0:T(8,128)(2,1)}, u32[]{:S(2)}, u32[]{:S(2)}) collective-permute-start(bf16[4,256,1024]{2,1,0:T(8,128)(2,1)} %collective-permute-done.18.refs_5_), channel_id=1, source_target_pairs={{0,6},{1,7},{2,0},{3,1},{4,2},{5,3},{6,4},{7,5},{8,14},{9,15},{10,... | collective-permute-start | bytes 6291464 | tf_op jit(solution)/shard_map/ppermute | solution.py:25
  140.0 44.5 %collective-permute-start.22 = (bf16[4,256,1024]{2,1,0:T(8,128)(2,1)}, bf16[4,256,1024]{2,1,0:T(8,128)(2,1)}, u32[]{:S(2)}, u32[]{:S(2)}) collective-permute-start(bf16[4,256,1024]{2,1,0:T(8,128)(2,1)} %collective-permute-done.18.refs_5_), channel_id=1, source_target_pairs={{0,2},{1,3},{2,4},{3,5},{4,6},{5,7},{6,0},{7,1},{8,10},{9,11},{10,... | collective-permute-start | bytes 6291464 | tf_op jit(solution)/shard_map/ppermute | solution.py:25
  141.0 26.8 %collective-permute-start.19 = (bf16[2,256,1024]{2,1,0:T(8,128)(2,1)}, bf16[2,256,1024]{2,1,0:T(8,128)(2,1)S(1)}, u32[]{:S(2)}, u32[]{:S(2)}) collective-permute-start(bf16[2,256,1024]{2,1,0:T(8,128)(2,1)} %collective-permute-done.15.refs_6_), channel_id=1, source_target_pairs={{0,8},{1,9},{2,10},{3,11},{4,12},{5,13},{6,14},{7,15},{8,0},{9,1},... | collective-permute-start | bytes 3145736 | tf_op jit(solution)/shard_map/ppermute | solution.py:25
  141.8 41.7 %collective-permute-start.20 = (bf16[2,256,1024]{2,1,0:T(8,128)(2,1)}, bf16[2,256,1024]{2,1,0:T(8,128)(2,1)}, u32[]{:S(2)}, u32[]{:S(2)}) collective-permute-start(bf16[2,256,1024]{2,1,0:T(8,128)(2,1)} %collective-permute-done.17.refs_7_), channel_id=1, source_target_pairs={{0,8},{1,9},{2,10},{3,11},{4,12},{5,13},{6,14},{7,15},{8,0},{9,1},... | collective-permute-start | bytes 3145736 | tf_op jit(solution)/shard_map/ppermute | solution.py:25
  154.4 51.1 %all-to-all-start.3 = ((bf16[16,32,1280]{2,1,0:T(8,128)(2,1)}), bf16[16,32,1280]{2,1,0:T(8,128)(2,1)S(1)}, u32[]{:S(2)}, u32[]{:S(2)}) async-start(bf16[16,32,1280]{2,1,0:T(8,128)(2,1)} %bitcast.50), calls=%async_computation.3 | async-start | bytes 2621440 | tf_op jit(solution)/shard_map/all_to_all | solution.py:164
  205.6 20.3 %all-to-all-start.2 = ((bf16[16,32,768]{2,1,0:T(8,128)(2,1)}), bf16[16,32,768]{2,1,0:T(8,128)(2,1)}, u32[]{:S(2)}, u32[]{:S(2)}) async-start(bf16[16,32,768]{2,1,0:T(8,128)(2,1)} %bitcast.51), calls=%async_computation.2 | async-start | bytes 1572864 | tf_op jit(solution)/shard_map/all_to_all | solution.py:164
  231.8 19.4 %all-to-all-start.4 = ((bf16[8,32,2048]{2,1,0:T(8,128)(2,1)}), bf16[8,32,2048]{2,1,0:T(8,128)(2,1)S(1)}, u32[]{:S(2)}, u32[]{:S(2)}) async-start(bf16[8,32,2048]{2,1,0:T(8,128)(2,1)} %late_rows.1), calls=%async_computation.4 | async-start | bytes 2097152 | tf_op jit(solution)/shard_map/all_to_all | solution.py:341
  237.3 14.3 %collective-permute-start.24 = (bf16[256,1024]{1,0:T(8,128)(2,1)S(1)}, bf16[256,1024]{1,0:T(8,128)(2,1)S(1)}, u32[]{:S(2)}, u32[]{:S(2)}) collective-permute-start(bf16[256,1024]{1,0:T(8,128)(2,1)S(1)} %bitcast.46), channel_id=1, source_target_pairs={{0,1},{1,0},{2,3},{3,2},{4,5},{5,4},{6,7},{7,6},{8,9},{9,8},{10,11... | collective-permute-start | bytes 1572872 | tf_op jit(solution)/shard_map/ppermute | solution.py:25
  252.0 13.7 %collective-permute-start.25 = (bf16[256,256]{1,0:T(8,128)(2,1)S(1)}, bf16[256,256]{1,0:T(8,128)(2,1)S(1)}, u32[]{:S(2)}, u32[]{:S(2)}) collective-permute-start(bf16[256,256]{1,0:T(8,128)(2,1)S(1)} %copy.15), channel_id=1, source_target_pairs={{0,1},{1,0},{2,17},{3,16},{4,33},{5,32},{6,49},{7,48},{8,65},{9,64... | collective-permute-start | bytes 393224 | tf_op jit(solution)/shard_map/ppermute | solution.py:25
  256.5 15.0 %collective-permute-start.23 = (bf16[256,256]{1,0:T(8,128)(2,1)S(1)}, bf16[256,256]{1,0:T(8,128)(2,1)S(1)}, u32[]{:S(2)}, u32[]{:S(2)}) collective-permute-start(bf16[256,256]{1,0:T(8,128)(2,1)S(1)} %copy.14), channel_id=1, source_target_pairs={{0,0},{1,1},{2,16},{3,17},{4,32},{5,33},{6,48},{7,49},{8,64},{9,65... | collective-permute-start | bytes 393224 | tf_op jit(solution)/shard_map/ppermute | solution.py:25
  (18 other events, 157.9 us)

commit v6 on v5

--- a/solution.py
+++ b/solution.py
@@ -264,6 +264,22 @@
     hb = ao_dev // 2
     flag = env_flag.astype(jnp.float32)[None, :]
 
+    order = (y + jnp.array([0, 1, NY - 1, 2], jnp.int32)) % NY
+    sides = jnp.concatenate([a * NY + order, (1 - a) * NY + order]).astype(jnp.int32)
+    cols = jnp.concatenate([sides * NK + core, sides * NK + 1 - core])
+    keep = jnp.repeat(block_mask[0], ATILE, axis=1).astype(jnp.float32)
+    own_m, oth_m = masked_columns(cols, keep, slab, ao_dev)
+    wide = 3 * ao_dev
+
+    def product(left, right):
+        return jnp.dot(left, right.reshape(-1, occ), preferred_element_type=jnp.float32)
+
+    def cross_over(t):
+        return [across_in(t[:hb]), across_out(t[hb:])]
+
+    nxt, prv, margin, *own_x, own_m, oth_m = lax.optimization_barrier(
+        (from_next(orbitals), from_prev(orbitals), margin, *cross_over(orbitals), own_m, oth_m)
+    )
     group = lax.axis_index("grp")
     row = (chip * NK + core) * ao_dev + lax.broadcasted_iota(jnp.int32, margin.shape, 0)
     col = group * 2 * ao_dev + lax.broadcasted_iota(jnp.int32, margin.shape, 1)
@@ -273,22 +289,6 @@
     )
     a_low, a_high = a_part[:ao_dev], a_part[ao_dev:]
     a_send = other_core(jnp.where(core == 0, a_high, a_low))
-    order = (y + jnp.array([0, 1, NY - 1, 2], jnp.int32)) % NY
-    sides = jnp.concatenate([a * NY + order, (1 - a) * NY + order]).astype(jnp.int32)
-    cols = jnp.concatenate([sides * NK + core, sides * NK + 1 - core])
-    keep = jnp.repeat(block_mask[0], ATILE, axis=1).astype(jnp.float32)
-    own_m, oth_m = masked_columns(cols, keep, slab, ao_dev)
-    wide = 3 * ao_dev
-
-    def product(left, right):
-        return jnp.dot(left, right.reshape(-1, occ), preferred_element_type=jnp.float32)
-
-    def cross_over(t):
-        return [across_in(t[:hb]), across_out(t[hb:])]
-
-    nxt, prv, *own_x, own_m, oth_m = lax.optimization_barrier(
-        (from_next(orbitals), from_prev(orbitals), *cross_over(orbitals), own_m, oth_m)
-    )
     near = jnp.concatenate([orbitals, nxt, prv]).reshape(3, ao_dev, occ)
     base = product(own_m[:, :wide], near)
     far_lo, far_hi, side_in, side_out, near, base, a_send = lax.optimization_barrier(

time: 274 us -> 273 us (level)
  waiting for transfers between devices: 134 us -> 139 us
    ppermute x26, waiting for transfers between devices: 79.3 us -> 85.3 us  [moved(): return lax.ppermute(x, AXES, pairs)]
  transfers between devices with their start and end apart: 31 -> 31, of which waited for: 16 -> 21; matrix products, arithmetic and copies ran while one was open for 10% -> 8% of each run, Pallas kernels for 10% -> 10%
where the time goes in v6:
time: 273 us
  waiting for transfers between devices  139 us (51%)
  starting transfers between devices  67.2 us (25%)
  Pallas kernels  32.3 us (12%)
  local copies, waits for them, and re-layouts  14.3 us (5%)
  matrix products  10.6 us (4%)
  other arithmetic  8.6 us (3%)
    ppermute x26, waiting for transfers between devices, moved(): return lax.ppermute(x, AXES, pairs)  85.3 us
    ppermute x26, starting transfers between devices, moved(): return lax.ppermute(x, AXES, pairs)  32.8 us
    all_to_all x1, waiting for transfers between devices, on_device(): a_own = lax.all_to_all(a_slice, 'chip', 0, 0).reshape(ao_dev, occ)  21.9 us
    all_to_all x2, starting transfers between devices, exchanged(): return lax.all_to_all(cut.reshape(16, rows, cols), ('grp', 'core'), 0, 0)  20.6 us
    pallas_call x2, Pallas kernels, pair_tiles(): pl.pallas_call(tiles_kernel, out_shape=out, grid_spec=pltpu.PrefetchScala...  20.4 us
    all_to_all x2, waiting for transfers between devices, exchanged(): return lax.all_to_all(cut.reshape(16, rows, cols), ('grp', 'core'), 0, 0)  19.1 us
    all_to_all x1, waiting for transfers between devices, on_device(): got = lax.all_to_all(packed, 'grp', 0, 0).reshape(ao_dev, -1)  12.7 us
    dot_general x4, matrix products, product(): jnp.dot(left, right.reshape(-1, occ), preferred_element_type=jnp.float32)  9.34 us
  transfers between devices with their start and end apart: 31, of which 21 were waited for; matrix products, arithmetic and copies ran while one was open for 8% of the time, Pallas kernels for 10%

profile of v6, /device:TPU:7, one launch (start us, length us, event | category | flops | bytes accessed | tf_op | source)
XLA Modules:
  0.0 272.6 jit_solution(10721482215088634336)
XLA Ops:
  0.0 2.7 %collective-permute-start = (bf16[256,1024]{1,0:T(8,128)(2,1)}, bf16[256,1024]{1,0:T(8,128)(2,1)S(1)}, u32[]{:S(2)}, u32[]{:S(2)}) collective-permute-start(bf16[256,1024]{1,0:T(8,128)(2,1)} %param.8), channel_id=1, source_target_pairs={{0,6},{1,7},{2,0},{3,1},{4,2},{5,3},{6,4},{7,5},{8,14},{9,15},{10,... | collective-permute-start | bytes 1572872 | tf_op jit(solution)/shard_map/ppermute | solution.py:25
  7.3 5.2 %masked_columns.1 = (bf16[1024,2048]{1,0:T(8,128)(2,1)S(1)}, bf16[1024,2048]{1,0:T(8,128)(2,1)S(1)}) custom-call(s32[16]{0:T(128)S(1)} %pad_add_fusion.2.cols, f32[8,4096]{1,0:T(8,128)S(1)} %convert_element_type.55.refs_0_.refs_1_.refs_2_.refs_3_, f32[8,4096]{1,0:T(8,128)S(1)} %convert_element_type.55.refs_0_.refs_1_.refs_2_.refs_3_, ...), custom_call_target="tpu_custom_call" | custom-call | tf_op jit(solution)/shard_map/masked_columns/pallas_call | solution.py:102
  13.6 3.0 %collective-permute-done.1 = bf16[256,1024]{1,0:T(8,128)(2,1)S(1)} collective-permute-done((bf16[256,1024]{1,0:T(8,128)(2,1)}, bf16[256,1024]{1,0:T(8,128)(2,1)S(1)}, u32[]{:S(2)}, u32[]{:S(2)}) %collective-permute-start.1) | collective-permute-done | bytes 524320 | tf_op jit(solution)/shard_map/ppermute | solution.py:25
  19.8 2.7 collective-permute-start.4
  25.1 2.5 collective-permute-done.4
  28.6 5.8 %collective-permute-done.7 = bf16[256,1024]{1,0:T(8,128)(2,1)S(1)} collective-permute-done((bf16[256,1024]{1,0:T(8,128)(2,1)S(1)}, bf16[256,1024]{1,0:T(8,128)(2,1)S(1)}, u32[]{:S(2)}, u32[]{:S(2)}) %collective-permute-start.7) | collective-permute-done | bytes 524320 | tf_op jit(solution)/shard_map/ppermute | solution.py:25
  36.9 2.5 collective-permute-start.10
  43.9 2.1 collective-permute-done.10
  48.5 2.9 %fusion.2 = f32[1024,1024]{1,0:T(8,128)S(1)} fusion(bf16[1280,1024]{1,0:T(8,128)(2,1)S(1)} %constant_dynamic-update-slice_fusion.3, bf16[1024,2048]{1,0:T(8,128)(2,1)S(1)} %get-tuple-element.37), kind=kOutput, calls=%fused_computation.3 | convolution fusion | flops 2684354560 | bytes 9437184 | tf_op jit(solution)/shard_map/dot_general | solution.py:275
  53.0 2.9 %fusion = f32[1024,1024]{1,0:T(8,128)S(1)} fusion(bf16[1280,1024]{1,0:T(8,128)(2,1)S(1)} %bitcast.45, bf16[1024,2048]{1,0:T(8,128)(2,1)S(1)} %get-tuple-element.46), kind=kOutput, calls=%fused_computation.1 | convolution fusion | flops 2684354560 | bytes 9437184 | tf_op jit(solution)/shard_map/dot_general | solution.py:275
  59.8 2.5 collective-permute-done.13.refs_1_
  63.8 3.4 %all-to-all-start = ((bf16[8,32,1024]{2,1,0:T(8,128)(2,1)}), bf16[8,32,1024]{2,1,0:T(8,128)(2,1)S(1)}, u32[]{:S(2)}, u32[]{:S(2)}) async-start(bf16[8,32,1024]{2,1,0:T(8,128)(2,1)} %bitcast.48), calls=%async_computation | async-start | bytes 1048576 | tf_op jit(solution)/shard_map/all_to_all | solution.py:323
  68.3 37.4 %collective-permute-done.14.refs_3_ = bf16[4,256,1024]{2,1,0:T(8,128)(2,1)} collective-permute-done((bf16[4,256,1024]{2,1,0:T(8,128)(2,1)}, bf16[4,256,1024]{2,1,0:T(8,128)(2,1)}, u32[]{:S(2)}, u32[]{:S(2)}) %collective-permute-start.14) | collective-permute-done | bytes 2097184 | tf_op jit(solution)/shard_map/ppermute | solution.py:25
  105.7 2.3 slice.98
  109.2 2.3 slice.99
  113.0 4.8 %all-to-all-start.1 = ((bf16[8,32,1024]{2,1,0:T(8,128)(2,1)}), bf16[8,32,1024]{2,1,0:T(8,128)(2,1)S(1)}, u32[]{:S(2)}, u32[]{:S(2)}) async-start(bf16[8,32,1024]{2,1,0:T(8,128)(2,1)} %broadcast_in_dim.14), calls=%async_computation.1 | async-start | bytes 1048576 | tf_op jit(solution)/shard_map/all_to_all | solution.py:329
  117.8 21.9 %all-to-all-done.1 = bf16[8,32,1024]{2,1,0:T(8,128)(2,1)S(1)} async-done(((bf16[8,32,1024]{2,1,0:T(8,128)(2,1)}), bf16[8,32,1024]{2,1,0:T(8,128)(2,1)S(1)}, u32[]{:S(2)}, u32[]{:S(2)}) %all-to-all-start.1) | async-done | bytes 524320 | tf_op jit(solution)/shard_map/all_to_all | solution.py:329
  142.7 12.0 %exchange_tiles.3 = bf16[8,2,32,1280]{3,2,1,0:T(8,128)(2,1)} custom-call(s32[1]{0:T(128)} %bitcast.core_ref, bf16[4,256,1024]{2,1,0:T(8,128)(2,1)} %bitcast.6.refs_0_.refs_2_, bf16[4,256,1024]{2,1,0:T(8,128)(2,1)} %copy-done.14, bf16[4,256,1024]{2,1,0:T(8,128)(2,1)} %bitcast.6.refs_0_.refs_2_, bf16[4,256,1024]{2,1,0:T(8,128)(2,1)} %collective-permute-done.14.refs_3_, ...), custom_call_target="tpu_custom_call" | custom-call | flops 5368709120 | bytes 15990784 | tf_op jit(solution)/shard_map/exchange_tiles/pallas_call | solution.py:143
  154.7 13.5 %all-to-all-start.3 = ((bf16[16,32,1280]{2,1,0:T(8,128)(2,1)}), bf16[16,32,1280]{2,1,0:T(8,128)(2,1)S(1)}, u32[]{:S(2)}, u32[]{:S(2)}) async-start(bf16[16,32,1280]{2,1,0:T(8,128)(2,1)} %bitcast.50), calls=%async_computation.3 | async-start | bytes 2621440 | tf_op jit(solution)/shard_map/all_to_all | solution.py:164
  168.2 15.5 %collective-permute-done.20.refs_3_ = bf16[2,256,1024]{2,1,0:T(8,128)(2,1)} collective-permute-done((bf16[2,256,1024]{2,1,0:T(8,128)(2,1)}, bf16[2,256,1024]{2,1,0:T(8,128)(2,1)}, u32[]{:S(2)}, u32[]{:S(2)}) %collective-permute-start.20) | collective-permute-done | bytes 1048608 | tf_op jit(solution)/shard_map/ppermute | solution.py:25
  185.6 8.4 %exchange_tiles.2 = bf16[8,2,32,768]{3,2,1,0:T(8,128)(2,1)} custom-call(s32[1]{0:T(128)} %bitcast.core_ref, bf16[4,256,1024]{2,1,0:T(8,128)(2,1)} %bitcast.6.refs_0_.refs_2_, bf16[4,256,1024]{2,1,0:T(8,128)(2,1)} %copy-done.14, bf16[2,256,1024]{2,1,0:T(8,128)(2,1)} %copy-done.15, bf16[2,256,1024]{2,1,0:T(8,128)(2,1)} %collective-permute-done.20.refs_3_, ...), custom_call_target="tpu_custom_call" | custom-call | flops 3221225472 | bytes 11272192 | tf_op jit(solution)/shard_map/exchange_tiles/pallas_call | solution.py:143
  194.1 11.5 %all-to-all-done.3.got = bf16[16,32,1280]{2,1,0:T(8,128)(2,1)S(1)} async-done(((bf16[16,32,1280]{2,1,0:T(8,128)(2,1)}), bf16[16,32,1280]{2,1,0:T(8,128)(2,1)S(1)}, u32[]{:S(2)}, u32[]{:S(2)}) %all-to-all-start.3) | async-done | bytes 1310752 | tf_op jit(solution)/shard_map/all_to_all | solution.py:164
  205.5 7.2 %all-to-all-start.2 = ((bf16[16,32,768]{2,1,0:T(8,128)(2,1)}), bf16[16,32,768]{2,1,0:T(8,128)(2,1)}, u32[]{:S(2)}, u32[]{:S(2)}) async-start(bf16[16,32,768]{2,1,0:T(8,128)(2,1)} %bitcast.51), calls=%async_computation.2 | async-start | bytes 1572864 | tf_op jit(solution)/shard_map/all_to_all | solution.py:164
  215.3 2.4 early_rows.1
  217.7 7.6 %all-to-all-done.2.got = bf16[16,32,768]{2,1,0:T(8,128)(2,1)} async-done(((bf16[16,32,768]{2,1,0:T(8,128)(2,1)}), bf16[16,32,768]{2,1,0:T(8,128)(2,1)}, u32[]{:S(2)}, u32[]{:S(2)}) %all-to-all-start.2) | async-done | bytes 786464 | tf_op jit(solution)/shard_map/all_to_all | solution.py:164
  227.1 4.2 %late_rows.1 = bf16[8,32,2048]{2,1,0:T(8,128)(2,1)} custom-call(s32[9]{0:T(128)S(1)} %pad_add_fusion.scalars, bf16[16,32,768]{2,1,0:T(8,128)(2,1)} %all-to-all-done.2.got, f32[2,32,1280]{2,1,0:T(8,128)S(1)} %get-tuple-element.58.k_early, f32[32,1024]{1,0:T(8,128)S(1)} %get-tuple-element.59.b_early, f32[1,1024]{1,0:T(1,128)S(1)} %bitcast.41, ...), custom_call_target="tpu_custom_call" | custom-call | flops 100663296 | bytes 8388608 | tf_op jit(solution)/shard_map/late_rows/pallas_call | solution.py:225
  231.3 5.5 %all-to-all-start.4 = ((bf16[8,32,2048]{2,1,0:T(8,128)(2,1)}), bf16[8,32,2048]{2,1,0:T(8,128)(2,1)S(1)}, u32[]{:S(2)}, u32[]{:S(2)}) async-start(bf16[8,32,2048]{2,1,0:T(8,128)(2,1)} %late_rows.1), calls=%async_computation.4 | async-start | bytes 2097152 | tf_op jit(solution)/shard_map/all_to_all | solution.py:341
  238.0 12.7 %all-to-all-done.4 = bf16[8,32,2048]{2,1,0:T(8,128)(2,1)S(1)} async-done(((bf16[8,32,2048]{2,1,0:T(8,128)(2,1)}), bf16[8,32,2048]{2,1,0:T(8,128)(2,1)S(1)}, u32[]{:S(2)}, u32[]{:S(2)}) %all-to-all-start.4) | async-done | bytes 1048608 | tf_op jit(solution)/shard_map/all_to_all | solution.py:341
  251.5 5.4 %collective-permute-start.25 = (bf16[256,256]{1,0:T(8,128)(2,1)S(1)}, bf16[256,256]{1,0:T(8,128)(2,1)S(1)}, u32[]{:S(2)}, u32[]{:S(2)}) collective-permute-start(bf16[256,256]{1,0:T(8,128)(2,1)S(1)} %copy.15), channel_id=1, source_target_pairs={{0,1},{1,0},{2,17},{3,16},{4,33},{5,32},{6,49},{7,48},{8,65},{9,64... | collective-permute-start | bytes 393224 | tf_op jit(solution)/shard_map/ppermute | solution.py:25
  257.0 4.4 %collective-permute-start.23 = (bf16[256,256]{1,0:T(8,128)(2,1)S(1)}, bf16[256,256]{1,0:T(8,128)(2,1)S(1)}, u32[]{:S(2)}, u32[]{:S(2)}) collective-permute-start(bf16[256,256]{1,0:T(8,128)(2,1)S(1)} %copy.14), channel_id=1, source_target_pairs={{0,0},{1,1},{2,16},{3,17},{4,32},{5,33},{6,48},{7,49},{8,64},{9,65... | collective-permute-start | bytes 393224 | tf_op jit(solution)/shard_map/ppermute | solution.py:25
  261.7 4.2 %collective-permute-done.25 = bf16[256,256]{1,0:T(8,128)(2,1)S(1)} collective-permute-done((bf16[256,256]{1,0:T(8,128)(2,1)S(1)}, bf16[256,256]{1,0:T(8,128)(2,1)S(1)}, u32[]{:S(2)}, u32[]{:S(2)}) %collective-permute-start.25) | collective-permute-done | bytes 131104 | tf_op jit(solution)/shard_map/ppermute | solution.py:25
  265.9 5.6 %collective-permute-done.23 = bf16[256,256]{1,0:T(8,128)(2,1)S(1)} collective-permute-done((bf16[256,256]{1,0:T(8,128)(2,1)S(1)}, bf16[256,256]{1,0:T(8,128)(2,1)S(1)}, u32[]{:S(2)}, u32[]{:S(2)}) %collective-permute-start.23) | collective-permute-done | bytes 131104 | tf_op jit(solution)/shard_map/ppermute | solution.py:25
  (127 shorter events, 45.1 us)
Async XLA Ops:
  0.0 13.6 %collective-permute-start = (bf16[256,1024]{1,0:T(8,128)(2,1)}, bf16[256,1024]{1,0:T(8,128)(2,1)S(1)}, u32[]{:S(2)}, u32[]{:S(2)}) collective-permute-start(bf16[256,1024]{1,0:T(8,128)(2,1)} %param.8), channel_id=1, source_target_pairs={{0,6},{1,7},{2,0},{3,1},{4,2},{5,3},{6,4},{7,5},{8,14},{9,15},{10,... | collective-permute-start | bytes 1572872 | tf_op jit(solution)/shard_map/ppermute | solution.py:25
  2.7 13.9 %collective-permute-start.1 = (bf16[256,1024]{1,0:T(8,128)(2,1)}, bf16[256,1024]{1,0:T(8,128)(2,1)S(1)}, u32[]{:S(2)}, u32[]{:S(2)}) collective-permute-start(bf16[256,1024]{1,0:T(8,128)(2,1)} %param.8), channel_id=1, source_target_pairs={{0,2},{1,3},{2,4},{3,5},{4,6},{5,7},{6,0},{7,1},{8,10},{9,11},{10,... | collective-permute-start | bytes 1572872 | tf_op jit(solution)/shard_map/ppermute | solution.py:25
  3.8 8.8 %collective-permute-start.2 = (bf16[128,1024]{1,0:T(8,128)(2,1)S(1)}, bf16[128,1024]{1,0:T(8,128)(2,1)S(1)}, u32[]{:S(2)}, u32[]{:S(2)}) collective-permute-start(bf16[128,1024]{1,0:T(8,128)(2,1)S(1)} %get-tuple-element.74), channel_id=1, source_target_pairs={{0,8},{1,9},{2,10},{3,11},{4,12},{5,13},{6,14},{7,15},{8,0},{9,1},... | collective-permute-start | bytes 786440 | tf_op jit(solution)/shard_map/ppermute | solution.py:25
  4.5 8.2 %collective-permute-start.3 = (bf16[128,1024]{1,0:T(8,128)(2,1)S(1)}, bf16[128,1024]{1,0:T(8,128)(2,1)S(1)}, u32[]{:S(2)}, u32[]{:S(2)}) collective-permute-start(bf16[128,1024]{1,0:T(8,128)(2,1)S(1)} %get-tuple-element.73), channel_id=1, source_target_pairs={{0,24},{1,25},{2,26},{3,27},{4,28},{5,29},{6,30},{7,31},{8,16},{9,... | collective-permute-start | bytes 786440 | tf_op jit(solution)/shard_map/ppermute | solution.py:25
  17.4 17.8 %collective-permute-start.8 = (f32[256,1024]{1,0:T(8,128)S(1)}, f32[256,1024]{1,0:T(8,128)S(1)}, u32[]{:S(2)}, u32[]{:S(2)}) collective-permute-start(f32[256,1024]{1,0:T(8,128)S(1)} %slice_select_fusion), channel_id=1, source_target_pairs={{0,1},{1,0},{2,3},{3,2},{4,5},{5,4},{6,7},{7,6},{8,9},{9,8},{10,11... | collective-permute-start | bytes 3145736 | tf_op jit(solution)/shard_map/ppermute | solution.py:25
  19.4 9.2 %collective-permute-start.5 = (bf16[128,1024]{1,0:T(8,128)(2,1)S(1)}, bf16[128,1024]{1,0:T(8,128)(2,1)S(1)}, u32[]{:S(2)}, u32[]{:S(2)}) collective-permute-start(bf16[128,1024]{1,0:T(8,128)(2,1)S(1)} %get-tuple-element.72), channel_id=1, source_target_pairs={{0,2},{1,3},{2,4},{3,5},{4,6},{5,7},{6,0},{7,1},{8,10},{9,11},{10,... | collective-permute-start | bytes 786440 | tf_op jit(solution)/shard_map/ppermute | solution.py:25
  19.5 14.8 %collective-permute-start.7 = (bf16[256,1024]{1,0:T(8,128)(2,1)S(1)}, bf16[256,1024]{1,0:T(8,128)(2,1)S(1)}, u32[]{:S(2)}, u32[]{:S(2)}) collective-permute-start(bf16[256,1024]{1,0:T(8,128)(2,1)S(1)} %pad_maximum_fusion.2), channel_id=1, source_target_pairs={{0,24},{1,25},{2,26},{3,27},{4,28},{5,29},{6,30},{7,31},{8,16},{9,... | collective-permute-start | bytes 1572872 | tf_op jit(solution)/shard_map/ppermute | solution.py:25
  19.8 7.7 %collective-permute-start.4 = (bf16[128,1024]{1,0:T(8,128)(2,1)S(1)}, bf16[128,1024]{1,0:T(8,128)(2,1)S(1)}, u32[]{:S(2)}, u32[]{:S(2)}) collective-permute-start(bf16[128,1024]{1,0:T(8,128)(2,1)S(1)} %get-tuple-element.70), channel_id=1, source_target_pairs={{0,6},{1,7},{2,0},{3,1},{4,2},{5,3},{6,4},{7,5},{8,14},{9,15},{10,... | collective-permute-start | bytes 786440 | tf_op jit(solution)/shard_map/ppermute | solution.py:25
  22.5 12.7 %collective-permute-start.6 = (bf16[256,1024]{1,0:T(8,128)(2,1)S(1)}, bf16[256,1024]{1,0:T(8,128)(2,1)S(1)}, u32[]{:S(2)}, u32[]{:S(2)}) collective-permute-start(bf16[256,1024]{1,0:T(8,128)(2,1)S(1)} %pad_maximum_fusion.1), channel_id=1, source_target_pairs={{0,8},{1,9},{2,10},{3,11},{4,12},{5,13},{6,14},{7,15},{8,0},{9,1},... | collective-permute-start | bytes 1572872 | tf_op jit(solution)/shard_map/ppermute | solution.py:25
  35.2 4.8 %collective-permute-start.11 = (bf16[3,256,1024]{2,1,0:T(8,128)(2,1)S(1)}, bf16[3,256,1024]{2,1,0:T(8,128)(2,1)S(1)}, u32[]{:S(2)}, u32[]{:S(2)}) collective-permute-start(bf16[3,256,1024]{2,1,0:T(8,128)(2,1)S(1)} %bitcast.38), channel_id=1, source_target_pairs={{0,1},{1,0},{2,3},{3,2},{4,5},{5,4},{6,7},{7,6},{8,9},{9,8},{10,11... | collective-permute-start | bytes 4718600 | tf_op jit(solution)/shard_map/ppermute | solution.py:25
  36.9 9.1 %collective-permute-start.10 = (bf16[128,1024]{1,0:T(8,128)(2,1)S(1)}, bf16[128,1024]{1,0:T(8,128)(2,1)S(1)}, u32[]{:S(2)}, u32[]{:S(2)}) collective-permute-start(bf16[128,1024]{1,0:T(8,128)(2,1)S(1)} %collective-permute-done.5), channel_id=1, source_target_pairs={{0,24},{1,25},{2,26},{3,27},{4,28},{5,29},{6,30},{7,31},{8,16},{9,... | collective-permute-start | bytes 786440 | tf_op jit(solution)/shard_map/ppermute | solution.py:25
  39.4 7.5 %collective-permute-start.9 = (bf16[128,1024]{1,0:T(8,128)(2,1)S(1)}, bf16[128,1024]{1,0:T(8,128)(2,1)S(1)}, u32[]{:S(2)}, u32[]{:S(2)}) collective-permute-start(bf16[128,1024]{1,0:T(8,128)(2,1)S(1)} %collective-permute-done.4), channel_id=1, source_target_pairs={{0,8},{1,9},{2,10},{3,11},{4,12},{5,13},{6,14},{7,15},{8,0},{9,1},... | collective-permute-start | bytes 786440 | tf_op jit(solution)/shard_map/ppermute | solution.py:25
  47.0 64.8 %copy-start = (bf16[1280,1024]{1,0:T(8,128)(2,1)}, bf16[1280,1024]{1,0:T(8,128)(2,1)S(1)}, u32[]{:S(2)}) copy-start(bf16[1280,1024]{1,0:T(8,128)(2,1)S(1)} %constant_dynamic-update-slice_fusion.3) | copy-start | bytes 7864324
  47.0 6.0 %collective-permute-start.12 = (bf16[5,256,1024]{2,1,0:T(8,128)(2,1)S(1)}, bf16[5,256,1024]{2,1,0:T(8,128)(2,1)S(1)}, u32[]{:S(2)}, u32[]{:S(2)}) collective-permute-start(bf16[5,256,1024]{2,1,0:T(8,128)(2,1)S(1)} %bitcast.35), channel_id=1, source_target_pairs={{0,1},{1,0},{2,3},{3,2},{4,5},{5,4},{6,7},{7,6},{8,9},{9,8},{10,11... | collective-permute-start | bytes 7864328 | tf_op jit(solution)/shard_map/ppermute | solution.py:25
  57.9 4.4 %collective-permute-start.13 = (bf16[4,256,1024]{2,1,0:T(8,128)(2,1)}, bf16[4,256,1024]{2,1,0:T(8,128)(2,1)S(1)}, u32[]{:S(2)}, u32[]{:S(2)}) collective-permute-start(bf16[4,256,1024]{2,1,0:T(8,128)(2,1)} %bitcast.6.refs_0_.refs_2_), channel_id=1, source_target_pairs={{0,1},{1,0},{2,3},{3,2},{4,5},{5,4},{6,7},{7,6},{8,9},{9,8},{10,11... | collective-permute-start | bytes 6291464 | tf_op jit(solution)/shard_map/ppermute | solution.py:25
  58.3 47.4 %collective-permute-start.14 = (bf16[4,256,1024]{2,1,0:T(8,128)(2,1)}, bf16[4,256,1024]{2,1,0:T(8,128)(2,1)}, u32[]{:S(2)}, u32[]{:S(2)}) collective-permute-start(bf16[4,256,1024]{2,1,0:T(8,128)(2,1)} %bitcast.6.refs_0_.refs_2_), channel_id=1, source_target_pairs={{0,6},{1,7},{2,0},{3,1},{4,2},{5,3},{6,4},{7,5},{8,14},{9,15},{10,... | collective-permute-start | bytes 6291464 | tf_op jit(solution)/shard_map/ppermute | solution.py:25
  58.3 50.9 %collective-permute-start.16 = (bf16[4,256,1024]{2,1,0:T(8,128)(2,1)}, bf16[4,256,1024]{2,1,0:T(8,128)(2,1)}, u32[]{:S(2)}, u32[]{:S(2)}) collective-permute-start(bf16[4,256,1024]{2,1,0:T(8,128)(2,1)} %bitcast.6.refs_0_.refs_2_), channel_id=1, source_target_pairs={{0,2},{1,3},{2,4},{3,5},{4,6},{5,7},{6,0},{7,1},{8,10},{9,11},{10,... | collective-permute-start | bytes 6291464 | tf_op jit(solution)/shard_map/ppermute | solution.py:25
  59.7 58.1 %collective-permute-start.18 = (bf16[4,256,1024]{2,1,0:T(8,128)(2,1)}, bf16[4,256,1024]{2,1,0:T(8,128)(2,1)}, u32[]{:S(2)}, u32[]{:S(2)}) collective-permute-start(bf16[4,256,1024]{2,1,0:T(8,128)(2,1)} %bitcast.6.refs_0_.refs_2_), channel_id=1, source_target_pairs={{0,8},{1,9},{2,10},{3,11},{4,12},{5,13},{6,14},{7,15},{8,0},{9,1},... | collective-permute-start | bytes 6291464 | tf_op jit(solution)/shard_map/ppermute | solution.py:25
  63.8 48.2 %all-to-all-start = ((bf16[8,32,1024]{2,1,0:T(8,128)(2,1)}), bf16[8,32,1024]{2,1,0:T(8,128)(2,1)S(1)}, u32[]{:S(2)}, u32[]{:S(2)}) async-start(bf16[8,32,1024]{2,1,0:T(8,128)(2,1)} %bitcast.48), calls=%async_computation | async-start | bytes 1048576 | tf_op jit(solution)/shard_map/all_to_all | solution.py:323
  108.0 31.8 %collective-permute-start.15 = (bf16[2,256,1024]{2,1,0:T(8,128)(2,1)}, bf16[2,256,1024]{2,1,0:T(8,128)(2,1)}, u32[]{:S(2)}, u32[]{:S(2)}) collective-permute-start(bf16[2,256,1024]{2,1,0:T(8,128)(2,1)} %slice.98), channel_id=1, source_target_pairs={{0,6},{1,7},{2,0},{3,1},{4,2},{5,3},{6,4},{7,5},{8,14},{9,15},{10,... | collective-permute-start | bytes 3145736 | tf_op jit(solution)/shard_map/ppermute | solution.py:25
  111.5 28.2 %collective-permute-start.17 = (bf16[2,256,1024]{2,1,0:T(8,128)(2,1)}, bf16[2,256,1024]{2,1,0:T(8,128)(2,1)}, u32[]{:S(2)}, u32[]{:S(2)}) collective-permute-start(bf16[2,256,1024]{2,1,0:T(8,128)(2,1)} %slice.99), channel_id=1, source_target_pairs={{0,2},{1,3},{2,4},{3,5},{4,6},{5,7},{6,0},{7,1},{8,10},{9,11},{10,... | collective-permute-start | bytes 3145736 | tf_op jit(solution)/shard_map/ppermute | solution.py:25
  113.0 26.7 %all-to-all-start.1 = ((bf16[8,32,1024]{2,1,0:T(8,128)(2,1)}), bf16[8,32,1024]{2,1,0:T(8,128)(2,1)S(1)}, u32[]{:S(2)}, u32[]{:S(2)}) async-start(bf16[8,32,1024]{2,1,0:T(8,128)(2,1)} %broadcast_in_dim.14), calls=%async_computation.1 | async-start | bytes 1048576 | tf_op jit(solution)/shard_map/all_to_all | solution.py:329
  139.7 44.0 %collective-permute-start.21 = (bf16[4,256,1024]{2,1,0:T(8,128)(2,1)}, bf16[4,256,1024]{2,1,0:T(8,128)(2,1)}, u32[]{:S(2)}, u32[]{:S(2)}) collective-permute-start(bf16[4,256,1024]{2,1,0:T(8,128)(2,1)} %collective-permute-done.18.refs_5_), channel_id=1, source_target_pairs={{0,6},{1,7},{2,0},{3,1},{4,2},{5,3},{6,4},{7,5},{8,14},{9,15},{10,... | collective-permute-start | bytes 6291464 | tf_op jit(solution)/shard_map/ppermute | solution.py:25
  140.6 45.0 %collective-permute-start.22 = (bf16[4,256,1024]{2,1,0:T(8,128)(2,1)}, bf16[4,256,1024]{2,1,0:T(8,128)(2,1)}, u32[]{:S(2)}, u32[]{:S(2)}) collective-permute-start(bf16[4,256,1024]{2,1,0:T(8,128)(2,1)} %collective-permute-done.18.refs_5_), channel_id=1, source_target_pairs={{0,2},{1,3},{2,4},{3,5},{4,6},{5,7},{6,0},{7,1},{8,10},{9,11},{10,... | collective-permute-start | bytes 6291464 | tf_op jit(solution)/shard_map/ppermute | solution.py:25
  141.3 26.9 %collective-permute-start.19 = (bf16[2,256,1024]{2,1,0:T(8,128)(2,1)}, bf16[2,256,1024]{2,1,0:T(8,128)(2,1)S(1)}, u32[]{:S(2)}, u32[]{:S(2)}) collective-permute-start(bf16[2,256,1024]{2,1,0:T(8,128)(2,1)} %collective-permute-done.15.refs_6_), channel_id=1, source_target_pairs={{0,8},{1,9},{2,10},{3,11},{4,12},{5,13},{6,14},{7,15},{8,0},{9,1},... | collective-permute-start | bytes 3145736 | tf_op jit(solution)/shard_map/ppermute | solution.py:25
  141.3 42.4 %collective-permute-start.20 = (bf16[2,256,1024]{2,1,0:T(8,128)(2,1)}, bf16[2,256,1024]{2,1,0:T(8,128)(2,1)}, u32[]{:S(2)}, u32[]{:S(2)}) collective-permute-start(bf16[2,256,1024]{2,1,0:T(8,128)(2,1)} %collective-permute-done.17.refs_7_), channel_id=1, source_target_pairs={{0,8},{1,9},{2,10},{3,11},{4,12},{5,13},{6,14},{7,15},{8,0},{9,1},... | collective-permute-start | bytes 3145736 | tf_op jit(solution)/shard_map/ppermute | solution.py:25
  154.7 50.8 %all-to-all-start.3 = ((bf16[16,32,1280]{2,1,0:T(8,128)(2,1)}), bf16[16,32,1280]{2,1,0:T(8,128)(2,1)S(1)}, u32[]{:S(2)}, u32[]{:S(2)}) async-start(bf16[16,32,1280]{2,1,0:T(8,128)(2,1)} %bitcast.50), calls=%async_computation.3 | async-start | bytes 2621440 | tf_op jit(solution)/shard_map/all_to_all | solution.py:164
  205.5 19.8 %all-to-all-start.2 = ((bf16[16,32,768]{2,1,0:T(8,128)(2,1)}), bf16[16,32,768]{2,1,0:T(8,128)(2,1)}, u32[]{:S(2)}, u32[]{:S(2)}) async-start(bf16[16,32,768]{2,1,0:T(8,128)(2,1)} %bitcast.51), calls=%async_computation.2 | async-start | bytes 1572864 | tf_op jit(solution)/shard_map/all_to_all | solution.py:164
  231.3 19.4 %all-to-all-start.4 = ((bf16[8,32,2048]{2,1,0:T(8,128)(2,1)}), bf16[8,32,2048]{2,1,0:T(8,128)(2,1)S(1)}, u32[]{:S(2)}, u32[]{:S(2)}) async-start(bf16[8,32,2048]{2,1,0:T(8,128)(2,1)} %late_rows.1), calls=%async_computation.4 | async-start | bytes 2097152 | tf_op jit(solution)/shard_map/all_to_all | solution.py:341
  236.8 14.3 %collective-permute-start.24 = (bf16[256,1024]{1,0:T(8,128)(2,1)S(1)}, bf16[256,1024]{1,0:T(8,128)(2,1)S(1)}, u32[]{:S(2)}, u32[]{:S(2)}) collective-permute-start(bf16[256,1024]{1,0:T(8,128)(2,1)S(1)} %bitcast.46), channel_id=1, source_target_pairs={{0,1},{1,0},{2,3},{3,2},{4,5},{5,4},{6,7},{7,6},{8,9},{9,8},{10,11... | collective-permute-start | bytes 1572872 | tf_op jit(solution)/shard_map/ppermute | solution.py:25
  251.5 14.3 %collective-permute-start.25 = (bf16[256,256]{1,0:T(8,128)(2,1)S(1)}, bf16[256,256]{1,0:T(8,128)(2,1)S(1)}, u32[]{:S(2)}, u32[]{:S(2)}) collective-permute-start(bf16[256,256]{1,0:T(8,128)(2,1)S(1)} %copy.15), channel_id=1, source_target_pairs={{0,1},{1,0},{2,17},{3,16},{4,33},{5,32},{6,49},{7,48},{8,65},{9,64... | collective-permute-start | bytes 393224 | tf_op jit(solution)/shard_map/ppermute | solution.py:25
  257.0 14.4 %collective-permute-start.23 = (bf16[256,256]{1,0:T(8,128)(2,1)S(1)}, bf16[256,256]{1,0:T(8,128)(2,1)S(1)}, u32[]{:S(2)}, u32[]{:S(2)}) collective-permute-start(bf16[256,256]{1,0:T(8,128)(2,1)S(1)} %copy.14), channel_id=1, source_target_pairs={{0,0},{1,1},{2,16},{3,17},{4,32},{5,33},{6,48},{7,49},{8,64},{9,65... | collective-permute-start | bytes 393224 | tf_op jit(solution)/shard_map/ppermute | solution.py:25
  (15 other events, 151.6 us)
